TPU v7x, 32 devices: a whole 2x2x4 slice. The times are simulated.
32 devices in a mesh: groups: 2 (over y), blk: 4 (over z), oct: 2 (over x), sub: 2 (over core).
Axes of the slice: x: 2, y: 2, z: 4, core: 2. Of those that a mesh axis runs over, the one named last changes fastest.
Arguments:
- positions: float32 [3, 65536], P(None, ('groups', 'blk', 'oct', 'sub')), parts along dimension 1, may hold values from 0 to 320
- polarizability: float32 [65536], P(('groups', 'blk', 'oct', 'sub')), parts along dimension 0, may hold values from 0.5 to 1.5
- permanent_field: float32 [3, 65536], P(None, ('groups', 'blk', 'oct', 'sub')), parts along dimension 1, may hold values from -40 to 40
- group_id: int32 [65536], P(('groups', 'blk', 'oct', 'sub')), parts along dimension 0, may hold values from 0 to 10921, never falling along the last dimension, each value on 1 to 6 neighbouring positions
- pair_mask: int32 [512, 9], P(('groups', 'blk', 'oct', 'sub')), parts along dimension 0, may hold values from 0 to 1, as said below
Outputs:
- dipoles: float32 [3, 65536], P(None, ('groups', 'blk', 'oct', 'sub')), parts along dimension 1
- residual: float32 [3, 65536], P(None, ('groups', 'blk', 'oct', 'sub')), parts along dimension 1
There are 2 independent parts, one for each index of `groups`. A program takes and returns all parts, laid end to end along the dimension named above; each array names one. Nothing has to cross between parts.
Inputs may be any that keep to these rules, and one draw needn't show every extreme that they name: `group_id`: never falls from one atom to the next; each value names 1 to 6 consecutive atoms. pair_mask[b, 4] = 1, and pair_mask[b, 4 + o] = pair_mask[(b + o) mod 256, 4 - o].
All inputs are finite; a program needn't handle non-finite values.
Results may differ from a plain program's by a relative error of at most 0.0003.
Values sent between devices are 32-bit elements; how exact they have to be, the bound alone decides.
No kernel may reach another device: no remote copies, remote signals or barrier semaphores. Data moves between devices by JAX's collectives and lax.ppermute only.
A program may use at most 64 MiB of HBM per device.

v0:
```python
import math

import jax
import jax.numpy as jnp
import numpy as np
from jax import lax
from jax.sharding import PartitionSpec as P

BOXES_DEV = 2
BLOCK = 128
ORDER = 5
NODE_PAD = 128
ITERS = 2


side_length = 32.0
layer_gap = 2.5
thole_damp = 0.39
highest = lax.Precision.HIGHEST


def padded(cells, sides, width):
    for axis, dim in sides:
        count = lax.axis_size(axis)
        head = lax.slice_in_dim(cells, 0, width, axis=dim)
        tail = lax.slice_in_dim(cells, cells.shape[dim] - width, cells.shape[dim], axis=dim)
        cells = jnp.concatenate(
            [
                lax.ppermute(tail, axis, [(i, (i + 1) % count) for i in range(count)]),
                cells,
                lax.ppermute(head, axis, [((i + 1) % count, i) for i in range(count)]),
            ],
            axis=dim,
        )
    return cells


def wrap_image(delta, period):
    return delta - period * jnp.floor(delta / period + 0.5)


def split_size(total, limit):
    best = 1
    for factor in range(1, min(total, limit) + 1):
        if total % factor == 0:
            best = factor
    return best


def near_tiles(target, source, moments, keep_tile, length_z):
    delta_x = wrap_image(target[0][:, :, None] - source[0][:, None, :], side_length)
    delta_y = wrap_image(target[1][:, :, None] - source[1][:, None, :], side_length)
    delta_z = wrap_image(target[2][:, :, None] - source[2][:, None, :], length_z)
    keep = (keep_tile[:, None, None] > 0.5) & (target[4][:, :, None] != source[4][:, None, :])
    dist_sq = jnp.where(keep, delta_x * delta_x + delta_y * delta_y + delta_z * delta_z, 1.0)
    inv_three = lax.rsqrt(dist_sq) / dist_sq
    scaled = (
        thole_damp
        * dist_sq
        * jnp.sqrt(dist_sq)
        * lax.rsqrt(target[3][:, :, None] * source[3][:, None, :])
    )
    lam_three = -jnp.expm1(-scaled)
    lam_five = lam_three - scaled * jnp.exp(-scaled)
    coef_five = jnp.where(keep, 3.0 * lam_five * inv_three / dist_sq, 0.0)
    coef_three = jnp.where(keep, lam_three * inv_three, 0.0)
    along = (
        delta_x * moments[0][:, None, :]
        + delta_y * moments[1][:, None, :]
        + delta_z * moments[2][:, None, :]
    )
    weighted = coef_five * along
    field_x = jnp.sum(weighted * delta_x - coef_three * moments[0][:, None, :], axis=2)
    field_y = jnp.sum(weighted * delta_y - coef_three * moments[1][:, None, :], axis=2)
    field_z = jnp.sum(weighted * delta_z - coef_three * moments[2][:, None, :], axis=2)
    return jnp.stack([field_x, field_y, field_z])


def near_total(static_ext, dipole_ext, mask_rows, length_z, atom_count):
    reach = (mask_rows.shape[1] - 1) // 2
    width = reach * BLOCK
    blocks = atom_count // BLOCK
    target = static_ext[:, width : width + atom_count].reshape(5, blocks, BLOCK)
    total = jnp.zeros((3, blocks, BLOCK), static_ext.dtype)
    for offset in range(-reach, reach + 1):
        begin = (reach + offset) * BLOCK
        source = static_ext[:, begin : begin + atom_count].reshape(5, blocks, BLOCK)
        moments = dipole_ext[:, begin : begin + atom_count].reshape(3, blocks, BLOCK)
        keep_tile = mask_rows[:, reach + offset].astype(static_ext.dtype)
        total = total + near_tiles(target, source, moments, keep_tile, length_z)
    return total.reshape(3, atom_count)


def node_tables():
    count = ORDER
    roots = np.cos((2.0 * np.arange(count) + 1.0) * np.pi / (2.0 * count))
    degree = np.arange(count)
    coeff = (
        2.0 / count * np.cos(np.outer(2.0 * np.arange(count) + 1.0, degree) * np.pi / (2.0 * count))
    )
    coeff = np.where(degree[None, :] == 0, 1.0 / count, coeff)
    index = np.arange(NODE_PAD)
    live = index < count**3
    safe = np.where(live, index, 0)
    first = safe // (count * count)
    second = safe // count % count
    third = safe % count
    levels = np.arange(count)[None, :]
    pick_a = (first[:, None] == levels) * live[:, None] * 1.0
    pick_b = (second[:, None] == levels) * 1.0
    pick_c = (third[:, None] == levels) * 1.0
    node_x = 16.0 * (1.0 + roots[first])
    node_y = 16.0 * (1.0 + roots[second])
    node_t = roots[third]
    tables = [coeff, pick_a, pick_b, pick_c, node_x, node_y, node_t]
    return [jnp.asarray(item, jnp.float32) for item in tables]


def interpolation(coords, box_ids, box_height):
    coeff, pick_a, pick_b, pick_c, node_x, node_y, node_t = node_tables()
    scaled_x = coords[0] / 16.0 - 1.0
    scaled_y = coords[1] / 16.0 - 1.0
    scaled_z = (
        2.0 * (coords[2] - box_ids.astype(coords.dtype)[:, None] * box_height) / box_height - 1.0
    )

    def basis(values, picks):
        terms = [jnp.ones_like(values), values]
        for degree in range(2, ORDER):
            terms.append(2.0 * values * terms[-1] - terms[-2])
        stacked = jnp.stack(terms[:ORDER])
        smooth = jnp.einsum("kn,nba->kba", coeff, stacked, precision=highest)
        return jnp.einsum("pk,kba->pba", picks, smooth, precision=highest)

    return basis(scaled_x, pick_a) * basis(scaled_y, pick_b) * basis(scaled_z, pick_c)


def far_block(target_ids, source_ids, weights, slabs, box_height, length_z):
    coeff, pick_a, pick_b, pick_c, node_x, node_y, node_t = node_tables()
    height_t = (
        target_ids.astype(weights.dtype)[:, None] * box_height
        + 0.5 * box_height * (1.0 + node_t)[None, :]
    )
    height_s = (
        source_ids.astype(weights.dtype)[:, None] * box_height
        + 0.5 * box_height * (1.0 + node_t)[None, :]
    )
    delta_x = wrap_image(node_x[:, None] - node_x[None, :], side_length)[None, :, None, :]
    delta_y = wrap_image(node_y[:, None] - node_y[None, :], side_length)[None, :, None, :]
    delta_z = wrap_image(height_t[:, :, None, None] - height_s[None, None, :, :], length_z)
    apart = jnp.abs(target_ids[:, None] // BOXES_DEV - source_ids[None, :] // BOXES_DEV)
    apart = jnp.minimum(apart, slabs - apart)
    keep = (apart >= 1)[:, None, :, None]
    dist_sq = jnp.where(
        keep,
        delta_x * delta_x + delta_y * delta_y + delta_z * delta_z + box_height * box_height,
        1.0,
    )
    inv_three = lax.rsqrt(dist_sq) / dist_sq
    coef_five = jnp.where(keep, 3.0 * inv_three / dist_sq, 0.0)
    coef_three = jnp.where(keep, inv_three, 0.0)
    weight_x = weights[:, 0, :][None, None]
    weight_y = weights[:, 1, :][None, None]
    weight_z = weights[:, 2, :][None, None]
    weighted = coef_five * (delta_x * weight_x + delta_y * weight_y + delta_z * weight_z)
    field_x = jnp.sum(weighted * delta_x - coef_three * weight_x, axis=(2, 3))
    field_y = jnp.sum(weighted * delta_y - coef_three * weight_y, axis=(2, 3))
    field_z = jnp.sum(weighted * delta_z - coef_three * weight_z, axis=(2, 3))
    return jnp.stack([field_x, field_y, field_z], axis=1)


def on_device(positions, polarizability, permanent_field, group_id, pair_mask):
    slabs = lax.axis_size(("blk", "oct", "sub"))
    member = lax.axis_index(("blk", "oct", "sub"))
    atom_count = positions.shape[1]
    length_z = layer_gap * atom_count * slabs / 256.0
    box_height = length_z / (BOXES_DEV * slabs)
    per_box = atom_count // BOXES_DEV
    width = (pair_mask.shape[1] - 1) // 2 * BLOCK
    group_limit = max(1, 32 // BOXES_DEV)
    static = jnp.concatenate(
        [positions, polarizability[None, :], group_id.astype(jnp.float32)[None, :]], axis=0
    )
    static_ext = padded(static, ((("blk", "oct", "sub"), 1),), width)
    own_boxes = member * BOXES_DEV + jnp.arange(BOXES_DEV, dtype=jnp.int32)
    interp = interpolation(positions.reshape(3, BOXES_DEV, per_box), own_boxes, box_height)
    surface = 4.0 * math.pi / 3.0 / (side_length * side_length * length_z)

    def induced(dipoles, total):
        dipole_ext = padded(dipoles, ((("blk", "oct", "sub"), 1),), width)
        near = near_total(static_ext, dipole_ext, pair_mask, length_z, atom_count)
        weights = jnp.einsum(
            "pba,cba->bcp", interp, dipoles.reshape(3, BOXES_DEV, per_box), precision=highest
        )
        piece = lax.all_gather(weights, ("blk", "oct", "sub"), axis=0, tiled=True)
        start = jnp.int32(0)
        count = piece.shape[0]
        size = split_size(count, group_limit)
        grouped = piece.reshape(count // size, size, 3, piece.shape[2])

        def visit(acc, item):
            index, bundle = item
            sources = start + index * size + jnp.arange(size, dtype=jnp.int32)
            return (acc + far_block(own_boxes, sources, bundle, slabs, box_height, length_z), None)

        result, unused = lax.scan(
            visit, jnp.zeros_like(weights), (jnp.arange(count // size, dtype=jnp.int32), grouped)
        )
        far = jnp.einsum("pba,bcp->cba", interp, result, precision=highest).reshape(3, atom_count)
        return near + far - surface * total[:, None]

    def moment(values):
        return lax.psum(jnp.sum(values, axis=1), ("blk", "oct", "sub"))

    def squares(resid, scaled):
        return lax.psum(jnp.sum(resid * scaled), ("blk", "oct", "sub"))

    dipoles = polarizability[None, :] * permanent_field
    residual = induced(dipoles, moment(dipoles))
    precond = polarizability[None, :] * residual
    direction = precond
    norm_now = squares(residual, precond)
    for step in range(ITERS):
        image = direction / polarizability[None, :] - induced(direction, moment(direction))
        rate = norm_now / lax.psum(jnp.sum(direction * image), ("blk", "oct", "sub"))
        dipoles = dipoles + rate * direction
        residual = residual - rate * image
        if step + 1 < ITERS:
            precond = polarizability[None, :] * residual
            norm_next = squares(residual, precond)
            direction = precond + norm_next / norm_now * direction
            norm_now = norm_next
    return (dipoles, residual)


def solution(mesh):
    return jax.shard_map(
        on_device,
        mesh=mesh,
        in_specs=(
            P(None, ("groups", "blk", "oct", "sub")),
            P(("groups", "blk", "oct", "sub")),
            P(None, ("groups", "blk", "oct", "sub")),
            P(("groups", "blk", "oct", "sub")),
            P(("groups", "blk", "oct", "sub"), None),
        ),
        out_specs=(
            P(None, ("groups", "blk", "oct", "sub")),
            P(None, ("groups", "blk", "oct", "sub")),
        ),
        check_vma=False,
    )
```

profile of v0, /device:TPU:0, one launch (start us, length us, event | category | flops | bytes accessed | tf_op | source)
XLA Modules:
  0.0 428.1 jit_solution(15247812564218952183)
XLA Ops:
  2.6 5.0 %collective-permute-start.2 = (f32[5,512]{1,0:T(8,128)S(1)}, f32[5,512]{1,0:T(8,128)S(1)}, u32[]{:S(2)}, u32[]{:S(2)}) collective-permute-start(f32[5,512]{1,0:T(8,128)S(1)} %get-tuple-element.990), channel_id=1, source_target_pairs={{1,0},{2,1},{3,2},{4,3},{5,4},{6,5},{7,6},{8,7},{9,8},{10,9},{11,1... | collective-permute-start | bytes 30728 | tf_op jit(solution)/shard_map/ppermute | solution.py:31
  8.6 4.4 %collective-permute-start.3 = (f32[3,512]{1,0:T(4,128)S(1)}, f32[3,512]{1,0:T(4,128)S(1)}, u32[]{:S(2)}, u32[]{:S(2)}) collective-permute-start(f32[3,512]{1,0:T(4,128)S(1)} %get-tuple-element.1086), channel_id=1, source_target_pairs={{1,0},{2,1},{3,2},{4,3},{5,4},{6,5},{7,6},{8,7},{9,8},{10,9},{11,1... | collective-permute-start | bytes 18440 | tf_op jit(solution)/shard_map/ppermute | solution.py:31
  14.0 29.5 %psum.49 = f32[3]{0:T(128)S(1)} all-reduce(f32[3]{0:T(128)S(1)} %get-tuple-element.927), channel_id=1, replica_groups=mesh['groups'=2,'blk'=4,'oct'=2,'sub'=2] {'blk','oct','sub'}, use_global_device_ids=true, to_apply=%region_33.34 | all-reduce | flops 3 | bytes 24 | tf_op jit(solution)/shard_map/psum | solution.py:213
  52.0 17.5 %all_gather.9 = f32[32,3,128]{2,1,0:T(4,128)S(1)} all-gather(f32[2,3,128]{2,1,0:T(4,128)S(1)} %fusion.782), channel_id=1, replica_groups=mesh['groups'=2,'blk'=4,'oct'=2,'sub'=2] {'blk','oct','sub'}, dimensions={0}, use_global_device_ids=true | all-gather | bytes 52224 | tf_op jit(solution)/shard_map/all_gather | solution.py:195
  69.6 13.5 %while.51 = (s32[]{:T(128)}, f32[2,3,128]{2,0,1:T(2,128)S(1)}, s32[2]{0:T(128)S(1)}, f32[2,16,3,128]{3,1,2,0:T(8,128)S(1)}, s32[]{:T(128)}, /*index=5*/s32[]{:T(...) while((s32[]{:T(128)}, f32[2,3,128]{2,0,1:T(2,128)S(1)}, ...), condition=%wide.region_31.32_spmd.clone.clone.clone.clone, body=%wide.region_27.31_spmd.sunk.clone.clone.clone.clone.sunk | while | flops 16765948 | bytes 2795035 | solution.py:206
  71.5 4.8 %subtract_reduce_fusion.9 = (f32[2,128]{1,0:T(2,128)S(1)}, f32[2,128]{1,0:T(2,128)S(1)}, f32[2,128]{1,0:T(2,128)S(1)}) fusion(f32[16,128]{1,0:T(8,128)S(1)} %get-tuple-element.1216, f32[128,128]{1,0:T(8,128)S(1)} %get-tuple-element.1217, pred[2,16]{1,0:T(4,128)(4,1)S(1)} %fusion.814, f32[16,128]{1,0:T(8,128)S(1)} %broadcast_add_fusion.12, ...), kind=kLoop, calls=%fused_computation.28.clone.1 | loop fusion | flops 15727872 | bytes 1282080 | tf_op jit(solution)/shard_map/while/body/eval_jaxpr/reduce_sum | solution.py:166
  78.3 4.8 %subtract_reduce_fusion.9 = (f32[2,128]{1,0:T(2,128)S(1)}, f32[2,128]{1,0:T(2,128)S(1)}, f32[2,128]{1,0:T(2,128)S(1)}) fusion(f32[16,128]{1,0:T(8,128)S(1)} %get-tuple-element.1216, f32[128,128]{1,0:T(8,128)S(1)} %get-tuple-element.1217, pred[2,16]{1,0:T(4,128)(4,1)S(1)} %fusion.814, f32[16,128]{1,0:T(8,128)S(1)} %broadcast_add_fusion.12, ...), kind=kLoop, calls=%fused_computation.28.clone.1 | loop fusion | flops 15727872 | bytes 1282080 | tf_op jit(solution)/shard_map/while/body/eval_jaxpr/reduce_sum | solution.py:166
  111.9 7.3 %fusion.630 = (f32[16,128]{1,0:T(8,128)S(1)}, f32[16,128]{1,0:T(8,128)S(1)}, f32[16,128]{1,0:T(8,128)S(1)}, f32[16,128]{1,0:T(8,128)S(1)}, f32[16,128]{1,0:T(8,128)S(1)}, /*index=5*/f32[16,128]{1,0:T(8,128)S(1)}) fusion(f32[16,128]{1,0:T(8,128)S(1)} %bitcast.840, f32[16,128]{1,0:T(8,128)S(1)} %bitcast.735, f32[16,128]{1,0:T(8,128)S(1)} %bitcast.931, ...), kind=kLoop, calls=%fused_computation.815 | loop fusion | flops 30920704 | bytes 180256 | tf_op jit(solution)/shard_map/reduce_sum | solution.py:73
  120.4 31.8 %psum.51 = f32[3]{0:T(128)S(1)} all-reduce(f32[3]{0:T(128)S(1)} %get-tuple-element.923), channel_id=1, replica_groups=mesh['groups'=2,'blk'=4,'oct'=2,'sub'=2] {'blk','oct','sub'}, use_global_device_ids=true, to_apply=%region_69.70 | all-reduce | flops 3 | bytes 24 | tf_op jit(solution)/shard_map/psum | solution.py:213
  153.1 4.4 %collective-permute-start.5 = (f32[3,512]{1,0:T(4,128)S(1)}, f32[3,512]{1,0:T(4,128)S(1)}, u32[]{:S(2)}, u32[]{:S(2)}) collective-permute-start(f32[3,512]{1,0:T(4,128)S(1)} %get-tuple-element.1078), channel_id=1, source_target_pairs={{1,0},{2,1},{3,2},{4,3},{5,4},{6,5},{7,6},{8,7},{9,8},{10,9},{11,1... | collective-permute-start | bytes 18440 | tf_op jit(solution)/shard_map/ppermute | solution.py:31
  157.5 17.3 %all_gather.10 = f32[32,3,128]{2,1,0:T(4,128)S(1)} all-gather(f32[2,3,128]{2,1,0:T(4,128)S(1)} %fusion.684), channel_id=1, replica_groups=mesh['groups'=2,'blk'=4,'oct'=2,'sub'=2] {'blk','oct','sub'}, dimensions={0}, use_global_device_ids=true | all-gather | bytes 52224 | tf_op jit(solution)/shard_map/all_gather | solution.py:195
  174.8 13.0 %while.52 = (s32[]{:T(128)}, f32[2,3,128]{2,0,1:T(2,128)S(1)}, s32[2]{0:T(128)S(1)}, f32[2,16,3,128]{3,1,2,0:T(8,128)S(1)}, s32[]{:T(128)}, /*index=5*/s32[]{:T(...) while((s32[]{:T(128)}, f32[2,3,128]{2,0,1:T(2,128)S(1)}, ...), condition=%wide.region_67.68_spmd.clone.clone.clone.clone, body=%wide.region_63.67_spmd.sunk.clone.clone.clone.clone.sunk | while | flops 16765948 | bytes 2795035 | solution.py:206
  176.5 4.8 %subtract_reduce_fusion.10 = (f32[2,128]{1,0:T(2,128)S(1)}, f32[2,128]{1,0:T(2,128)S(1)}, f32[2,128]{1,0:T(2,128)S(1)}) fusion(f32[16,128]{1,0:T(8,128)S(1)} %get-tuple-element.1230, f32[128,128]{1,0:T(8,128)S(1)} %get-tuple-element.1231, pred[2,16]{1,0:T(4,128)(4,1)S(1)} %fusion.817, f32[16,128]{1,0:T(8,128)S(1)} %broadcast_add_fusion.14, ...), kind=kLoop, calls=%fused_computation.82.clone.1 | loop fusion | flops 15727872 | bytes 1282080 | tf_op jit(solution)/shard_map/while/body/eval_jaxpr/reduce_sum | solution.py:166
  183.0 4.8 %subtract_reduce_fusion.10 = (f32[2,128]{1,0:T(2,128)S(1)}, f32[2,128]{1,0:T(2,128)S(1)}, f32[2,128]{1,0:T(2,128)S(1)}) fusion(f32[16,128]{1,0:T(8,128)S(1)} %get-tuple-element.1230, f32[128,128]{1,0:T(8,128)S(1)} %get-tuple-element.1231, pred[2,16]{1,0:T(4,128)(4,1)S(1)} %fusion.817, f32[16,128]{1,0:T(8,128)S(1)} %broadcast_add_fusion.14, ...), kind=kLoop, calls=%fused_computation.82.clone.1 | loop fusion | flops 15727872 | bytes 1282080 | tf_op jit(solution)/shard_map/while/body/eval_jaxpr/reduce_sum | solution.py:166
  216.1 7.3 %fusion.629 = (f32[16,128]{1,0:T(8,128)S(1)}, f32[16,128]{1,0:T(8,128)S(1)}, f32[16,128]{1,0:T(8,128)S(1)}, f32[16,128]{1,0:T(8,128)S(1)}, f32[16,128]{1,0:T(8,128)S(1)}, /*index=5*/f32[16,128]{1,0:T(8,128)S(1)}) fusion(f32[16,128]{1,0:T(8,128)S(1)} %bitcast.872, f32[16,128]{1,0:T(8,128)S(1)} %bitcast.736, f32[16,128]{1,0:T(8,128)S(1)} %bitcast.939, ...), kind=kLoop, calls=%fused_computation.814 | loop fusion | flops 30920704 | bytes 180256 | tf_op jit(solution)/shard_map/reduce_sum | solution.py:73
  225.0 32.1 %all-reduce = (f32[]{:T(128)}, f32[]{:T(128)}) all-reduce(f32[]{:T(128)} %get-tuple-element.870, f32[]{:T(128)} %get-tuple-element.869), channel_id=1, replica_groups=mesh['groups'=2,'blk'=4,'oct'=2,'sub'=2] {'blk','oct','sub'}, use_global_device_ids=true, to_apply=%region_35.36 | all-reduce | flops 2 | bytes 16 | tf_op jit(solution)/shard_map/psum | solution.py:216
  259.0 30.1 %psum.53 = f32[]{:T(128)} all-reduce(f32[]{:T(128)} %fusion.632), channel_id=1, replica_groups=mesh['groups'=2,'blk'=4,'oct'=2,'sub'=2] {'blk','oct','sub'}, use_global_device_ids=true, to_apply=%region_73.74 | all-reduce | flops 1 | bytes 8 | tf_op jit(solution)/shard_map/psum | solution.py:216
  290.6 29.7 %psum.54 = f32[3]{0:T(128)S(1)} all-reduce(f32[3]{0:T(128)S(1)} %get-tuple-element.918), channel_id=1, replica_groups=mesh['groups'=2,'blk'=4,'oct'=2,'sub'=2] {'blk','oct','sub'}, use_global_device_ids=true, to_apply=%region_107.108 | all-reduce | flops 3 | bytes 24 | tf_op jit(solution)/shard_map/psum | solution.py:213
  325.6 17.3 %all_gather.11 = f32[32,3,128]{2,1,0:T(4,128)S(1)} all-gather(f32[2,3,128]{2,1,0:T(4,128)S(1)} %fusion.783), channel_id=1, replica_groups=mesh['groups'=2,'blk'=4,'oct'=2,'sub'=2] {'blk','oct','sub'}, dimensions={0}, use_global_device_ids=true | all-gather | bytes 52224 | tf_op jit(solution)/shard_map/all_gather | solution.py:195
  342.9 13.0 %while.53 = (s32[]{:T(128)}, f32[2,3,128]{2,0,1:T(2,128)S(1)}, s32[2]{0:T(128)S(1)}, f32[2,16,3,128]{3,1,2,0:T(8,128)S(1)}, s32[]{:T(128)}, /*index=5*/s32[]{:T(...) while((s32[]{:T(128)}, f32[2,3,128]{2,0,1:T(2,128)S(1)}, ...), condition=%wide.region_105.106_spmd.clone.clone.clone.clone, body=%wide.region_101.105_spmd.sunk.clone.clone.clone.clone.sunk | while | flops 16765948 | bytes 2795035 | solution.py:206
  344.6 4.8 %subtract_reduce_fusion.11 = (f32[2,128]{1,0:T(2,128)S(1)}, f32[2,128]{1,0:T(2,128)S(1)}, f32[2,128]{1,0:T(2,128)S(1)}) fusion(f32[16,128]{1,0:T(8,128)S(1)} %get-tuple-element.1244, f32[128,128]{1,0:T(8,128)S(1)} %get-tuple-element.1245, pred[2,16]{1,0:T(4,128)(4,1)S(1)} %fusion.820, f32[16,128]{1,0:T(8,128)S(1)} %broadcast_add_fusion.16, ...), kind=kLoop, calls=%fused_computation.136.clone.1 | loop fusion | flops 15727872 | bytes 1282080 | tf_op jit(solution)/shard_map/while/body/eval_jaxpr/reduce_sum | solution.py:166
  351.1 4.8 %subtract_reduce_fusion.11 = (f32[2,128]{1,0:T(2,128)S(1)}, f32[2,128]{1,0:T(2,128)S(1)}, f32[2,128]{1,0:T(2,128)S(1)}) fusion(f32[16,128]{1,0:T(8,128)S(1)} %get-tuple-element.1244, f32[128,128]{1,0:T(8,128)S(1)} %get-tuple-element.1245, pred[2,16]{1,0:T(4,128)(4,1)S(1)} %fusion.820, f32[16,128]{1,0:T(8,128)S(1)} %broadcast_add_fusion.16, ...), kind=kLoop, calls=%fused_computation.136.clone.1 | loop fusion | flops 15727872 | bytes 1282080 | tf_op jit(solution)/shard_map/while/body/eval_jaxpr/reduce_sum | solution.py:166
  384.2 7.3 %fusion.628 = (f32[16,128]{1,0:T(8,128)S(1)}, f32[16,128]{1,0:T(8,128)S(1)}, f32[16,128]{1,0:T(8,128)S(1)}, f32[16,128]{1,0:T(8,128)S(1)}, f32[16,128]{1,0:T(8,128)S(1)}, /*index=5*/f32[16,128]{1,0:T(8,128)S(1)}) fusion(f32[16,128]{1,0:T(8,128)S(1)} %bitcast.862, f32[16,128]{1,0:T(8,128)S(1)} %bitcast.737, f32[16,128]{1,0:T(8,128)S(1)} %bitcast.947, ...), kind=kLoop, calls=%fused_computation.813 | loop fusion | flops 30920704 | bytes 180256 | tf_op jit(solution)/shard_map/reduce_sum | solution.py:73
  393.1 32.0 %psum.55 = f32[]{:T(128)} all-reduce(f32[]{:T(128)} %get-tuple-element.1104), channel_id=1, replica_groups=mesh['groups'=2,'blk'=4,'oct'=2,'sub'=2] {'blk','oct','sub'}, use_global_device_ids=true, to_apply=%region_109.110 | all-reduce | flops 1 | bytes 8 | tf_op jit(solution)/shard_map/psum | solution.py:225
  (198 shorter events, 116.9 us)
Async XLA Ops:
  0.6 45.0 %copy-start.8 = (f32[5,5,1]{1,0,2:T(8,128)S(1)}, f32[5,5,1]{1,0,2:T(8,128)}, u32[]{:S(2)}) copy-start(f32[5,5,1]{1,0,2:T(8,128)} %constant.532) | copy-start | bytes 304
  0.6 45.2 %copy-start.11 = (f32[128,5,1]{0,1,2:T(8,128)S(1)}, f32[128,5,1]{0,1,2:T(8,128)}, u32[]{:S(2)}) copy-start(f32[128,5,1]{0,1,2:T(8,128)} %constant.533) | copy-start | bytes 7684
  2.1 81.5 %collective-permute-start = (f32[5,512]{1,0:T(8,128)S(1)}, f32[5,512]{1,0:T(8,128)S(1)}, u32[]{:S(2)}, u32[]{:S(2)}) collective-permute-start(f32[5,512]{1,0:T(8,128)S(1)} %get-tuple-element.989), channel_id=1, source_target_pairs={{0,1},{1,2},{2,3},{3,4},{4,5},{5,6},{6,7},{7,8},{8,9},{9,10},{10,1... | collective-permute-start | bytes 30728 | tf_op jit(solution)/shard_map/ppermute | solution.py:29
  2.6 81.0 %collective-permute-start.2 = (f32[5,512]{1,0:T(8,128)S(1)}, f32[5,512]{1,0:T(8,128)S(1)}, u32[]{:S(2)}, u32[]{:S(2)}) collective-permute-start(f32[5,512]{1,0:T(8,128)S(1)} %get-tuple-element.990), channel_id=1, source_target_pairs={{1,0},{2,1},{3,2},{4,3},{5,4},{6,5},{7,6},{8,7},{9,8},{10,9},{11,1... | collective-permute-start | bytes 30728 | tf_op jit(solution)/shard_map/ppermute | solution.py:31
  8.6 74.9 %collective-permute-start.1 = (f32[3,512]{1,0:T(4,128)S(1)}, f32[3,512]{1,0:T(4,128)S(1)}, u32[]{:S(2)}, u32[]{:S(2)}) collective-permute-start(f32[3,512]{1,0:T(4,128)S(1)} %get-tuple-element.1085), channel_id=1, source_target_pairs={{0,1},{1,2},{2,3},{3,4},{4,5},{5,6},{6,7},{7,8},{8,9},{9,10},{10,1... | collective-permute-start | bytes 18440 | tf_op jit(solution)/shard_map/ppermute | solution.py:29
  8.6 74.9 %collective-permute-start.3 = (f32[3,512]{1,0:T(4,128)S(1)}, f32[3,512]{1,0:T(4,128)S(1)}, u32[]{:S(2)}, u32[]{:S(2)}) collective-permute-start(f32[3,512]{1,0:T(4,128)S(1)} %get-tuple-element.1086), channel_id=1, source_target_pairs={{1,0},{2,1},{3,2},{4,3},{5,4},{6,5},{7,6},{8,7},{9,8},{10,9},{11,1... | collective-permute-start | bytes 18440 | tf_op jit(solution)/shard_map/ppermute | solution.py:31
  13.1 34.7 %copy-start.10 = (f32[128,5,1]{0,1,2:T(8,128)S(1)}, f32[128,5,1]{0,1,2:T(8,128)}, u32[]{:S(2)}) copy-start(f32[128,5,1]{0,1,2:T(8,128)} %constant.534) | copy-start | bytes 7684
  47.7 1.8 copy-start.9
  51.4 18.2 %copy-start.2 = (f32[128]{0:T(128)S(1)}, f32[128]{0:T(128)}, u32[]{:S(2)}) copy-start(f32[128]{0:T(128)} %constant.2011) | copy-start | bytes 1540
  51.4 18.1 %copy-start.4 = (f32[128]{0:T(128)S(1)}, f32[128]{0:T(128)}, u32[]{:S(2)}) copy-start(f32[128]{0:T(128)} %constant.489.clone..sunk.15) | copy-start | bytes 1540
  51.4 18.1 %copy-start.5 = (f32[128]{0:T(128)S(1)}, f32[128]{0:T(128)}, u32[]{:S(2)}) copy-start(f32[128]{0:T(128)} %constant.2010) | copy-start | bytes 1540
  51.4 18.1 %copy-start.6 = (f32[128]{0:T(128)S(1)}, f32[128]{0:T(128)}, u32[]{:S(2)}) copy-start(f32[128]{0:T(128)} %constant.490.clone..sunk.15) | copy-start | bytes 1540
  51.4 18.1 %copy-start.7 = (f32[128]{0:T(128)S(1)}, f32[128]{0:T(128)}, u32[]{:S(2)}) copy-start(f32[128]{0:T(128)} %constant.2009) | copy-start | bytes 1540
  69.6 13.5 %copy-start = (s32[16,9]{1,0:T(8,128)S(1)}, s32[16,9]{1,0:T(8,128)}, u32[]{:S(2)}) copy-start(s32[16,9]{1,0:T(8,128)} %param.28) | copy-start | bytes 1732
  69.6 13.8 %copy-start.1 = (f32[2048]{0:T(1024)S(1)}, f32[2048]{0:T(1024)}, u32[]{:S(2)}) copy-start(f32[2048]{0:T(1024)} %param.25) | copy-start | bytes 24580
  69.6 14.0 %copy-start.3 = (f32[3,2048]{1,0:T(4,128)S(1)}, f32[3,2048]{1,0:T(4,128)}, u32[]{:S(2)}) copy-start(f32[3,2048]{1,0:T(4,128)} %param.24) | copy-start | bytes 73732
  153.0 34.8 %collective-permute-start.4 = (f32[3,512]{1,0:T(4,128)S(1)}, f32[3,512]{1,0:T(4,128)S(1)}, u32[]{:S(2)}, u32[]{:S(2)}) collective-permute-start(f32[3,512]{1,0:T(4,128)S(1)} %get-tuple-element.1077), channel_id=1, source_target_pairs={{0,1},{1,2},{2,3},{3,4},{4,5},{5,6},{6,7},{7,8},{8,9},{9,10},{10,1... | collective-permute-start | bytes 18440 | tf_op jit(solution)/shard_map/ppermute | solution.py:29
  153.1 34.8 %collective-permute-start.5 = (f32[3,512]{1,0:T(4,128)S(1)}, f32[3,512]{1,0:T(4,128)S(1)}, u32[]{:S(2)}, u32[]{:S(2)}) collective-permute-start(f32[3,512]{1,0:T(4,128)S(1)} %get-tuple-element.1078), channel_id=1, source_target_pairs={{1,0},{2,1},{3,2},{4,3},{5,4},{6,5},{7,6},{8,7},{9,8},{10,9},{11,1... | collective-permute-start | bytes 18440 | tf_op jit(solution)/shard_map/ppermute | solution.py:31
  321.1 34.8 %collective-permute-start.6 = (f32[3,512]{1,0:T(4,128)S(1)}, f32[3,512]{1,0:T(4,128)S(1)}, u32[]{:S(2)}, u32[]{:S(2)}) collective-permute-start(f32[3,512]{1,0:T(4,128)S(1)} %get-tuple-element.1069), channel_id=1, source_target_pairs={{0,1},{1,2},{2,3},{3,4},{4,5},{5,6},{6,7},{7,8},{8,9},{9,10},{10,1... | collective-permute-start | bytes 18440 | tf_op jit(solution)/shard_map/ppermute | solution.py:29
  321.2 34.8 %collective-permute-start.7 = (f32[3,512]{1,0:T(4,128)S(1)}, f32[3,512]{1,0:T(4,128)S(1)}, u32[]{:S(2)}, u32[]{:S(2)}) collective-permute-start(f32[3,512]{1,0:T(4,128)S(1)} %get-tuple-element.1070), channel_id=1, source_target_pairs={{1,0},{2,1},{3,2},{4,3},{5,4},{6,5},{7,6},{8,7},{9,8},{10,9},{11,1... | collective-permute-start | bytes 18440 | tf_op jit(solution)/shard_map/ppermute | solution.py:31
where the time goes:
time: 434 us; the launch traced here: 428 us
  blocking collectives  237 us (55%)
  other arithmetic  145 us (33%)
  starting transfers between devices  19 us (4%)
  matrix products  13.6 us (3%)
  between operations  5.57 us (1%)
    reduce_sum x24, other arithmetic, near_tiles(): jnp.sum(weighted * delta_x - coef_three * moments[0][:, None, :], axis=2)  106 us
    psum x3, blocking collectives, moment(): return lax.psum(jnp.sum(values, axis=1), ('blk', 'oct', 'sub'))  91 us
    psum x2, blocking collectives, squares(): return lax.psum(jnp.sum(resid * scaled), ('blk', 'oct', 'sub'))  62.2 us
    all_gather x3, blocking collectives, induced(): piece = lax.all_gather(weights, ('blk', 'oct', 'sub'), axis=0, tiled=True)  52 us
    psum x1, blocking collectives, on_device(): lax.psum(jnp.sum(direction * image), ('blk', 'oct', 'sub'))  32 us
    reduce_sum x6, other arithmetic, far_block(): field_x = jnp.sum(weighted * delta_x - coef_three * weight_x, axis=(2, 3))  28.8 us
    ppermute x4, starting transfers between devices, padded(): lax.ppermute(head, axis, [((i + 1) % count, i) for i in range(count)])  18.3 us
  transfers between devices with their start and end apart: 8, of which 0 were waited for; matrix products, arithmetic and copies ran while one was open for 11% of the time, Pallas kernels for 0%

commit v1 on v0

v1 whole, which is shorter than its diff:
```python
import functools
import math

import jax
import jax.numpy as jnp
import numpy as np
from jax import lax
from jax.experimental import pallas as pl
from jax.experimental.pallas import tpu as pltpu
from jax.sharding import PartitionSpec as P

BOXES_DEV = 2
BLOCK = 128
ORDER = 5
NODE_PAD = 128
ITERS = 2
SUB = 8
CHUNK = 32

side_length = 32.0
layer_gap = 2.5
thole_damp = 0.39
highest = lax.Precision.HIGHEST
f32 = jnp.float32
RING = ("blk", "oct", "sub")

VM = pl.BlockSpec(memory_space=pltpu.VMEM)
SM = pl.BlockSpec(memory_space=pltpu.SMEM)
TABLE_LIMIT = 16 << 20


def call(body, outs, args, smem=0, scratch=(), limit=None, cost=None, pinned=()):
    shapes = [
        pltpu.VMEM(shape, f32) if at in pinned else jax.ShapeDtypeStruct(shape, f32)
        for at, shape in enumerate(outs)
    ]
    return list(pl.pallas_call(
        body,
        out_shape=shapes,
        in_specs=[SM] * smem + [VM] * (len(args) - smem),
        out_specs=[VM] * len(outs),
        scratch_shapes=[pltpu.VMEM(shape, f32) for shape in scratch],
        compiler_params=pltpu.CompilerParams(vmem_limit_bytes=limit or (6 << 20)),
        cost_estimate=cost,
    )(*args))


def node_tables():
    count = ORDER
    roots = np.cos((2.0 * np.arange(count) + 1.0) * np.pi / (2.0 * count))
    degree = np.arange(count)
    coeff = (
        2.0 / count * np.cos(np.outer(2.0 * np.arange(count) + 1.0, degree) * np.pi / (2.0 * count))
    )
    coeff = np.where(degree[None, :] == 0, 1.0 / count, coeff)
    index = np.arange(NODE_PAD)
    live = index < count**3
    safe = np.where(live, index, 0)
    levels = np.stack([safe // (count * count), safe // count % count, safe % count])
    picks = (levels[:, :, None] == np.arange(8)) * 1.0
    picks[0] *= live[:, None]
    nodes = np.zeros((8, NODE_PAD))
    nodes[0] = 0.5 * (1.0 + roots[levels[0]])
    nodes[1] = 0.5 * (1.0 + roots[levels[1]])
    nodes[2] = 0.5 * roots[levels[2]]
    return coeff.astype(np.float32), picks.astype(np.float32), nodes.astype(np.float32)


def wrap_unit(delta):
    return (delta - jnp.floor(delta + 0.5)) * side_length


def wrap_z(delta, length_z):
    return delta - length_z * jnp.floor(delta * (1.0 / length_z) + 0.5)


def tensor(five, three, dx, dy, dz):
    fx, fy, fz = five * dx, five * dy, five * dz
    return (fx * dx - three, fx * dy, fx * dz, fy * dy - three, fy * dz, fz * dz - three)


def columns(tile, count, put):
    turned = tile.T
    for k in range(count):
        put(k, jnp.broadcast_to(turned[:, k : k + 1], (BLOCK, BLOCK)))


def diagonal(step):
    row = lax.broadcasted_iota(jnp.int32, (SUB, BLOCK), 0)
    lane = lax.broadcasted_iota(jnp.int32, (SUB, BLOCK), 1)
    return lane - row == step * SUB


def spread(tile, k):
    return jnp.broadcast_to(tile[k : k + 1, :], (SUB, BLOCK))


def row_sum(x):
    return jnp.sum(x, axis=0, keepdims=True)


def build_pair(col, rows, put, length_z):
    def part(step, unused):
        at = pl.ds(pl.multiple_of(step * CHUNK, CHUNK), CHUNK)
        wide = [jnp.broadcast_to(r, (CHUNK, BLOCK)) for r in rows]
        dx = wrap_unit(col[0, at, :] - wide[0])
        dy = wrap_unit(col[1, at, :] - wide[1])
        dz = wrap_z(col[2, at, :] - wide[2], length_z)
        keep = col[4, at, :] != wide[4]
        dist = jnp.where(keep, dx * dx + dy * dy + dz * dz, 1.0)
        inv = lax.rsqrt(dist)
        inv_two = inv * inv
        inv_three = inv * inv_two
        s = dist * (dist * inv) * (col[3, at, :] * wide[3])
        decay = jnp.exp(-s)
        small = s * (1.0 - s * (0.5 - s * (1.0 / 6.0 - s * (1.0 / 24.0 - s * (1.0 / 120.0)))))
        three = jnp.where(s < 0.0625, small, 1.0 - decay)
        five = 3.0 * (three - s * decay) * (inv_three * inv_two)
        three = jnp.where(keep, three * inv_three, 0.0)
        five = jnp.where(keep, five, 0.0)
        for k, value in enumerate(tensor(five, three, dx, dy, dz)):
            put(k, at, value)
        return unused

    lax.fori_loop(0, BLOCK // CHUNK, part, 0)


def project(phi, v, tiles):
    out = []
    per = tiles // BOXES_DEV
    for box in range(BOXES_DEV):
        wide = [[spread(v[box * per + t], c) for c in range(3)] for t in range(per)]

        def part(step, acc):
            at = pl.ds(pl.multiple_of(step * SUB, SUB), SUB)
            sums = [None] * 3
            for t in range(per):
                value = phi[box * per + t, at, :]
                for c in range(3):
                    term = value * wide[t][c]
                    sums[c] = term if sums[c] is None else sums[c] + term
            mask = diagonal(step)
            return tuple(
                a + jnp.where(mask, jnp.sum(x, axis=1, keepdims=True), 0.0)
                for a, x in zip(acc, sums)
            )

        zero = jnp.zeros((SUB, BLOCK), f32)
        acc = lax.fori_loop(0, BLOCK // SUB, part, (zero, zero, zero))
        out += [row_sum(a) for a in acc]
    return out


def edges(meta, put_core, put_ring, tiles, reach):
    even = meta[0] % 2 == 0
    high, low = tiles - reach, 0
    put_core(jnp.where(even, high, low))
    put_ring(jnp.where(even, low, high))


def first_body(
    meta, pos, alpha, field, gid, picks, stat, x0, phi, weights, core, ring, *, coeff, box_height, tiles, reach
):
    total = tiles * BLOCK
    lane = lax.broadcasted_iota(jnp.int32, (1, total), 1)
    first = meta[0] * BOXES_DEV
    box = jnp.where(lane < total // BOXES_DEV, first, first + 1).astype(f32)
    p = pos[...]
    al = alpha[...]
    coords = [
        p[0:1] / 16.0 - 1.0,
        p[1:2] / 16.0 - 1.0,
        2.0 * (p[2:3] - box * box_height) / box_height - 1.0,
    ]
    levels = []
    for u in coords:
        terms = [None, u]
        for degree in range(2, ORDER):
            prev = terms[-2] if degree > 2 else 1.0
            terms.append(2.0 * u * terms[-1] - prev)
        rows = []
        for k in range(ORDER):
            value = float(coeff[k, 0]) + float(coeff[k, 1]) * terms[1]
            for n in range(2, ORDER):
                value = value + float(coeff[k, n]) * terms[n]
            rows.append(value)
        levels.append(jnp.concatenate(rows + [jnp.zeros((8 - ORDER, total), f32)], axis=0))
    wide = 4 * BLOCK
    for begin in range(0, total, wide):
        value = None
        for d in range(3):
            part = jnp.dot(
                picks[d], levels[d][:, begin : begin + wide], precision=highest, preferred_element_type=f32
            )
            value = part if value is None else value * part
        for t in range(4):
            phi[begin // BLOCK + t] = value[:, t * BLOCK : (t + 1) * BLOCK]
    start = al * field[...]
    scaled = jnp.concatenate(
        [
            p[0:2] * (1.0 / side_length),
            p[2:3],
            lax.rsqrt(al) * math.sqrt(thole_damp),
            gid[...].astype(f32),
            al,
            jnp.zeros((2, total), f32),
        ],
        axis=0,
    )
    vec = jnp.concatenate([start, jnp.zeros((5, total), f32)], axis=0)
    for t in range(tiles):
        stat[t] = scaled[:, t * BLOCK : (t + 1) * BLOCK]
        x0[t] = vec[:, t * BLOCK : (t + 1) * BLOCK]
    rows = project(phi, x0, tiles)
    weights[...] = jnp.concatenate(rows + [jnp.zeros((2, BLOCK), f32)], axis=0)

    def put(ref):
        def at(begin):
            for k in range(reach):
                ref[k] = stat[begin + k]
                ref[reach + k] = x0[begin + k]

        return at

    edges(meta, put(core), put(ring), tiles, reach)


def own_slot(b, begin, tiles, reach):
    k = jnp.maximum(b - (tiles - reach), 0)
    return (b - begin) * (reach + 1) - k * (k + 1) // 2


def own_slots(begin, end, tiles, reach):
    return sum(min(reach + 1, tiles - b) for b in range(begin, end))


def tensors_body(mask, stat, out, col, *, begin, end, tiles, reach, length_z):
    def visit(b, unused):
        def put(k, value):
            col[k] = value

        columns(stat[b], 5, put)
        slot = own_slot(b, begin, tiles, reach)
        for o in range(reach + 1):

            @pl.when((b + o < tiles) & (mask[b * (2 * reach + 1) + reach + o] != 0))
            def _():
                other = stat[b + o]
                rows = [other[k : k + 1, :] for k in range(5)]

                def store(k, at, value):
                    out[slot + o, k, at, :] = value

                build_pair(col, rows, store, length_z)

        return unused

    lax.fori_loop(begin, end, visit, 0)


def own_body(mask, v, *rest, ranges, tiles, reach):
    tabs = rest[: len(ranges)]
    out, acc_i, acc_j, col = rest[len(ranges) :]

    def clear(t, unused):
        for c in range(3):
            acc_j[t, c] = jnp.zeros((SUB, BLOCK), f32)
        return unused

    lax.fori_loop(0, tiles, clear, 0)
    for (begin, end), tab in zip(ranges, tabs):

        def visit(b, unused):
            def put(k, value):
                col[k] = value

            columns(v[b], 3, put)
            for c in range(3):
                acc_i[c] = jnp.zeros((BLOCK, BLOCK), f32)
            slot = own_slot(b, begin, tiles, reach)
            for o in range(reach + 1):

                @pl.when((b + o < tiles) & (mask[b * (2 * reach + 1) + reach + o] != 0))
                def _():
                    other = v[b + o]
                    wide = [spread(other, c) for c in range(3)]

                    def part(step, acc):
                        at = pl.ds(pl.multiple_of(step * SUB, SUB), SUB)
                        xx, xy, xz, yy, yz, zz = [tab[slot + o, k, at, :] for k in range(6)]
                        vx, vy, vz = wide
                        acc_i[0, at, :] += xx * vx + xy * vy + xz * vz
                        acc_i[1, at, :] += xy * vx + yy * vy + yz * vz
                        acc_i[2, at, :] += xz * vx + yz * vy + zz * vz
                        if o == 0:
                            return acc
                        ux, uy, uz = [col[c, at, :] for c in range(3)]
                        return (
                            acc[0] + (xx * ux + xy * uy + xz * uz),
                            acc[1] + (xy * ux + yy * uy + yz * uz),
                            acc[2] + (xz * ux + yz * uy + zz * uz),
                        )

                    zero = jnp.zeros((SUB, BLOCK), f32)
                    acc = lax.fori_loop(0, BLOCK // SUB, part, (zero, zero, zero), unroll=4)
                    if o > 0:
                        for c in range(3):
                            acc_j[b + o, c] += acc[c]

            for c in range(3):
                total = acc_j[b, c]
                for step in range(BLOCK // SUB):
                    value = jnp.sum(acc_i[c, step * SUB : (step + 1) * SUB, :], axis=1, keepdims=True)
                    total = total + jnp.where(diagonal(step), value, 0.0)
                acc_j[b, c] = total
            return unused

        lax.fori_loop(begin, end, visit, 0)

    def finish(t, unused):
        rows = [row_sum(acc_j[t, c]) for c in range(3)]
        out[t] = jnp.concatenate(rows + [jnp.zeros((5, BLOCK), f32)], axis=0)
        return unused

    lax.fori_loop(0, tiles, finish, 0)


def halo_pairs(tiles, reach):
    pairs = []
    for l in range(reach):
        for c in range(l + 1):
            pairs.append((l, c, l - c))
    for l in range(reach):
        for c in range(tiles - reach + l, tiles):
            pairs.append((reach + l, c, reach + tiles + l - c))
    return pairs


def halo_tiles(meta, core, ring, begin, reach, put):
    even = meta[0] % 2 == 0
    for k in range(reach):
        a, b = core[begin + k], ring[begin + k]
        put(k, jnp.where(even, b, a))
        put(reach + k, jnp.where(even, a, b))


def halo_tensors_body(meta, mask, stat, core, ring, out, held, col, *, tiles, reach, length_z):
    def keep(k, value):
        held[k] = value

    halo_tiles(meta, core, ring, 0, reach, keep)
    last = None
    for index, (h, c, m) in enumerate(halo_pairs(tiles, reach)):
        if h != last:

            def put(k, value):
                col[k] = value

            columns(held[h], 5, put)
            last = h

        @pl.when(mask[c * (2 * reach + 1) + m] != 0)
        def _():
            own = stat[c]
            rows = [own[k : k + 1, :] for k in range(5)]

            def store(k, at, value):
                out[index, k, at, :] = value

            build_pair(col, rows, store, length_z)


def far_geometry(nodes, geo, box_height):
    turned = nodes[...].T
    row = nodes[...]

    def delta(k):
        return jnp.broadcast_to(turned[:, k : k + 1], (BLOCK, BLOCK)) - jnp.broadcast_to(
            row[k : k + 1, :], (BLOCK, BLOCK)
        )

    dx, dy = wrap_unit(delta(0)), wrap_unit(delta(1))
    geo[0] = dx
    geo[1] = dy
    geo[2] = box_height * delta(2)
    geo[3] = dx * dx + dy * dy + box_height * box_height


def far_tensor(geo, apart, put, box_height, length_z):
    def part(step, unused):
        at = pl.ds(pl.multiple_of(step * CHUNK, CHUNK), CHUNK)
        dx, dy = geo[0, at, :], geo[1, at, :]
        dz = wrap_z(geo[2, at, :] - apart * box_height, length_z)
        inv = lax.rsqrt(geo[3, at, :] + dz * dz)
        inv_two = inv * inv
        three = inv * inv_two
        five = 3.0 * three * inv_two
        for k, value in enumerate(tensor(five, three, dx, dy, dz)):
            put(k, at, value)
        return unused

    lax.fori_loop(0, BLOCK // CHUNK, part, 0)


def far_tensors_body(nodes, out, geo, *, box_height, length_z):
    far_geometry(nodes, geo, box_height)

    def visit(d, unused):
        def put(k, at, value):
            out[d - 1, k, at, :] = value

        far_tensor(geo, d.astype(f32), put, box_height, length_z)
        return unused

    lax.fori_loop(1, out.shape[0] + 1, visit, 0)


def apply_tensor(t, v):
    xx, xy, xz, yy, yz, zz = t
    x, y, z = v
    return (
        xx * x + xy * y + xz * z,
        xy * x + yy * y + yz * z,
        xz * x + yz * y + zz * z,
    )


def far_nodes(table, geo, wide, fcol, boxes, box_height, length_z):
    if table is not None:
        def rows(step, unused):
            at = pl.ds(pl.multiple_of(step * SUB, SUB), SUB)

            def load(d):
                return [table[d - 1, k, at, :] for k in range(6)]

            def field(t, k):
                return apply_tensor(t, [wide[k, c] for c in range(3)])

            def visit(d, acc):
                t = load(d)
                new = field(t, d) + field(t, d + 1)
                return tuple(a + n for a, n in zip(acc, new))

            acc = field(load(boxes - 1), boxes - 1) + field(load(1), 2)
            acc = lax.fori_loop(2, boxes - 1, visit, acc, unroll=4)
            for box in range(BOXES_DEV):
                for c in range(3):
                    fcol[box, c, at, :] = jnp.broadcast_to(
                        jnp.sum(acc[box * 3 + c], axis=1, keepdims=True), (SUB, BLOCK)
                    )
            return unused

        lax.fori_loop(0, BLOCK // SUB, rows, 0)
        return
    for box in range(BOXES_DEV):
        for c in range(3):
            fcol[box, c] = jnp.zeros((BLOCK, BLOCK), f32)

    def visit(d, unused):
        def hold(k, at, value):
            geo[4 + k, at, :] = value

        far_tensor(geo, d.astype(f32), hold, box_height, length_z)
        for box in range(BOXES_DEV):

            @pl.when(d < boxes - 1 if box else d > 1)
            def _():
                v = [wide[d + box, c] for c in range(3)]

                def part(step, skip):
                    at = pl.ds(pl.multiple_of(step * SUB, SUB), SUB)
                    new = apply_tensor([geo[4 + k, at, :] for k in range(6)], v)
                    for c in range(3):
                        fcol[box, c, at, :] += new[c]
                    return skip

                lax.fori_loop(0, BLOCK // SUB, part, 0)

        return unused

    lax.fori_loop(1, boxes, visit, 0)
    for box in range(BOXES_DEV):
        for c in range(3):
            fcol[box, c] = jnp.broadcast_to(
                jnp.sum(fcol[box, c], axis=1, keepdims=True), (BLOCK, BLOCK)
            )


def field_body(meta, mask, nodes, stat, v, near, phi, gathered, core, ring, halo_tab, *rest,
               mode, tiles, reach, plane, slabs, box_height, length_z, surface, kept, offset):
    rest = list(rest)
    table = rest.pop(0) if kept else None
    extra = [rest.pop(0) for _ in range((0, 0, 4)[mode])]
    outs = [rest.pop(0) for _ in range((5, 6, 5)[mode])]
    acc, held, col, wide, fcol, geo = rest
    boxes = slabs * BOXES_DEV
    member = meta[0]
    own_row, own_col = member // plane, member % plane

    def expand(k, total):
        other = lax.rem(member + k, slabs)
        slot = lax.bitwise_xor(other // plane, own_row) * plane + lax.bitwise_xor(other % plane, own_col)
        tile = gathered[slot]
        for box in range(BOXES_DEV):
            for c in range(3):
                wide[k * BOXES_DEV + box, c] = spread(tile, box * 3 + c)
        return total + tile

    total = lax.fori_loop(0, slabs, expand, jnp.zeros((SUB, BLOCK), f32))
    sums = jnp.sum(total, axis=1, keepdims=True)
    moment = [surface * (sums[c : c + 1] + sums[3 + c : 4 + c]) for c in range(3)]

    def keep(k, value):
        held[k] = value

    halo_tiles(meta, core, ring, offset, reach, keep)

    def clear(t, unused):
        for c in range(3):
            acc[t, c] = jnp.zeros((SUB, BLOCK), f32)
        return unused

    lax.fori_loop(0, tiles, clear, 0)
    last = None
    for index, (h, c, m) in enumerate(halo_pairs(tiles, reach)):
        if h != last:

            def put(k, value):
                col[k] = value

            columns(held[h], 3, put)
            last = h

        @pl.when(mask[c * (2 * reach + 1) + m] != 0)
        def _():
            def part(step, sofar):
                at = pl.ds(pl.multiple_of(step * SUB, SUB), SUB)
                new = apply_tensor(
                    [halo_tab[index, k, at, :] for k in range(6)], [col[k, at, :] for k in range(3)]
                )
                return tuple(a + n for a, n in zip(sofar, new))

            zero = jnp.zeros((SUB, BLOCK), f32)
            new = lax.fori_loop(0, BLOCK // SUB, part, (zero, zero, zero), unroll=4)
            for k in range(3):
                acc[c, k] += new[k]

    if not kept:
        far_geometry(nodes, geo, box_height)
    far_nodes(table, geo, wide, fcol, boxes, box_height, length_z)

    per = tiles // BOXES_DEV
    zero = jnp.zeros((5, BLOCK), f32)
    fields = []
    for t in range(tiles):
        box = t // per
        sofar = [acc[t, c] for c in range(3)]
        for step in range(BLOCK // SUB):
            at = slice(step * SUB, (step + 1) * SUB)
            value = phi[t, at, :]
            sofar = [a + value * fcol[box, c, at, :] for c, a in enumerate(sofar)]
        rows = [row_sum(a) - m for a, m in zip(sofar, moment)]
        fields.append(near[t] + jnp.concatenate(rows + [zero], axis=0))

    def alpha(t):
        return spread(stat[t], 5)

    none = jnp.zeros((1, BLOCK), f32)

    def send(u, weights, core_out, ring_out, scalar):
        rows = project(phi, u, tiles)
        weights[...] = jnp.concatenate(rows + [scalar, none], axis=0)

        def at(ref):
            def store(begin):
                for k in range(reach):
                    ref[k] = u[begin + k]

            return store

        edges(meta, at(core_out), at(ring_out), tiles, reach)

    def fold(parts):
        out = parts[0]
        for x in parts[1:]:
            out = out + x
        return row_sum(out)

    if mode == 0:
        res, u, weights, core_out, ring_out = outs
        dots = []
        for t in range(tiles):
            scaled = alpha(t) * fields[t]
            res[t] = fields[t]
            u[t] = scaled
            dots.append(scaled * fields[t])
        send(u, weights, core_out, ring_out, fold(dots))
    elif mode == 1:
        image, u, weights, core_out, ring_out, norm = outs
        dots = []
        for t in range(tiles):
            w = v[t] / alpha(t) - fields[t]
            image[t] = w
            u[t] = alpha(t) * w
            dots.append(v[t] * w)
        norm[...] = jnp.broadcast_to(sums[6:7], (SUB, BLOCK))
        send(u, weights, core_out, ring_out, fold(dots))
    else:
        first, res, w0, norm = extra
        x1, r1, z1, q1, scal = outs
        rate = norm[...] / jnp.broadcast_to(sums[6:7], (SUB, BLOCK))
        one, two, three = [], [], []
        for t in range(tiles):
            y = v[t] / alpha(t) - fields[t]
            r = res[t] - rate * w0[t]
            z = alpha(t) * r
            q = w0[t] - rate * y
            x1[t] = first[t] + rate * (alpha(t) * res[t])
            r1[t] = r
            z1[t] = z
            q1[t] = q
            one.append(r * z)
            two.append(z * q)
            three.append(z * w0[t])
        scal[...] = jnp.concatenate(
            [fold(one), fold(two), fold(three), jnp.broadcast_to(sums[6:7], (1, BLOCK)), norm[0:1], none, none, none],
            axis=0,
        )


def last_body(gathered, scal, stat, res, w0, x1, r1, z1, q1, dip, out, *, tiles):
    total = gathered[0]
    for k in range(1, gathered.shape[0]):
        total = total + gathered[k]
    sums = jnp.sum(total, axis=1, keepdims=True)

    def value(x):
        return jnp.broadcast_to(x, (1, BLOCK))

    norm, curve, cross = value(sums[0:1]), value(sums[1:2]), value(sums[2:3])
    along, start = scal[3:4], scal[4:5]
    beta = norm / start
    rate = norm / (curve + 2.0 * beta * cross + beta * beta * along)
    for t in range(tiles):
        at = slice(t * BLOCK, (t + 1) * BLOCK)
        u0 = stat[t][5:6] * res[t][0:3]
        p = z1[t][0:3] + beta * u0
        w = q1[t][0:3] + beta * w0[t][0:3]
        dip[:, at] = x1[t][0:3] + rate * p
        out[:, at] = r1[t][0:3] - rate * w


def swap(x, axes, count):
    got = [x]
    for s in range(1, count):
        got.append(lax.ppermute(x, axes, [(i, i ^ s) for i in range(count)]))
    return got


def gather(x, plane, rows):
    near = jnp.stack(swap(x, ("oct", "sub"), plane))
    return jnp.concatenate(swap(near, "blk", rows), axis=0)


def halo(core, ring):
    count = lax.axis_size(RING)
    size = lax.axis_size("sub")
    got_core = lax.ppermute(core, "sub", [(i, i ^ 1) for i in range(size)])
    pairs = [(i, (i + 1) % count) for i in range(1, count, 2)]
    got_ring = lax.ppermute(ring, RING, pairs + [(b, a) for a, b in pairs])
    return got_core, got_ring


def on_device(positions, polarizability, permanent_field, group_id, pair_mask):
    slabs = lax.axis_size(RING)
    member = lax.axis_index(RING)
    plane = lax.axis_size(("oct", "sub"))
    rows = lax.axis_size("blk")
    atoms = positions.shape[1]
    tiles = atoms // BLOCK
    length_z = layer_gap * atoms * slabs / 256.0
    boxes = BOXES_DEV * slabs
    box_height = length_z / boxes
    reach = (pair_mask.shape[1] - 1) // 2
    surface = 4.0 * math.pi / 3.0 / (side_length * side_length * length_z)
    coeff, picks, nodes = node_tables()
    nodes = jnp.asarray(nodes)
    meta = jnp.reshape(member, (1,)).astype(jnp.int32)
    mask = pair_mask.reshape(-1)
    tile_shape = (tiles, 8, BLOCK)
    edge = (reach, 8, BLOCK)
    kept = (boxes - 1) * 6 * BLOCK * BLOCK * 4 <= TABLE_LIMIT

    stat, x0, phi, weights, core, ring = call(
        functools.partial(first_body, coeff=coeff, box_height=box_height, tiles=tiles, reach=reach),
        [tile_shape, tile_shape, (tiles, BLOCK, BLOCK), (8, BLOCK), (2 * reach, 8, BLOCK), (2 * reach, 8, BLOCK)],
        [meta, positions, polarizability[None], permanent_field, group_id[None], jnp.asarray(picks)],
        smem=1,
        limit=16 << 20,
    )
    got_core, got_ring = halo(core, ring)
    gathered = gather(weights, plane, rows)

    ranges = [(0, tiles // 2), (tiles // 2, tiles)]
    tabs = []
    for begin, end in ranges:
        count = own_slots(begin, end, tiles, reach)
        tabs += call(
            functools.partial(tensors_body, begin=begin, end=end, tiles=tiles, reach=reach, length_z=length_z),
            [(count, 6, BLOCK, BLOCK)],
            [mask, stat],
            smem=1,
            scratch=[(5, BLOCK, BLOCK)],
            cost=pl.CostEstimate(flops=count * BLOCK * BLOCK * 70, bytes_accessed=1 << 20, transcendentals=count * BLOCK * BLOCK * 2),
            pinned=(0,),
        )
    table = []
    if kept:
        table = call(
            functools.partial(far_tensors_body, box_height=box_height, length_z=length_z),
            [(boxes - 1, 6, BLOCK, BLOCK)],
            [nodes],
            scratch=[(4, BLOCK, BLOCK)],
            cost=pl.CostEstimate(flops=boxes * BLOCK * BLOCK * 28, bytes_accessed=1 << 20, transcendentals=boxes * BLOCK * BLOCK),
            pinned=(0,),
        )
    (halo_tab,) = call(
        functools.partial(halo_tensors_body, tiles=tiles, reach=reach, length_z=length_z),
        [(len(halo_pairs(tiles, reach)), 6, BLOCK, BLOCK)],
        [meta, mask, stat, got_core, got_ring],
        smem=2,
        scratch=[(2 * reach, 8, BLOCK), (5, BLOCK, BLOCK)],
        pinned=(0,),
    )

    def own_field(v):
        return call(
            functools.partial(own_body, ranges=ranges, tiles=tiles, reach=reach),
            [tile_shape],
            [mask, v] + tabs,
            smem=1,
            scratch=[(3, BLOCK, BLOCK), (tiles, 3, SUB, BLOCK), (3, BLOCK, BLOCK)],
            cost=pl.CostEstimate(flops=72 * 2 * BLOCK * BLOCK * 18, bytes_accessed=1 << 20, transcendentals=0),
        )[0]

    def field(mode, v, gathered, got_core, got_ring, extra):
        near = own_field(v)
        offset = reach if mode == 0 else 0
        outs = [
            [tile_shape, tile_shape, (8, BLOCK), edge, edge],
            [tile_shape, tile_shape, (8, BLOCK), edge, edge, (SUB, BLOCK)],
            [tile_shape] * 4 + [(8, BLOCK)],
        ][mode]
        return call(
            functools.partial(
                field_body, mode=mode, tiles=tiles, reach=reach, plane=plane, slabs=slabs, box_height=box_height,
                length_z=length_z, surface=surface, kept=kept, offset=offset,
            ),
            outs,
            [meta, mask, nodes, stat, v, near, phi, gathered, got_core, got_ring, halo_tab] + table + extra,
            smem=2,
            scratch=[
                (tiles, 3, SUB, BLOCK),
                (2 * reach, 8, BLOCK),
                (3, BLOCK, BLOCK),
                (boxes, 3, SUB, BLOCK),
                (BOXES_DEV, 3, BLOCK, BLOCK),
                (10, BLOCK, BLOCK) if not kept else (1, 8, BLOCK),
            ],
        )

    r0, u0, weights, core, ring = field(0, x0, gathered, got_core, got_ring, [])
    got_core, got_ring = halo(core, ring)
    gathered = gather(weights, plane, rows)
    w0, u1, weights, core, ring, norm = field(1, u0, gathered, got_core, got_ring, [])
    got_core, got_ring = halo(core, ring)
    gathered = gather(weights, plane, rows)
    x1, r1, z1, q1, scal = field(2, u1, gathered, got_core, got_ring, [x0, r0, w0, norm])
    gathered = gather(scal, plane, rows)
    return call(
        functools.partial(last_body, tiles=tiles),
        [(3, atoms), (3, atoms)],
        [gathered, scal, stat, r0, w0, x1, r1, z1, q1],
    )


def solution(mesh):
    split = P(("groups", "blk", "oct", "sub"))
    wide = P(None, ("groups", "blk", "oct", "sub"))
    return jax.shard_map(
        lambda *args: tuple(on_device(*args)),
        mesh=mesh,
        in_specs=(wide, split, wide, split, P(("groups", "blk", "oct", "sub"), None)),
        out_specs=(wide, wide),
        check_vma=False,
    )
```

time: 434 us -> 162 us (0.37); the launches traced: 428 us -> 162 us
  blocking collectives: 237 us -> 0 us
  other arithmetic: 145 us -> 0.02 us
  Pallas kernels: 0 us -> 100 us
  starting transfers between devices: 19 us -> 36.3 us
  matrix products: 13.6 us -> 0 us
  waiting for transfers between devices: 0.02 us -> 10.1 us
  local copies, waits for them, and re-layouts: 4.24 us -> 14.2 us
  between operations: 5.57 us -> 1.05 us
    psum x6 -> x0, blocking collectives: 185 us -> none  [the longest x3 91 us: moment(): return lax.psum(jnp.sum(values, axis=1), ('blk', 'oct', 'sub'))]
    reduce_sum x33 -> x0, other arithmetic: 136 us -> none  [the longest x24 106 us: near_tiles(): jnp.sum(weighted * delta_x - coef_three * moments[0][:, None, :], axis=2)]
    pallas_call x0 -> x12, Pallas kernels: none -> 100 us  [call(): pl.pallas_call(body, out_shape=shapes, in_specs=[SM] * smem + [VM] * (len...]
    all_gather x3 -> x0, blocking collectives: 52 us -> none  [induced(): piece = lax.all_gather(weights, ('blk', 'oct', 'sub'), axis=0, tiled=True)]
    ppermute x8 -> x30, starting transfers between devices: 19 us -> 36.3 us  [the longest x24 26.6 us: swap(): got.append(lax.ppermute(x, axes, [(i, i ^ s) for i in range(count)]))]
    dot_general x12 -> x0, matrix products: 13.6 us -> none  [the longest x3 5.43 us: basis(): return jnp.einsum('pk,kba->pba', picks, smooth, precision=highest)]
    unnamed x27 -> x50, local copies, waits for them, and re-layouts: 0.09 us -> 13.4 us
    ppermute x8 -> x30, waiting for transfers between devices: 0.02 us -> 10.1 us  [the longest x24 10.1 us: swap(): got.append(lax.ppermute(x, axes, [(i, i ^ s) for i in range(count)]))]
  transfers between devices with their start and end apart: 8 -> 30, of which waited for: 0 -> 8; matrix products, arithmetic and copies ran while one was open for 11% -> 1% of each run, Pallas kernels for 0% -> 35%
where the time goes in v1:
time: 162 us
  Pallas kernels  100 us (62%)
  starting transfers between devices  36.3 us (22%)
  local copies, waits for them, and re-layouts  14.2 us (9%)
  waiting for transfers between devices  10.1 us (6%)
    pallas_call x12, Pallas kernels, call(): pl.pallas_call(body, out_shape=shapes, in_specs=[SM] * smem + [VM] * (len...  100 us
    ppermute x24, starting transfers between devices, swap(): got.append(lax.ppermute(x, axes, [(i, i ^ s) for i in range(count)]))  26.6 us
    unnamed x50, local copies, waits for them, and re-layouts  13.4 us
    ppermute x24, waiting for transfers between devices, swap(): got.append(lax.ppermute(x, axes, [(i, i ^ s) for i in range(count)]))  10.1 us
    ppermute x3, starting transfers between devices, halo(): got_ring = lax.ppermute(ring, RING, pairs + [(b, a) for a, b in pairs])  8.96 us
  transfers between devices with their start and end apart: 30, of which 8 were waited for; matrix products, arithmetic and copies ran while one was open for 1% of the time, Pallas kernels for 35%

profile of v1, /device:TPU:0, one launch (start us, length us, event | category | flops | bytes accessed | tf_op | source)
XLA Modules:
  0.0 161.7 jit_solution(16341041965493673610)
XLA Ops:
  4.5 5.5 %shard_map.86 = (f32[16,8,128]{2,1,0:T(8,128)S(1)}, f32[16,8,128]{2,1,0:T(8,128)S(1)}, f32[16,128,128]{2,1,0:T(8,128)S(1)}, f32[8,128]{1,0:T(8,128)S(1)}, f32[8,...) custom-call(s32[1]{0:T(128)} %bitcast.meta, f32[3,2048]{1,0:T(4,128)S(1)} %copy-done.6, f32[1,2048]{1,0:T(1,128)S(1)} %bitcast.41, ...), custom_call_target="tpu_custom_call" | custom-call | tf_op jit(solution)/shard_map/pallas_call | solution.py:37
  10.0 2.4 %collective-permute-start.2 = (f32[8,128]{1,0:T(8,128)S(1)}, f32[8,128]{1,0:T(8,128)S(1)}, u32[]{:S(2)}, u32[]{:S(2)}) collective-permute-start(f32[8,128]{1,0:T(8,128)S(1)} %get-tuple-element.27), channel_id=1, source_target_pairs={{0,3},{1,2},{2,1},{3,0},{4,7},{5,6},{6,5},{7,4},{8,11},{9,10},{10,... | collective-permute-start | bytes 12296 | tf_op jit(solution)/shard_map/ppermute | solution.py:656
  13.6 4.4 %collective-permute-start.7 = (f32[8,8,128]{2,1,0:T(8,128)S(1)}, f32[8,8,128]{2,1,0:T(8,128)S(1)}, u32[]{:S(2)}, u32[]{:S(2)}) collective-permute-start(f32[8,8,128]{2,1,0:T(8,128)S(1)} %get-tuple-element.29), channel_id=1, source_target_pairs={{1,2},{3,4},{5,6},{7,8},{9,10},{11,12},{13,14},{15,0},{2,1},{4,3},... | collective-permute-start | bytes 98312 | tf_op jit(solution)/shard_map/ppermute | solution.py:670
  18.8 7.5 %shard_map.88.rest_1_ = f32[30,6,128,128]{3,2,1,0:T(8,128)S(1)} custom-call(s32[144]{0:T(256)S(1)} %reshape.11.mask, f32[16,8,128]{2,1,0:T(8,128)S(1)} %get-tuple-element.24.stat), custom_call_target="tpu_custom_call" | custom-call | flops 34406400 | bytes 1048576 | tf_op jit(solution)/shard_map/pallas_call | solution.py:37
  26.4 9.2 %shard_map.87.rest_0_ = f32[40,6,128,128]{3,2,1,0:T(8,128)S(1)} custom-call(s32[144]{0:T(256)S(1)} %reshape.11.mask, f32[16,8,128]{2,1,0:T(8,128)S(1)} %get-tuple-element.24.stat), custom_call_target="tpu_custom_call" | custom-call | flops 45875200 | bytes 1048576 | tf_op jit(solution)/shard_map/pallas_call | solution.py:37
  35.6 4.0 %shard_map.91.rest_0_ = f32[31,6,128,128]{3,2,1,0:T(8,128)S(1)} custom-call(f32[8,128]{1,0:T(8,128)S(1)} %copy-done.5), custom_call_target="tpu_custom_call" | custom-call | flops 14680064 | bytes 1048576 | tf_op jit(solution)/shard_map/pallas_call | solution.py:37
  39.6 12.0 %shard_map.89.near = f32[16,8,128]{2,1,0:T(8,128)S(1)} custom-call(s32[144]{0:T(256)S(1)} %reshape.11.mask, f32[16,8,128]{2,1,0:T(8,128)S(1)} %get-tuple-element.25.v.rest_1_, f32[40,6,128,128]{3,2,1,0:T(8,128)S(1)} %shard_map.87.rest_0_, f32[30,6,128,128]{3,2,1,0:T(8,128)S(1)} %shard_map.88.rest_1_), custom_call_target="tpu_custom_call" | custom-call | flops 42467328 | bytes 1048576 | tf_op jit(solution)/shard_map/pallas_call | solution.py:37
  52.1 3.9 %collective-permute-start.3 = (f32[4,8,128]{2,1,0:T(8,128)S(1)}, f32[4,8,128]{2,1,0:T(8,128)S(1)}, u32[]{:S(2)}, u32[]{:S(2)}) collective-permute-start(f32[4,8,128]{2,1,0:T(8,128)S(1)} %pad_maximum_fusion), channel_id=1, source_target_pairs={{0,4},{4,0},{8,12},{12,8},{1,5},{5,1},{9,13},{13,9},{2,6},{6,2},{1... | collective-permute-start | bytes 49160 | tf_op jit(solution)/shard_map/ppermute | solution.py:656
  57.9 5.6 %shard_map.90.halo_tab = f32[20,6,128,128]{3,2,1,0:T(8,128)S(1)} custom-call(s32[1]{0:T(128)} %bitcast.meta, s32[144]{0:T(256)S(1)} %reshape.11.mask, f32[16,8,128]{2,1,0:T(8,128)S(1)} %get-tuple-element.24.stat, f32[8,8,128]{2,1,0:T(8,128)S(1)} %collective-permute-done.6.core, f32[8,8,128]{2,1,0:T(8,128)S(1)} %collective-permute-done.7.ring), custom_call_target="tpu_custom_call" | custom-call | tf_op jit(solution)/shard_map/pallas_call | solution.py:37
  63.5 11.4 %shard_map.92 = (f32[16,8,128]{2,1,0:T(8,128)S(1)}, f32[16,8,128]{2,1,0:T(8,128)S(1)}, f32[8,128]{1,0:T(8,128)S(1)}, f32[4,8,128]{2,1,0:T(8,128)S(1)}, f32[4,8,128]{2,1,0:T(8,128)S(1)}) custom-call(s32[1]{0:T(128)} %bitcast.meta, s32[144]{0:T(256)S(1)} %reshape.11.mask, f32[8,128]{1,0:T(8,128)S(1)} %copy-done.5, f32[16,8,128]{2,1,0:T(8,128)S(1)} %get-tuple-element.24.stat, ...), custom_call_target="tpu_custom_call" | custom-call | tf_op jit(solution)/shard_map/pallas_call | solution.py:37
  74.9 3.0 %copy-done.1 = f32[20,6,128,128]{3,2,1,0:T(8,128)} copy-done((f32[20,6,128,128]{3,2,1,0:T(8,128)}, f32[20,6,128,128]{3,2,1,0:T(8,128)S(1)}, u32[]{:S(2)}) %copy-start.1) | copy-done | bytes 7864344
  80.1 2.4 %collective-permute-start.15 = (f32[4,8,128]{2,1,0:T(8,128)S(1)}, f32[4,8,128]{2,1,0:T(8,128)S(1)}, u32[]{:S(2)}, u32[]{:S(2)}) collective-permute-start(f32[4,8,128]{2,1,0:T(8,128)S(1)} %get-tuple-element.33), channel_id=1, source_target_pairs={{1,2},{3,4},{5,6},{7,8},{9,10},{11,12},{13,14},{15,0},{2,1},{4,3},... | collective-permute-start | bytes 49160 | tf_op jit(solution)/shard_map/ppermute | solution.py:670
  82.5 12.0 %shard_map.93.near = f32[16,8,128]{2,1,0:T(8,128)S(1)} custom-call(s32[144]{0:T(256)S(1)} %reshape.11.mask, f32[16,8,128]{2,1,0:T(8,128)S(1)} %get-tuple-element.30.v, f32[40,6,128,128]{3,2,1,0:T(8,128)S(1)} %shard_map.87.rest_0_, f32[30,6,128,128]{3,2,1,0:T(8,128)S(1)} %bitcast.36), custom_call_target="tpu_custom_call" | custom-call | flops 42467328 | bytes 1048576 | tf_op jit(solution)/shard_map/pallas_call | solution.py:37
  96.4 2.7 %collective-permute-start.11 = (f32[4,8,128]{2,1,0:T(8,128)S(1)}, f32[4,8,128]{2,1,0:T(8,128)S(1)}, u32[]{:S(2)}, u32[]{:S(2)}) collective-permute-start(f32[4,8,128]{2,1,0:T(8,128)S(1)} %pad_maximum_fusion.1), channel_id=1, source_target_pairs={{0,4},{4,0},{8,12},{12,8},{1,5},{5,1},{9,13},{13,9},{2,6},{6,2},{1... | collective-permute-start | bytes 49160 | tf_op jit(solution)/shard_map/ppermute | solution.py:656
  101.0 3.2 %copy-done.2 = f32[20,6,128,128]{3,2,1,0:T(8,128)S(1)} copy-done((f32[20,6,128,128]{3,2,1,0:T(8,128)S(1)}, f32[20,6,128,128]{3,2,1,0:T(8,128)}, u32[]{:S(2)}) %copy-start.2) | copy-done | bytes 7864344
  104.2 11.5 %shard_map.94 = (f32[16,8,128]{2,1,0:T(8,128)S(1)}, f32[16,8,128]{2,1,0:T(8,128)S(1)}, f32[8,128]{1,0:T(8,128)S(1)}, f32[4,8,128]{2,1,0:T(8,128)S(1)}, f32[4,8,128]{2,1,0:T(8,128)S(1)}, /*index=5*/f32[8,128]{1,0:T(8,128)S(1)}) custom-call(s32[1]{0:T(128)} %bitcast.meta, s32[144]{0:T(256)S(1)} %reshape.11.mask, f32[8,128]{1,0:T(8,128)S(1)} %copy-done.5, ...), custom_call_target="tpu_custom_call" | custom-call | tf_op jit(solution)/shard_map/pallas_call | solution.py:37
  117.7 2.1 %collective-permute-start.23 = (f32[4,8,128]{2,1,0:T(8,128)S(1)}, f32[4,8,128]{2,1,0:T(8,128)S(1)}, u32[]{:S(2)}, u32[]{:S(2)}) collective-permute-start(f32[4,8,128]{2,1,0:T(8,128)S(1)} %get-tuple-element.37), channel_id=1, source_target_pairs={{1,2},{3,4},{5,6},{7,8},{9,10},{11,12},{13,14},{15,0},{2,1},{4,3},... | collective-permute-start | bytes 49160 | tf_op jit(solution)/shard_map/ppermute | solution.py:670
  119.8 12.0 %shard_map.95.near = f32[16,8,128]{2,1,0:T(8,128)S(1)} custom-call(s32[144]{0:T(256)S(1)} %reshape.11.mask, f32[16,8,128]{2,1,0:T(8,128)S(1)} %get-tuple-element.34.v, f32[40,6,128,128]{3,2,1,0:T(8,128)S(1)} %shard_map.87.rest_0_, f32[30,6,128,128]{3,2,1,0:T(8,128)S(1)} %bitcast.36), custom_call_target="tpu_custom_call" | custom-call | flops 42467328 | bytes 1048576 | tf_op jit(solution)/shard_map/pallas_call | solution.py:37
  131.9 2.2 %collective-permute-start.21 = (f32[4,8,128]{2,1,0:T(8,128)S(1)}, f32[4,8,128]{2,1,0:T(8,128)S(1)}, u32[]{:S(2)}, u32[]{:S(2)}) collective-permute-start(f32[4,8,128]{2,1,0:T(8,128)S(1)} %pad_maximum_fusion.2), channel_id=1, source_target_pairs={{0,12},{4,8},{8,4},{12,0},{1,13},{5,9},{9,5},{13,1},{2,14},{6,10},... | collective-permute-start | bytes 49160 | tf_op jit(solution)/shard_map/ppermute | solution.py:656
  134.1 2.2 %collective-permute-start.19 = (f32[4,8,128]{2,1,0:T(8,128)S(1)}, f32[4,8,128]{2,1,0:T(8,128)S(1)}, u32[]{:S(2)}, u32[]{:S(2)}) collective-permute-start(f32[4,8,128]{2,1,0:T(8,128)S(1)} %pad_maximum_fusion.2), channel_id=1, source_target_pairs={{0,4},{4,0},{8,12},{12,8},{1,5},{5,1},{9,13},{13,9},{2,6},{6,2},{1... | collective-permute-start | bytes 49160 | tf_op jit(solution)/shard_map/ppermute | solution.py:656
  138.8 3.2 %copy-done.3 = f32[20,6,128,128]{3,2,1,0:T(8,128)S(1)} copy-done((f32[20,6,128,128]{3,2,1,0:T(8,128)S(1)}, f32[20,6,128,128]{3,2,1,0:T(8,128)}, u32[]{:S(2)}) %copy-start.3) | copy-done | bytes 7864344
  142.0 8.5 %shard_map.96 = (f32[16,8,128]{2,1,0:T(8,128)S(1)}, f32[16,8,128]{2,1,0:T(8,128)S(1)}, f32[16,8,128]{2,1,0:T(8,128)S(1)}, f32[16,8,128]{2,1,0:T(8,128)S(1)}, f32[8,128]{1,0:T(8,128)S(1)}) custom-call(s32[1]{0:T(128)} %bitcast.meta, s32[144]{0:T(256)S(1)} %reshape.11.mask, f32[8,128]{1,0:T(8,128)S(1)} %copy-done.5, f32[16,8,128]{2,1,0:T(8,128)S(1)} %get-tuple-element.24.stat, ...), custom_call_target="tpu_custom_call" | custom-call | tf_op jit(solution)/shard_map/pallas_call | solution.py:37
  154.3 1.8 %collective-permute-start.29 = (f32[4,8,128]{2,1,0:T(8,128)S(1)}, f32[4,8,128]{2,1,0:T(8,128)S(1)}, u32[]{:S(2)}, u32[]{:S(2)}) collective-permute-start(f32[4,8,128]{2,1,0:T(8,128)S(1)} %pad_maximum_fusion.3), channel_id=1, source_target_pairs={{0,12},{4,8},{8,4},{12,0},{1,13},{5,9},{9,5},{13,1},{2,14},{6,10},... | collective-permute-start | bytes 49160 | tf_op jit(solution)/shard_map/ppermute | solution.py:656
  158.7 2.2 %collective-permute-done.27 = f32[4,8,128]{2,1,0:T(8,128)S(1)} collective-permute-done((f32[4,8,128]{2,1,0:T(8,128)S(1)}, f32[4,8,128]{2,1,0:T(8,128)S(1)}, u32[]{:S(2)}, u32[]{:S(2)}) %collective-permute-start.27) | collective-permute-done | bytes 16416 | tf_op jit(solution)/shard_map/ppermute | solution.py:656
  (108 shorter events, 25.4 us)
Async XLA Ops:
  10.0 41.6 %collective-permute-start.2 = (f32[8,128]{1,0:T(8,128)S(1)}, f32[8,128]{1,0:T(8,128)S(1)}, u32[]{:S(2)}, u32[]{:S(2)}) collective-permute-start(f32[8,128]{1,0:T(8,128)S(1)} %get-tuple-element.27), channel_id=1, source_target_pairs={{0,3},{1,2},{2,1},{3,0},{4,7},{5,6},{6,5},{7,4},{8,11},{9,10},{10,... | collective-permute-start | bytes 12296 | tf_op jit(solution)/shard_map/ppermute | solution.py:656
  12.4 39.2 %collective-permute-start.1 = (f32[8,128]{1,0:T(8,128)S(1)}, f32[8,128]{1,0:T(8,128)S(1)}, u32[]{:S(2)}, u32[]{:S(2)}) collective-permute-start(f32[8,128]{1,0:T(8,128)S(1)} %get-tuple-element.27), channel_id=1, source_target_pairs={{0,2},{1,3},{2,0},{3,1},{4,6},{5,7},{6,4},{7,5},{8,10},{9,11},{10,... | collective-permute-start | bytes 12296 | tf_op jit(solution)/shard_map/ppermute | solution.py:656
  13.1 38.5 %collective-permute-start = (f32[8,128]{1,0:T(8,128)S(1)}, f32[8,128]{1,0:T(8,128)S(1)}, u32[]{:S(2)}, u32[]{:S(2)}) collective-permute-start(f32[8,128]{1,0:T(8,128)S(1)} %get-tuple-element.27), channel_id=1, source_target_pairs={{0,1},{1,0},{2,3},{3,2},{4,5},{5,4},{6,7},{7,6},{8,9},{9,8},{10,11... | collective-permute-start | bytes 12296 | tf_op jit(solution)/shard_map/ppermute | solution.py:656
  13.1 44.7 %collective-permute-start.6 = (f32[8,8,128]{2,1,0:T(8,128)S(1)}, f32[8,8,128]{2,1,0:T(8,128)S(1)}, u32[]{:S(2)}, u32[]{:S(2)}) collective-permute-start(f32[8,8,128]{2,1,0:T(8,128)S(1)} %get-tuple-element.28), channel_id=1, source_target_pairs={{0,1},{1,0},{2,3},{3,2},{4,5},{5,4},{6,7},{7,6},{8,9},{9,8},{10,11... | collective-permute-start | bytes 98312 | tf_op jit(solution)/shard_map/ppermute | solution.py:668
  13.6 44.3 %collective-permute-start.7 = (f32[8,8,128]{2,1,0:T(8,128)S(1)}, f32[8,8,128]{2,1,0:T(8,128)S(1)}, u32[]{:S(2)}, u32[]{:S(2)}) collective-permute-start(f32[8,8,128]{2,1,0:T(8,128)S(1)} %get-tuple-element.29), channel_id=1, source_target_pairs={{1,2},{3,4},{5,6},{7,8},{9,10},{11,12},{13,14},{15,0},{2,1},{4,3},... | collective-permute-start | bytes 98312 | tf_op jit(solution)/shard_map/ppermute | solution.py:670
  51.6 6.2 %collective-permute-start.5 = (f32[4,8,128]{2,1,0:T(8,128)S(1)}, f32[4,8,128]{2,1,0:T(8,128)S(1)}, u32[]{:S(2)}, u32[]{:S(2)}) collective-permute-start(f32[4,8,128]{2,1,0:T(8,128)S(1)} %pad_maximum_fusion), channel_id=1, source_target_pairs={{0,12},{4,8},{8,4},{12,0},{1,13},{5,9},{9,5},{13,1},{2,14},{6,10},... | collective-permute-start | bytes 49160 | tf_op jit(solution)/shard_map/ppermute | solution.py:656
  52.1 5.7 %collective-permute-start.4 = (f32[4,8,128]{2,1,0:T(8,128)S(1)}, f32[4,8,128]{2,1,0:T(8,128)S(1)}, u32[]{:S(2)}, u32[]{:S(2)}) collective-permute-start(f32[4,8,128]{2,1,0:T(8,128)S(1)} %pad_maximum_fusion), channel_id=1, source_target_pairs={{0,8},{4,12},{8,0},{12,4},{1,9},{5,13},{9,1},{13,5},{2,10},{6,14},... | collective-permute-start | bytes 49160 | tf_op jit(solution)/shard_map/ppermute | solution.py:656
  52.1 5.7 %collective-permute-start.3 = (f32[4,8,128]{2,1,0:T(8,128)S(1)}, f32[4,8,128]{2,1,0:T(8,128)S(1)}, u32[]{:S(2)}, u32[]{:S(2)}) collective-permute-start(f32[4,8,128]{2,1,0:T(8,128)S(1)} %pad_maximum_fusion), channel_id=1, source_target_pairs={{0,4},{4,0},{8,12},{12,8},{1,5},{5,1},{9,13},{13,9},{2,6},{6,2},{1... | collective-permute-start | bytes 49160 | tf_op jit(solution)/shard_map/ppermute | solution.py:656
  77.9 16.6 %collective-permute-start.10 = (f32[8,128]{1,0:T(8,128)S(1)}, f32[8,128]{1,0:T(8,128)S(1)}, u32[]{:S(2)}, u32[]{:S(2)}) collective-permute-start(f32[8,128]{1,0:T(8,128)S(1)} %get-tuple-element.31), channel_id=1, source_target_pairs={{0,3},{1,2},{2,1},{3,0},{4,7},{5,6},{6,5},{7,4},{8,11},{9,10},{10,... | collective-permute-start | bytes 12296 | tf_op jit(solution)/shard_map/ppermute | solution.py:656
  77.9 16.6 %collective-permute-start.9 = (f32[8,128]{1,0:T(8,128)S(1)}, f32[8,128]{1,0:T(8,128)S(1)}, u32[]{:S(2)}, u32[]{:S(2)}) collective-permute-start(f32[8,128]{1,0:T(8,128)S(1)} %get-tuple-element.31), channel_id=1, source_target_pairs={{0,2},{1,3},{2,0},{3,1},{4,6},{5,7},{6,4},{7,5},{8,10},{9,11},{10,... | collective-permute-start | bytes 12296 | tf_op jit(solution)/shard_map/ppermute | solution.py:656
  79.5 15.0 %collective-permute-start.8 = (f32[8,128]{1,0:T(8,128)S(1)}, f32[8,128]{1,0:T(8,128)S(1)}, u32[]{:S(2)}, u32[]{:S(2)}) collective-permute-start(f32[8,128]{1,0:T(8,128)S(1)} %get-tuple-element.31), channel_id=1, source_target_pairs={{0,1},{1,0},{2,3},{3,2},{4,5},{5,4},{6,7},{7,6},{8,9},{9,8},{10,11... | collective-permute-start | bytes 12296 | tf_op jit(solution)/shard_map/ppermute | solution.py:656
  79.8 21.2 %collective-permute-start.14 = (f32[4,8,128]{2,1,0:T(8,128)S(1)}, f32[4,8,128]{2,1,0:T(8,128)S(1)}, u32[]{:S(2)}, u32[]{:S(2)}) collective-permute-start(f32[4,8,128]{2,1,0:T(8,128)S(1)} %get-tuple-element.32), channel_id=1, source_target_pairs={{0,1},{1,0},{2,3},{3,2},{4,5},{5,4},{6,7},{7,6},{8,9},{9,8},{10,11... | collective-permute-start | bytes 49160 | tf_op jit(solution)/shard_map/ppermute | solution.py:668
  80.1 20.9 %collective-permute-start.15 = (f32[4,8,128]{2,1,0:T(8,128)S(1)}, f32[4,8,128]{2,1,0:T(8,128)S(1)}, u32[]{:S(2)}, u32[]{:S(2)}) collective-permute-start(f32[4,8,128]{2,1,0:T(8,128)S(1)} %get-tuple-element.33), channel_id=1, source_target_pairs={{1,2},{3,4},{5,6},{7,8},{9,10},{11,12},{13,14},{15,0},{2,1},{4,3},... | collective-permute-start | bytes 49160 | tf_op jit(solution)/shard_map/ppermute | solution.py:670
  94.6 6.4 %collective-permute-start.13 = (f32[4,8,128]{2,1,0:T(8,128)S(1)}, f32[4,8,128]{2,1,0:T(8,128)S(1)}, u32[]{:S(2)}, u32[]{:S(2)}) collective-permute-start(f32[4,8,128]{2,1,0:T(8,128)S(1)} %pad_maximum_fusion.1), channel_id=1, source_target_pairs={{0,12},{4,8},{8,4},{12,0},{1,13},{5,9},{9,5},{13,1},{2,14},{6,10},... | collective-permute-start | bytes 49160 | tf_op jit(solution)/shard_map/ppermute | solution.py:656
  96.3 4.6 %collective-permute-start.12 = (f32[4,8,128]{2,1,0:T(8,128)S(1)}, f32[4,8,128]{2,1,0:T(8,128)S(1)}, u32[]{:S(2)}, u32[]{:S(2)}) collective-permute-start(f32[4,8,128]{2,1,0:T(8,128)S(1)} %pad_maximum_fusion.1), channel_id=1, source_target_pairs={{0,8},{4,12},{8,0},{12,4},{1,9},{5,13},{9,1},{13,5},{2,10},{6,14},... | collective-permute-start | bytes 49160 | tf_op jit(solution)/shard_map/ppermute | solution.py:656
  115.8 16.1 %collective-permute-start.18 = (f32[8,128]{1,0:T(8,128)S(1)}, f32[8,128]{1,0:T(8,128)S(1)}, u32[]{:S(2)}, u32[]{:S(2)}) collective-permute-start(f32[8,128]{1,0:T(8,128)S(1)} %get-tuple-element.35), channel_id=1, source_target_pairs={{0,3},{1,2},{2,1},{3,0},{4,7},{5,6},{6,5},{7,4},{8,11},{9,10},{10,... | collective-permute-start | bytes 12296 | tf_op jit(solution)/shard_map/ppermute | solution.py:656
  115.8 16.0 %collective-permute-start.17 = (f32[8,128]{1,0:T(8,128)S(1)}, f32[8,128]{1,0:T(8,128)S(1)}, u32[]{:S(2)}, u32[]{:S(2)}) collective-permute-start(f32[8,128]{1,0:T(8,128)S(1)} %get-tuple-element.35), channel_id=1, source_target_pairs={{0,2},{1,3},{2,0},{3,1},{4,6},{5,7},{6,4},{7,5},{8,10},{9,11},{10,... | collective-permute-start | bytes 12296 | tf_op jit(solution)/shard_map/ppermute | solution.py:656
  117.2 14.7 %collective-permute-start.16 = (f32[8,128]{1,0:T(8,128)S(1)}, f32[8,128]{1,0:T(8,128)S(1)}, u32[]{:S(2)}, u32[]{:S(2)}) collective-permute-start(f32[8,128]{1,0:T(8,128)S(1)} %get-tuple-element.35), channel_id=1, source_target_pairs={{0,1},{1,0},{2,3},{3,2},{4,5},{5,4},{6,7},{7,6},{8,9},{9,8},{10,11... | collective-permute-start | bytes 12296 | tf_op jit(solution)/shard_map/ppermute | solution.py:656
  117.7 21.1 %collective-permute-start.22 = (f32[4,8,128]{2,1,0:T(8,128)S(1)}, f32[4,8,128]{2,1,0:T(8,128)S(1)}, u32[]{:S(2)}, u32[]{:S(2)}) collective-permute-start(f32[4,8,128]{2,1,0:T(8,128)S(1)} %get-tuple-element.36), channel_id=1, source_target_pairs={{0,1},{1,0},{2,3},{3,2},{4,5},{5,4},{6,7},{7,6},{8,9},{9,8},{10,11... | collective-permute-start | bytes 49160 | tf_op jit(solution)/shard_map/ppermute | solution.py:668
  117.7 21.1 %collective-permute-start.23 = (f32[4,8,128]{2,1,0:T(8,128)S(1)}, f32[4,8,128]{2,1,0:T(8,128)S(1)}, u32[]{:S(2)}, u32[]{:S(2)}) collective-permute-start(f32[4,8,128]{2,1,0:T(8,128)S(1)} %get-tuple-element.37), channel_id=1, source_target_pairs={{1,2},{3,4},{5,6},{7,8},{9,10},{11,12},{13,14},{15,0},{2,1},{4,3},... | collective-permute-start | bytes 49160 | tf_op jit(solution)/shard_map/ppermute | solution.py:670
  131.9 6.9 %collective-permute-start.21 = (f32[4,8,128]{2,1,0:T(8,128)S(1)}, f32[4,8,128]{2,1,0:T(8,128)S(1)}, u32[]{:S(2)}, u32[]{:S(2)}) collective-permute-start(f32[4,8,128]{2,1,0:T(8,128)S(1)} %pad_maximum_fusion.2), channel_id=1, source_target_pairs={{0,12},{4,8},{8,4},{12,0},{1,13},{5,9},{9,5},{13,1},{2,14},{6,10},... | collective-permute-start | bytes 49160 | tf_op jit(solution)/shard_map/ppermute | solution.py:656
  134.1 4.6 %collective-permute-start.20 = (f32[4,8,128]{2,1,0:T(8,128)S(1)}, f32[4,8,128]{2,1,0:T(8,128)S(1)}, u32[]{:S(2)}, u32[]{:S(2)}) collective-permute-start(f32[4,8,128]{2,1,0:T(8,128)S(1)} %pad_maximum_fusion.2), channel_id=1, source_target_pairs={{0,8},{4,12},{8,0},{12,4},{1,9},{5,13},{9,1},{13,5},{2,10},{6,14},... | collective-permute-start | bytes 49160 | tf_op jit(solution)/shard_map/ppermute | solution.py:656
  154.3 6.6 %collective-permute-start.29 = (f32[4,8,128]{2,1,0:T(8,128)S(1)}, f32[4,8,128]{2,1,0:T(8,128)S(1)}, u32[]{:S(2)}, u32[]{:S(2)}) collective-permute-start(f32[4,8,128]{2,1,0:T(8,128)S(1)} %pad_maximum_fusion.3), channel_id=1, source_target_pairs={{0,12},{4,8},{8,4},{12,0},{1,13},{5,9},{9,5},{13,1},{2,14},{6,10},... | collective-permute-start | bytes 49160 | tf_op jit(solution)/shard_map/ppermute | solution.py:656
  156.1 4.8 %collective-permute-start.28 = (f32[4,8,128]{2,1,0:T(8,128)S(1)}, f32[4,8,128]{2,1,0:T(8,128)S(1)}, u32[]{:S(2)}, u32[]{:S(2)}) collective-permute-start(f32[4,8,128]{2,1,0:T(8,128)S(1)} %pad_maximum_fusion.3), channel_id=1, source_target_pairs={{0,8},{4,12},{8,0},{12,4},{1,9},{5,13},{9,1},{13,5},{2,10},{6,14},... | collective-permute-start | bytes 49160 | tf_op jit(solution)/shard_map/ppermute | solution.py:656
  (19 other events, 122.1 us)

commit v2 on v1

--- a/solution.py
+++ b/solution.py
@@ -29,7 +29,7 @@
 TABLE_LIMIT = 16 << 20
 
 
-def call(body, outs, args, smem=0, scratch=(), limit=None, cost=None, pinned=()):
+def call(body, outs, args, smem=0, scratch=(), limit=None, cost=None, pinned=(), far=False, more=()):
     shapes = [
         pltpu.VMEM(shape, f32) if at in pinned else jax.ShapeDtypeStruct(shape, f32)
         for at, shape in enumerate(outs)
@@ -37,10 +37,10 @@
     return list(pl.pallas_call(
         body,
         out_shape=shapes,
-        in_specs=[SM] * smem + [VM] * (len(args) - smem),
+        in_specs=[SM] * smem + [pl.BlockSpec(memory_space=pltpu.HBM) if far else VM] * (len(args) - smem),
         out_specs=[VM] * len(outs),
-        scratch_shapes=[pltpu.VMEM(shape, f32) for shape in scratch],
-        compiler_params=pltpu.CompilerParams(vmem_limit_bytes=limit or (6 << 20)),
+        scratch_shapes=[pltpu.VMEM(shape, f32) for shape in scratch] + list(more),
+        compiler_params=pltpu.CompilerParams(vmem_limit_bytes=limit or (12 << 20)),
         cost_estimate=cost,
     )(*args))
 
@@ -75,14 +75,16 @@
 
 
 def tensor(five, three, dx, dy, dz):
-    fx, fy, fz = five * dx, five * dy, five * dz
-    return (fx * dx - three, fx * dy, fx * dz, fy * dy - three, fy * dz, fz * dz - three)
-
-
-def columns(tile, count, put):
-    turned = tile.T
-    for k in range(count):
-        put(k, jnp.broadcast_to(turned[:, k : k + 1], (BLOCK, BLOCK)))
+    five = jnp.maximum(five, 1e-36)
+    root = five * lax.rsqrt(five)
+    return (root * dx, root * dy, root * dz, three)
+
+
+def columns(tiles, count, out):
+    for t, tile in enumerate(tiles):
+        turned = tile.T
+        for k in range(count):
+            out[t, k] = jnp.broadcast_to(turned[:, k : k + 1], (BLOCK, BLOCK))
 
 
 def diagonal(step):
@@ -100,29 +102,32 @@
 
 
 def build_pair(col, rows, put, length_z):
-    def part(step, unused):
-        at = pl.ds(pl.multiple_of(step * CHUNK, CHUNK), CHUNK)
-        wide = [jnp.broadcast_to(r, (CHUNK, BLOCK)) for r in rows]
-        dx = wrap_unit(col[0, at, :] - wide[0])
-        dy = wrap_unit(col[1, at, :] - wide[1])
-        dz = wrap_z(col[2, at, :] - wide[2], length_z)
-        keep = col[4, at, :] != wide[4]
-        dist = jnp.where(keep, dx * dx + dy * dy + dz * dz, 1.0)
+    wide = [jnp.broadcast_to(r, (CHUNK, BLOCK)) for r in rows]
+    for step in range(BLOCK // CHUNK):
+        at = slice(step * CHUNK, (step + 1) * CHUNK)
+        dx = wrap_unit(col(0, at) - wide[0])
+        dy = wrap_unit(col(1, at) - wide[1])
+        dz = wrap_z(col(2, at) - wide[2], length_z)
+        keep = col(4, at) != wide[4]
+        dist = jnp.where(keep, dx * dx + dy * dy + dz * dz, 1e24)
         inv = lax.rsqrt(dist)
         inv_two = inv * inv
         inv_three = inv * inv_two
-        s = dist * (dist * inv) * (col[3, at, :] * wide[3])
+        s = dist * (dist * inv) * (col(3, at) * wide[3])
         decay = jnp.exp(-s)
-        small = s * (1.0 - s * (0.5 - s * (1.0 / 6.0 - s * (1.0 / 24.0 - s * (1.0 / 120.0)))))
-        three = jnp.where(s < 0.0625, small, 1.0 - decay)
-        five = 3.0 * (three - s * decay) * (inv_three * inv_two)
-        three = jnp.where(keep, three * inv_three, 0.0)
-        five = jnp.where(keep, five, 0.0)
-        for k, value in enumerate(tensor(five, three, dx, dy, dz)):
+        small = s * (1.0 - s * (0.5 - s * (1.0 / 6.0 - s * (1.0 / 24.0))))
+        three = jnp.where(s < 0.015625, small, 1.0 - decay)
+        five = (three - s * decay) * (3.0 * inv_two * inv_three)
+        for k, value in enumerate(tensor(five, three * inv_three, dx, dy, dz)):
             put(k, at, value)
-        return unused
-
-    lax.fori_loop(0, BLOCK // CHUNK, part, 0)
+
+
+def lane_sums(parts):
+    total = None
+    for step, x in enumerate(parts):
+        term = jnp.where(diagonal(step), jnp.sum(x, axis=1, keepdims=True), 0.0)
+        total = term if total is None else total + term
+    return total
 
 
 def project(phi, v, tiles):
@@ -130,24 +135,18 @@
     per = tiles // BOXES_DEV
     for box in range(BOXES_DEV):
         wide = [[spread(v[box * per + t], c) for c in range(3)] for t in range(per)]
-
-        def part(step, acc):
-            at = pl.ds(pl.multiple_of(step * SUB, SUB), SUB)
+        parts = [[], [], []]
+        for step in range(BLOCK // SUB):
+            at = slice(step * SUB, (step + 1) * SUB)
             sums = [None] * 3
             for t in range(per):
                 value = phi[box * per + t, at, :]
                 for c in range(3):
                     term = value * wide[t][c]
                     sums[c] = term if sums[c] is None else sums[c] + term
-            mask = diagonal(step)
-            return tuple(
-                a + jnp.where(mask, jnp.sum(x, axis=1, keepdims=True), 0.0)
-                for a, x in zip(acc, sums)
-            )
-
-        zero = jnp.zeros((SUB, BLOCK), f32)
-        acc = lax.fori_loop(0, BLOCK // SUB, part, (zero, zero, zero))
-        out += [row_sum(a) for a in acc]
+            for c in range(3):
+                parts[c].append(sums[c])
+        out += [row_sum(lane_sums(p)) for p in parts]
     return out
 
 
@@ -159,8 +158,15 @@
 
 
 def first_body(
-    meta, pos, alpha, field, gid, picks, stat, x0, phi, weights, core, ring, *, coeff, box_height, tiles, reach
+    meta, pos_in, alpha_in, field_in, gid_in, picks_in, stat, x0, phi, weights, core, ring,
+    pos, alpha, field, gid, picks, sems, *, coeff, box_height, tiles, reach
 ):
+    pairs = [(pos_in, pos), (alpha_in, alpha), (field_in, field), (gid_in, gid), (picks_in, picks)]
+    copies = [pltpu.make_async_copy(a, b, sems.at[k]) for k, (a, b) in enumerate(pairs)]
+    for copy in copies:
+        copy.start()
+    for copy in copies:
+        copy.wait()
     total = tiles * BLOCK
     lane = lax.broadcasted_iota(jnp.int32, (1, total), 1)
     first = meta[0] * BOXES_DEV
@@ -235,15 +241,13 @@
 
 
 def tensors_body(mask, stat, out, col, *, begin, end, tiles, reach, length_z):
+    columns([stat[t] for t in range(begin, end)], 5, col)
+
     def visit(b, unused):
-        def put(k, value):
-            col[k] = value
-
-        columns(stat[b], 5, put)
         slot = own_slot(b, begin, tiles, reach)
         for o in range(reach + 1):
 
-            @pl.when((b + o < tiles) & (mask[b * (2 * reach + 1) + reach + o] != 0))
+            @pl.when((b + o < tiles) & (mask[b, reach + o] != 0) if o else b >= 0)
             def _():
                 other = stat[b + o]
                 rows = [other[k : k + 1, :] for k in range(5)]
@@ -251,7 +255,7 @@
                 def store(k, at, value):
                     out[slot + o, k, at, :] = value
 
-                build_pair(col, rows, store, length_z)
+                build_pair(lambda k, at: col[b - begin, k, at, :], rows, store, length_z)
 
         return unused
 
@@ -261,68 +265,46 @@
 def own_body(mask, v, *rest, ranges, tiles, reach):
     tabs = rest[: len(ranges)]
     out, acc_i, acc_j, col = rest[len(ranges) :]
-
-    def clear(t, unused):
+    columns([v[t] for t in range(tiles)], 3, col)
+    for t in range(tiles):
         for c in range(3):
             acc_j[t, c] = jnp.zeros((SUB, BLOCK), f32)
-        return unused
-
-    lax.fori_loop(0, tiles, clear, 0)
     for (begin, end), tab in zip(ranges, tabs):
 
         def visit(b, unused):
-            def put(k, value):
-                col[k] = value
-
-            columns(v[b], 3, put)
-            for c in range(3):
-                acc_i[c] = jnp.zeros((BLOCK, BLOCK), f32)
             slot = own_slot(b, begin, tiles, reach)
             for o in range(reach + 1):
 
-                @pl.when((b + o < tiles) & (mask[b * (2 * reach + 1) + reach + o] != 0))
+                @pl.when((b + o < tiles) & (mask[b, reach + o] != 0) if o else b >= 0)
                 def _():
                     other = v[b + o]
                     wide = [spread(other, c) for c in range(3)]
-
-                    def part(step, acc):
-                        at = pl.ds(pl.multiple_of(step * SUB, SUB), SUB)
-                        xx, xy, xz, yy, yz, zz = [tab[slot + o, k, at, :] for k in range(6)]
-                        vx, vy, vz = wide
-                        acc_i[0, at, :] += xx * vx + xy * vy + xz * vz
-                        acc_i[1, at, :] += xy * vx + yy * vy + yz * vz
-                        acc_i[2, at, :] += xz * vx + yz * vy + zz * vz
-                        if o == 0:
-                            return acc
-                        ux, uy, uz = [col[c, at, :] for c in range(3)]
-                        return (
-                            acc[0] + (xx * ux + xy * uy + xz * uz),
-                            acc[1] + (xy * ux + yy * uy + yz * uz),
-                            acc[2] + (xz * ux + yz * uy + zz * uz),
-                        )
-
-                    zero = jnp.zeros((SUB, BLOCK), f32)
-                    acc = lax.fori_loop(0, BLOCK // SUB, part, (zero, zero, zero), unroll=4)
-                    if o > 0:
+                    acc = [acc_j[b + o, c] for c in range(3)] if o else None
+                    for step in range(BLOCK // SUB):
+                        at = slice(step * SUB, (step + 1) * SUB)
+                        t = [tab[slot + o, k, at, :] for k in range(4)]
+                        new = apply_tensor(t, wide)
                         for c in range(3):
-                            acc_j[b + o, c] += acc[c]
-
-            for c in range(3):
-                total = acc_j[b, c]
-                for step in range(BLOCK // SUB):
-                    value = jnp.sum(acc_i[c, step * SUB : (step + 1) * SUB, :], axis=1, keepdims=True)
-                    total = total + jnp.where(diagonal(step), value, 0.0)
-                acc_j[b, c] = total
+                            if o == 0:
+                                acc_i[b, c, at, :] = new[c]
+                            else:
+                                acc_i[b, c, at, :] += new[c]
+                        if o:
+                            new = apply_tensor(t, [col[b, c, at, :] for c in range(3)])
+                            acc = [a + n for a, n in zip(acc, new)]
+                    if o:
+                        for c in range(3):
+                            acc_j[b + o, c] = acc[c]
+
             return unused
 
         lax.fori_loop(begin, end, visit, 0)
-
-    def finish(t, unused):
-        rows = [row_sum(acc_j[t, c]) for c in range(3)]
+    for t in range(tiles):
+        rows = []
+        for c in range(3):
+            parts = [acc_i[t, c, k * SUB : (k + 1) * SUB, :] for k in range(BLOCK // SUB)]
+            rows.append(row_sum(acc_j[t, c] + lane_sums(parts)))
         out[t] = jnp.concatenate(rows + [jnp.zeros((5, BLOCK), f32)], axis=0)
-        return unused
-
-    lax.fori_loop(0, tiles, finish, 0)
 
 
 def halo_pairs(tiles, reach):
@@ -336,30 +318,21 @@
     return pairs
 
 
-def halo_tiles(meta, core, ring, begin, reach, put):
+def halo_tiles(meta, core, ring, begin, reach):
     even = meta[0] % 2 == 0
+    low, high = [], []
     for k in range(reach):
         a, b = core[begin + k], ring[begin + k]
-        put(k, jnp.where(even, b, a))
-        put(reach + k, jnp.where(even, a, b))
-
-
-def halo_tensors_body(meta, mask, stat, core, ring, out, held, col, *, tiles, reach, length_z):
-    def keep(k, value):
-        held[k] = value
-
-    halo_tiles(meta, core, ring, 0, reach, keep)
-    last = None
+        low.append(jnp.where(even, b, a))
+        high.append(jnp.where(even, a, b))
+    return low + high
+
+
+def halo_tensors_body(meta, mask, stat, core, ring, out, col, *, tiles, reach, length_z):
+    columns(halo_tiles(meta, core, ring, 0, reach), 5, col)
     for index, (h, c, m) in enumerate(halo_pairs(tiles, reach)):
-        if h != last:
-
-            def put(k, value):
-                col[k] = value
-
-            columns(held[h], 5, put)
-            last = h
-
-        @pl.when(mask[c * (2 * reach + 1) + m] != 0)
+
+        @pl.when(mask[c, m] != 0)
         def _():
             own = stat[c]
             rows = [own[k : k + 1, :] for k in range(5)]
@@ -367,7 +340,7 @@
             def store(k, at, value):
                 out[index, k, at, :] = value
 
-            build_pair(col, rows, store, length_z)
+            build_pair(lambda k, at: col[h, k, at, :], rows, store, length_z)
 
 
 def far_geometry(nodes, geo, box_height):
@@ -387,8 +360,8 @@
 
 
 def far_tensor(geo, apart, put, box_height, length_z):
-    def part(step, unused):
-        at = pl.ds(pl.multiple_of(step * CHUNK, CHUNK), CHUNK)
+    for step in range(BLOCK // CHUNK):
+        at = slice(step * CHUNK, (step + 1) * CHUNK)
         dx, dy = geo[0, at, :], geo[1, at, :]
         dz = wrap_z(geo[2, at, :] - apart * box_height, length_z)
         inv = lax.rsqrt(geo[3, at, :] + dz * dz)
@@ -397,9 +370,6 @@
         five = 3.0 * three * inv_two
         for k, value in enumerate(tensor(five, three, dx, dy, dz)):
             put(k, at, value)
-        return unused
-
-    lax.fori_loop(0, BLOCK // CHUNK, part, 0)
 
 
 def far_tensors_body(nodes, out, geo, *, box_height, length_z):
@@ -416,41 +386,38 @@
 
 
 def apply_tensor(t, v):
-    xx, xy, xz, yy, yz, zz = t
+    ex, ey, ez, three = t
     x, y, z = v
-    return (
-        xx * x + xy * y + xz * z,
-        xy * x + yy * y + yz * z,
-        xz * x + yz * y + zz * z,
-    )
+    along = ex * x + ey * y + ez * z
+    return (ex * along - three * x, ey * along - three * y, ez * along - three * z)
 
 
 def far_nodes(table, geo, wide, fcol, boxes, box_height, length_z):
     if table is not None:
         def rows(step, unused):
-            at = pl.ds(pl.multiple_of(step * SUB, SUB), SUB)
+            ats = [pl.ds(pl.multiple_of(step * 2 * SUB + k * SUB, SUB), SUB) for k in range(2)]
 
             def load(d):
-                return [table[d - 1, k, at, :] for k in range(6)]
-
-            def field(t, k):
-                return apply_tensor(t, [wide[k, c] for c in range(3)])
-
-            def visit(d, acc):
-                t = load(d)
-                new = field(t, d) + field(t, d + 1)
-                return tuple(a + n for a, n in zip(acc, new))
+                return [[table[d - 1, k, at, :] for k in range(4)] for at in ats]
+
+            def field(ts, k):
+                v = [wide[k, c] for c in range(3)]
+                return sum([apply_tensor(t, v) for t in ts], ())
 
             acc = field(load(boxes - 1), boxes - 1) + field(load(1), 2)
-            acc = lax.fori_loop(2, boxes - 1, visit, acc, unroll=4)
+            for d in range(2, boxes - 1):
+                ts = load(d)
+                new = field(ts, d) + field(ts, d + 1)
+                acc = tuple(a + n for a, n in zip(acc, new))
             for box in range(BOXES_DEV):
-                for c in range(3):
-                    fcol[box, c, at, :] = jnp.broadcast_to(
-                        jnp.sum(acc[box * 3 + c], axis=1, keepdims=True), (SUB, BLOCK)
-                    )
+                for half in range(2):
+                    for c in range(3):
+                        fcol[box, c, ats[half], :] = jnp.broadcast_to(
+                            jnp.sum(acc[box * 6 + half * 3 + c], axis=1, keepdims=True), (SUB, BLOCK)
+                        )
             return unused
 
-        lax.fori_loop(0, BLOCK // SUB, rows, 0)
+        lax.fori_loop(0, BLOCK // (2 * SUB), rows, 0)
         return
     for box in range(BOXES_DEV):
         for c in range(3):
@@ -469,7 +436,7 @@
 
                 def part(step, skip):
                     at = pl.ds(pl.multiple_of(step * SUB, SUB), SUB)
-                    new = apply_tensor([geo[4 + k, at, :] for k in range(6)], v)
+                    new = apply_tensor([geo[4 + k, at, :] for k in range(4)], v)
                     for c in range(3):
                         fcol[box, c, at, :] += new[c]
                     return skip
@@ -492,7 +459,7 @@
     table = rest.pop(0) if kept else None
     extra = [rest.pop(0) for _ in range((0, 0, 4)[mode])]
     outs = [rest.pop(0) for _ in range((5, 6, 5)[mode])]
-    acc, held, col, wide, fcol, geo = rest
+    acc, col, wide, fcol, geo = rest
     boxes = slabs * BOXES_DEV
     member = meta[0]
     own_row, own_col = member // plane, member % plane
@@ -510,40 +477,23 @@
     sums = jnp.sum(total, axis=1, keepdims=True)
     moment = [surface * (sums[c : c + 1] + sums[3 + c : 4 + c]) for c in range(3)]
 
-    def keep(k, value):
-        held[k] = value
-
-    halo_tiles(meta, core, ring, offset, reach, keep)
-
-    def clear(t, unused):
+    columns(halo_tiles(meta, core, ring, offset, reach), 3, col)
+    for t in range(tiles):
         for c in range(3):
             acc[t, c] = jnp.zeros((SUB, BLOCK), f32)
-        return unused
-
-    lax.fori_loop(0, tiles, clear, 0)
-    last = None
     for index, (h, c, m) in enumerate(halo_pairs(tiles, reach)):
-        if h != last:
-
-            def put(k, value):
-                col[k] = value
-
-            columns(held[h], 3, put)
-            last = h
-
-        @pl.when(mask[c * (2 * reach + 1) + m] != 0)
+
+        @pl.when(mask[c, m] != 0)
         def _():
-            def part(step, sofar):
-                at = pl.ds(pl.multiple_of(step * SUB, SUB), SUB)
+            sofar = [acc[c, k] for k in range(3)]
+            for step in range(BLOCK // SUB):
+                at = slice(step * SUB, (step + 1) * SUB)
                 new = apply_tensor(
-                    [halo_tab[index, k, at, :] for k in range(6)], [col[k, at, :] for k in range(3)]
+                    [halo_tab[index, k, at, :] for k in range(4)], [col[h, k, at, :] for k in range(3)]
                 )
-                return tuple(a + n for a, n in zip(sofar, new))
-
-            zero = jnp.zeros((SUB, BLOCK), f32)
-            new = lax.fori_loop(0, BLOCK // SUB, part, (zero, zero, zero), unroll=4)
+                sofar = [a + n for a, n in zip(sofar, new)]
             for k in range(3):
-                acc[c, k] += new[k]
+                acc[c, k] = sofar[k]
 
     if not kept:
         far_geometry(nodes, geo, box_height)
@@ -686,10 +636,10 @@
     coeff, picks, nodes = node_tables()
     nodes = jnp.asarray(nodes)
     meta = jnp.reshape(member, (1,)).astype(jnp.int32)
-    mask = pair_mask.reshape(-1)
+    mask = pair_mask
     tile_shape = (tiles, 8, BLOCK)
     edge = (reach, 8, BLOCK)
-    kept = (boxes - 1) * 6 * BLOCK * BLOCK * 4 <= TABLE_LIMIT
+    kept = (boxes - 1) * 4 * BLOCK * BLOCK * 4 <= TABLE_LIMIT
 
     stat, x0, phi, weights, core, ring = call(
         functools.partial(first_body, coeff=coeff, box_height=box_height, tiles=tiles, reach=reach),
@@ -697,6 +647,15 @@
         [meta, positions, polarizability[None], permanent_field, group_id[None], jnp.asarray(picks)],
         smem=1,
         limit=16 << 20,
+        far=True,
+        more=[
+            pltpu.VMEM((3, atoms), f32),
+            pltpu.VMEM((1, atoms), f32),
+            pltpu.VMEM((3, atoms), f32),
+            pltpu.VMEM((1, atoms), jnp.int32),
+            pltpu.VMEM(picks.shape, f32),
+            pltpu.SemaphoreType.DMA((5,)),
+        ],
     )
     got_core, got_ring = halo(core, ring)
     gathered = gather(weights, plane, rows)
@@ -707,10 +666,10 @@
         count = own_slots(begin, end, tiles, reach)
         tabs += call(
             functools.partial(tensors_body, begin=begin, end=end, tiles=tiles, reach=reach, length_z=length_z),
-            [(count, 6, BLOCK, BLOCK)],
+            [(count, 4, BLOCK, BLOCK)],
             [mask, stat],
             smem=1,
-            scratch=[(5, BLOCK, BLOCK)],
+            scratch=[(end - begin, 5, BLOCK, BLOCK)],
             cost=pl.CostEstimate(flops=count * BLOCK * BLOCK * 70, bytes_accessed=1 << 20, transcendentals=count * BLOCK * BLOCK * 2),
             pinned=(0,),
         )
@@ -718,7 +677,7 @@
     if kept:
         table = call(
             functools.partial(far_tensors_body, box_height=box_height, length_z=length_z),
-            [(boxes - 1, 6, BLOCK, BLOCK)],
+            [(boxes - 1, 4, BLOCK, BLOCK)],
             [nodes],
             scratch=[(4, BLOCK, BLOCK)],
             cost=pl.CostEstimate(flops=boxes * BLOCK * BLOCK * 28, bytes_accessed=1 << 20, transcendentals=boxes * BLOCK * BLOCK),
@@ -726,10 +685,10 @@
         )
     (halo_tab,) = call(
         functools.partial(halo_tensors_body, tiles=tiles, reach=reach, length_z=length_z),
-        [(len(halo_pairs(tiles, reach)), 6, BLOCK, BLOCK)],
+        [(len(halo_pairs(tiles, reach)), 4, BLOCK, BLOCK)],
         [meta, mask, stat, got_core, got_ring],
         smem=2,
-        scratch=[(2 * reach, 8, BLOCK), (5, BLOCK, BLOCK)],
+        scratch=[(2 * reach, 5, BLOCK, BLOCK)],
         pinned=(0,),
     )
 
@@ -739,7 +698,7 @@
             [tile_shape],
             [mask, v] + tabs,
             smem=1,
-            scratch=[(3, BLOCK, BLOCK), (tiles, 3, SUB, BLOCK), (3, BLOCK, BLOCK)],
+            scratch=[(tiles, 3, BLOCK, BLOCK), (tiles, 3, SUB, BLOCK), (tiles, 3, BLOCK, BLOCK)],
             cost=pl.CostEstimate(flops=72 * 2 * BLOCK * BLOCK * 18, bytes_accessed=1 << 20, transcendentals=0),
         )[0]
 
@@ -761,11 +720,10 @@
             smem=2,
             scratch=[
                 (tiles, 3, SUB, BLOCK),
-                (2 * reach, 8, BLOCK),
-                (3, BLOCK, BLOCK),
+                (2 * reach, 3, BLOCK, BLOCK),
                 (boxes, 3, SUB, BLOCK),
                 (BOXES_DEV, 3, BLOCK, BLOCK),
-                (10, BLOCK, BLOCK) if not kept else (1, 8, BLOCK),
+                (8, BLOCK, BLOCK) if not kept else (1, 8, BLOCK),
             ],
         )
 

time: 162 us -> 121 us (0.75)
  Pallas kernels: 100 us -> 68.8 us
  local copies, waits for them, and re-layouts: 14.2 us -> 4.59 us
    pallas_call x12, Pallas kernels: 100 us -> 68.8 us  [call(): pl.pallas_call(body, out_shape=shapes, in_specs=[SM] * smem + [pl.BlockSp...]
    unnamed x50 -> x38, local copies, waits for them, and re-layouts: 13.4 us -> 4.57 us
  transfers between devices with their start and end apart: 30 -> 30, of which waited for: 8 -> 6; matrix products, arithmetic and copies ran while one was open for 1% -> 0% of each run, Pallas kernels for 35% -> 32%
where the time goes in v2:
time: 121 us
  Pallas kernels  68.8 us (57%)
  starting transfers between devices  36.3 us (30%)
  waiting for transfers between devices  9.93 us (8%)
  local copies, waits for them, and re-layouts  4.59 us (4%)
    pallas_call x12, Pallas kernels, call(): pl.pallas_call(body, out_shape=shapes, in_specs=[SM] * smem + [pl.BlockSp...  68.8 us
    ppermute x24, starting transfers between devices, swap(): got.append(lax.ppermute(x, axes, [(i, i ^ s) for i in range(count)]))  26.6 us
    ppermute x24, waiting for transfers between devices, swap(): got.append(lax.ppermute(x, axes, [(i, i ^ s) for i in range(count)]))  9.91 us
    ppermute x3, starting transfers between devices, halo(): got_ring = lax.ppermute(ring, RING, pairs + [(b, a) for a, b in pairs])  9.2 us
    unnamed x38, local copies, waits for them, and re-layouts  4.57 us
  transfers between devices with their start and end apart: 30, of which 6 were waited for; matrix products, arithmetic and copies ran while one was open for 0% of the time, Pallas kernels for 32%

profile of v2, /device:TPU:0, one launch (start us, length us, event | category | flops | bytes accessed | tf_op | source)
XLA Modules:
  0.0 120.6 jit_solution(8693502352393869222)
XLA Ops:
  4.5 3.1 %shard_map.86 = (f32[16,8,128]{2,1,0:T(8,128)S(1)}, f32[16,8,128]{2,1,0:T(8,128)S(1)}, f32[16,128,128]{2,1,0:T(8,128)S(1)}, f32[8,128]{1,0:T(8,128)S(1)}, f32[8,...) custom-call(s32[1]{0:T(128)} %bitcast.meta, f32[3,2048]{1,0:T(4,128)S(1)} %copy-done.3, f32[1,2048]{1,0:T(1,128)S(1)} %bitcast.39, ...), custom_call_target="tpu_custom_call" | custom-call | tf_op jit(solution)/shard_map/pallas_call | solution.py:37
  7.6 2.4 %collective-permute-start.2 = (f32[8,128]{1,0:T(8,128)S(1)}, f32[8,128]{1,0:T(8,128)S(1)}, u32[]{:S(2)}, u32[]{:S(2)}) collective-permute-start(f32[8,128]{1,0:T(8,128)S(1)} %get-tuple-element.27), channel_id=1, source_target_pairs={{0,3},{1,2},{2,1},{3,0},{4,7},{5,6},{6,5},{7,4},{8,11},{9,10},{10,... | collective-permute-start | bytes 12296 | tf_op jit(solution)/shard_map/ppermute | solution.py:606
  11.2 4.4 %collective-permute-start.7 = (f32[8,8,128]{2,1,0:T(8,128)S(1)}, f32[8,8,128]{2,1,0:T(8,128)S(1)}, u32[]{:S(2)}, u32[]{:S(2)}) collective-permute-start(f32[8,8,128]{2,1,0:T(8,128)S(1)} %get-tuple-element.29), channel_id=1, source_target_pairs={{1,2},{3,4},{5,6},{7,8},{9,10},{11,12},{13,14},{15,0},{2,1},{4,3},... | collective-permute-start | bytes 98312 | tf_op jit(solution)/shard_map/ppermute | solution.py:620
  16.3 5.5 %shard_map.88.rest_1_ = f32[30,4,128,128]{3,2,1,0:T(8,128)S(1)} custom-call(s32[16,9]{1,0:T(8,128)S(1)} %copy-done, f32[16,8,128]{2,1,0:T(8,128)S(1)} %get-tuple-element.24.stat), custom_call_target="tpu_custom_call" | custom-call | flops 34406400 | bytes 1048576 | tf_op jit(solution)/shard_map/pallas_call | solution.py:37
  21.8 6.6 %shard_map.87.rest_0_ = f32[40,4,128,128]{3,2,1,0:T(8,128)S(1)} custom-call(s32[16,9]{1,0:T(8,128)S(1)} %copy-done, f32[16,8,128]{2,1,0:T(8,128)S(1)} %get-tuple-element.24.stat), custom_call_target="tpu_custom_call" | custom-call | flops 45875200 | bytes 1048576 | tf_op jit(solution)/shard_map/pallas_call | solution.py:37
  28.4 2.1 %shard_map.91.rest_0_ = f32[31,4,128,128]{3,2,1,0:T(8,128)S(1)} custom-call(f32[8,128]{1,0:T(8,128)S(1)} %copy-done.2), custom_call_target="tpu_custom_call" | custom-call | flops 14680064 | bytes 1048576 | tf_op jit(solution)/shard_map/pallas_call | solution.py:37
  30.5 8.0 %shard_map.89.near = f32[16,8,128]{2,1,0:T(8,128)S(1)} custom-call(s32[16,9]{1,0:T(8,128)S(1)} %copy-done, f32[16,8,128]{2,1,0:T(8,128)S(1)} %get-tuple-element.25.v.rest_1_, f32[40,4,128,128]{3,2,1,0:T(8,128)S(1)} %shard_map.87.rest_0_, f32[30,4,128,128]{3,2,1,0:T(8,128)S(1)} %shard_map.88.rest_1_), custom_call_target="tpu_custom_call" | custom-call | flops 42467328 | bytes 1048576 | tf_op jit(solution)/shard_map/pallas_call | solution.py:37
  38.7 4.3 %collective-permute-start.3 = (f32[4,8,128]{2,1,0:T(8,128)S(1)}, f32[4,8,128]{2,1,0:T(8,128)S(1)}, u32[]{:S(2)}, u32[]{:S(2)}) collective-permute-start(f32[4,8,128]{2,1,0:T(8,128)S(1)} %pad_maximum_fusion), channel_id=1, source_target_pairs={{0,4},{4,0},{8,12},{12,8},{1,5},{5,1},{9,13},{13,9},{2,6},{6,2},{1... | collective-permute-start | bytes 49160 | tf_op jit(solution)/shard_map/ppermute | solution.py:606
  43.0 1.7 %collective-permute-done.3 = f32[4,8,128]{2,1,0:T(8,128)S(1)} collective-permute-done((f32[4,8,128]{2,1,0:T(8,128)S(1)}, f32[4,8,128]{2,1,0:T(8,128)S(1)}, u32[]{:S(2)}, u32[]{:S(2)}) %collective-permute-start.3) | collective-permute-done | bytes 16416 | tf_op jit(solution)/shard_map/ppermute | solution.py:606
  44.8 3.8 %shard_map.90.halo_tab = f32[20,4,128,128]{3,2,1,0:T(8,128)S(1)} custom-call(s32[1]{0:T(128)} %bitcast.meta, s32[16,9]{1,0:T(8,128)S(1)} %copy-done, f32[16,8,128]{2,1,0:T(8,128)S(1)} %get-tuple-element.24.stat, f32[8,8,128]{2,1,0:T(8,128)S(1)} %collective-permute-done.6.core, f32[8,8,128]{2,1,0:T(8,128)S(1)} %collective-permute-done.7.ring), custom_call_target="tpu_custom_call" | custom-call | tf_op jit(solution)/shard_map/pallas_call | solution.py:37
  48.6 7.6 %shard_map.92 = (f32[16,8,128]{2,1,0:T(8,128)S(1)}, f32[16,8,128]{2,1,0:T(8,128)S(1)}, f32[8,128]{1,0:T(8,128)S(1)}, f32[4,8,128]{2,1,0:T(8,128)S(1)}, f32[4,8,128]{2,1,0:T(8,128)S(1)}) custom-call(s32[1]{0:T(128)} %bitcast.meta, s32[16,9]{1,0:T(8,128)S(1)} %copy-done, f32[8,128]{1,0:T(8,128)S(1)} %copy-done.2, f32[16,8,128]{2,1,0:T(8,128)S(1)} %get-tuple-element.24.stat, ...), custom_call_target="tpu_custom_call" | custom-call | tf_op jit(solution)/shard_map/pallas_call | solution.py:37
  56.4 1.8 %collective-permute-start.8 = (f32[8,128]{1,0:T(8,128)S(1)}, f32[8,128]{1,0:T(8,128)S(1)}, u32[]{:S(2)}, u32[]{:S(2)}) collective-permute-start(f32[8,128]{1,0:T(8,128)S(1)} %get-tuple-element.31), channel_id=1, source_target_pairs={{0,1},{1,0},{2,3},{3,2},{4,5},{5,4},{6,7},{7,6},{8,9},{9,8},{10,11... | collective-permute-start | bytes 12296 | tf_op jit(solution)/shard_map/ppermute | solution.py:606
  58.2 2.5 %collective-permute-start.15 = (f32[4,8,128]{2,1,0:T(8,128)S(1)}, f32[4,8,128]{2,1,0:T(8,128)S(1)}, u32[]{:S(2)}, u32[]{:S(2)}) collective-permute-start(f32[4,8,128]{2,1,0:T(8,128)S(1)} %get-tuple-element.33), channel_id=1, source_target_pairs={{1,2},{3,4},{5,6},{7,8},{9,10},{11,12},{13,14},{15,0},{2,1},{4,3},... | collective-permute-start | bytes 49160 | tf_op jit(solution)/shard_map/ppermute | solution.py:620
  60.7 8.0 %shard_map.93.near = f32[16,8,128]{2,1,0:T(8,128)S(1)} custom-call(s32[16,9]{1,0:T(8,128)S(1)} %copy-done, f32[16,8,128]{2,1,0:T(8,128)S(1)} %get-tuple-element.30.v, f32[40,4,128,128]{3,2,1,0:T(8,128)S(1)} %shard_map.87.rest_0_, f32[30,4,128,128]{3,2,1,0:T(8,128)S(1)} %shard_map.88.rest_1_), custom_call_target="tpu_custom_call" | custom-call | flops 42467328 | bytes 1048576 | tf_op jit(solution)/shard_map/pallas_call | solution.py:37
  70.0 3.2 %collective-permute-start.11 = (f32[4,8,128]{2,1,0:T(8,128)S(1)}, f32[4,8,128]{2,1,0:T(8,128)S(1)}, u32[]{:S(2)}, u32[]{:S(2)}) collective-permute-start(f32[4,8,128]{2,1,0:T(8,128)S(1)} %pad_maximum_fusion.1), channel_id=1, source_target_pairs={{0,4},{4,0},{8,12},{12,8},{1,5},{5,1},{9,13},{13,9},{2,6},{6,2},{1... | collective-permute-start | bytes 49160 | tf_op jit(solution)/shard_map/ppermute | solution.py:606
  73.3 1.7 %collective-permute-done.11 = f32[4,8,128]{2,1,0:T(8,128)S(1)} collective-permute-done((f32[4,8,128]{2,1,0:T(8,128)S(1)}, f32[4,8,128]{2,1,0:T(8,128)S(1)}, u32[]{:S(2)}, u32[]{:S(2)}) %collective-permute-start.11) | collective-permute-done | bytes 16416 | tf_op jit(solution)/shard_map/ppermute | solution.py:606
  75.0 7.9 %shard_map.94 = (f32[16,8,128]{2,1,0:T(8,128)S(1)}, f32[16,8,128]{2,1,0:T(8,128)S(1)}, f32[8,128]{1,0:T(8,128)S(1)}, f32[4,8,128]{2,1,0:T(8,128)S(1)}, f32[4,8,128]{2,1,0:T(8,128)S(1)}, /*index=5*/f32[8,128]{1,0:T(8,128)S(1)}) custom-call(s32[1]{0:T(128)} %bitcast.meta, s32[16,9]{1,0:T(8,128)S(1)} %copy-done, f32[8,128]{1,0:T(8,128)S(1)} %copy-done.2, ...), custom_call_target="tpu_custom_call" | custom-call | tf_op jit(solution)/shard_map/pallas_call | solution.py:37
  84.8 2.3 %collective-permute-start.23 = (f32[4,8,128]{2,1,0:T(8,128)S(1)}, f32[4,8,128]{2,1,0:T(8,128)S(1)}, u32[]{:S(2)}, u32[]{:S(2)}) collective-permute-start(f32[4,8,128]{2,1,0:T(8,128)S(1)} %get-tuple-element.37), channel_id=1, source_target_pairs={{1,2},{3,4},{5,6},{7,8},{9,10},{11,12},{13,14},{15,0},{2,1},{4,3},... | collective-permute-start | bytes 49160 | tf_op jit(solution)/shard_map/ppermute | solution.py:620
  87.1 8.0 %shard_map.95.near = f32[16,8,128]{2,1,0:T(8,128)S(1)} custom-call(s32[16,9]{1,0:T(8,128)S(1)} %copy-done, f32[16,8,128]{2,1,0:T(8,128)S(1)} %get-tuple-element.34.v, f32[40,4,128,128]{3,2,1,0:T(8,128)S(1)} %shard_map.87.rest_0_, f32[30,4,128,128]{3,2,1,0:T(8,128)S(1)} %shard_map.88.rest_1_), custom_call_target="tpu_custom_call" | custom-call | flops 42467328 | bytes 1048576 | tf_op jit(solution)/shard_map/pallas_call | solution.py:37
  96.5 3.1 %collective-permute-start.19 = (f32[4,8,128]{2,1,0:T(8,128)S(1)}, f32[4,8,128]{2,1,0:T(8,128)S(1)}, u32[]{:S(2)}, u32[]{:S(2)}) collective-permute-start(f32[4,8,128]{2,1,0:T(8,128)S(1)} %pad_maximum_fusion.2), channel_id=1, source_target_pairs={{0,4},{4,0},{8,12},{12,8},{1,5},{5,1},{9,13},{13,9},{2,6},{6,2},{1... | collective-permute-start | bytes 49160 | tf_op jit(solution)/shard_map/ppermute | solution.py:606
  99.6 1.7 %collective-permute-done.19 = f32[4,8,128]{2,1,0:T(8,128)S(1)} collective-permute-done((f32[4,8,128]{2,1,0:T(8,128)S(1)}, f32[4,8,128]{2,1,0:T(8,128)S(1)}, u32[]{:S(2)}, u32[]{:S(2)}) %collective-permute-start.19) | collective-permute-done | bytes 16416 | tf_op jit(solution)/shard_map/ppermute | solution.py:606
  101.4 7.3 %shard_map.96 = (f32[16,8,128]{2,1,0:T(8,128)S(1)}, f32[16,8,128]{2,1,0:T(8,128)S(1)}, f32[16,8,128]{2,1,0:T(8,128)S(1)}, f32[16,8,128]{2,1,0:T(8,128)S(1)}, f32[8,128]{1,0:T(8,128)S(1)}) custom-call(s32[1]{0:T(128)} %bitcast.meta, s32[16,9]{1,0:T(8,128)S(1)} %copy-done, f32[8,128]{1,0:T(8,128)S(1)} %copy-done.2, f32[16,8,128]{2,1,0:T(8,128)S(1)} %get-tuple-element.24.stat, ...), custom_call_target="tpu_custom_call" | custom-call | tf_op jit(solution)/shard_map/pallas_call | solution.py:37
  112.5 2.4 %collective-permute-start.29 = (f32[4,8,128]{2,1,0:T(8,128)S(1)}, f32[4,8,128]{2,1,0:T(8,128)S(1)}, u32[]{:S(2)}, u32[]{:S(2)}) collective-permute-start(f32[4,8,128]{2,1,0:T(8,128)S(1)} %pad_maximum_fusion.3), channel_id=1, source_target_pairs={{0,12},{4,8},{8,4},{12,0},{1,13},{5,9},{9,5},{13,1},{2,14},{6,10},... | collective-permute-start | bytes 49160 | tf_op jit(solution)/shard_map/ppermute | solution.py:606
  116.9 2.9 %collective-permute-done.27 = f32[4,8,128]{2,1,0:T(8,128)S(1)} collective-permute-done((f32[4,8,128]{2,1,0:T(8,128)S(1)}, f32[4,8,128]{2,1,0:T(8,128)S(1)}, u32[]{:S(2)}, u32[]{:S(2)}) %collective-permute-start.27) | collective-permute-done | bytes 16416 | tf_op jit(solution)/shard_map/ppermute | solution.py:606
  (94 shorter events, 17.1 us)
Async XLA Ops:
  7.6 30.9 %collective-permute-start.2 = (f32[8,128]{1,0:T(8,128)S(1)}, f32[8,128]{1,0:T(8,128)S(1)}, u32[]{:S(2)}, u32[]{:S(2)}) collective-permute-start(f32[8,128]{1,0:T(8,128)S(1)} %get-tuple-element.27), channel_id=1, source_target_pairs={{0,3},{1,2},{2,1},{3,0},{4,7},{5,6},{6,5},{7,4},{8,11},{9,10},{10,... | collective-permute-start | bytes 12296 | tf_op jit(solution)/shard_map/ppermute | solution.py:606
  10.0 28.5 %collective-permute-start.1 = (f32[8,128]{1,0:T(8,128)S(1)}, f32[8,128]{1,0:T(8,128)S(1)}, u32[]{:S(2)}, u32[]{:S(2)}) collective-permute-start(f32[8,128]{1,0:T(8,128)S(1)} %get-tuple-element.27), channel_id=1, source_target_pairs={{0,2},{1,3},{2,0},{3,1},{4,6},{5,7},{6,4},{7,5},{8,10},{9,11},{10,... | collective-permute-start | bytes 12296 | tf_op jit(solution)/shard_map/ppermute | solution.py:606
  10.7 27.9 %collective-permute-start = (f32[8,128]{1,0:T(8,128)S(1)}, f32[8,128]{1,0:T(8,128)S(1)}, u32[]{:S(2)}, u32[]{:S(2)}) collective-permute-start(f32[8,128]{1,0:T(8,128)S(1)} %get-tuple-element.27), channel_id=1, source_target_pairs={{0,1},{1,0},{2,3},{3,2},{4,5},{5,4},{6,7},{7,6},{8,9},{9,8},{10,11... | collective-permute-start | bytes 12296 | tf_op jit(solution)/shard_map/ppermute | solution.py:606
  10.7 34.0 %collective-permute-start.6 = (f32[8,8,128]{2,1,0:T(8,128)S(1)}, f32[8,8,128]{2,1,0:T(8,128)S(1)}, u32[]{:S(2)}, u32[]{:S(2)}) collective-permute-start(f32[8,8,128]{2,1,0:T(8,128)S(1)} %get-tuple-element.28), channel_id=1, source_target_pairs={{0,1},{1,0},{2,3},{3,2},{4,5},{5,4},{6,7},{7,6},{8,9},{9,8},{10,11... | collective-permute-start | bytes 98312 | tf_op jit(solution)/shard_map/ppermute | solution.py:618
  11.2 33.6 %collective-permute-start.7 = (f32[8,8,128]{2,1,0:T(8,128)S(1)}, f32[8,8,128]{2,1,0:T(8,128)S(1)}, u32[]{:S(2)}, u32[]{:S(2)}) collective-permute-start(f32[8,8,128]{2,1,0:T(8,128)S(1)} %get-tuple-element.29), channel_id=1, source_target_pairs={{1,2},{3,4},{5,6},{7,8},{9,10},{11,12},{13,14},{15,0},{2,1},{4,3},... | collective-permute-start | bytes 98312 | tf_op jit(solution)/shard_map/ppermute | solution.py:620
  38.6 6.2 %collective-permute-start.5 = (f32[4,8,128]{2,1,0:T(8,128)S(1)}, f32[4,8,128]{2,1,0:T(8,128)S(1)}, u32[]{:S(2)}, u32[]{:S(2)}) collective-permute-start(f32[4,8,128]{2,1,0:T(8,128)S(1)} %pad_maximum_fusion), channel_id=1, source_target_pairs={{0,12},{4,8},{8,4},{12,0},{1,13},{5,9},{9,5},{13,1},{2,14},{6,10},... | collective-permute-start | bytes 49160 | tf_op jit(solution)/shard_map/ppermute | solution.py:606
  38.6 6.1 %collective-permute-start.4 = (f32[4,8,128]{2,1,0:T(8,128)S(1)}, f32[4,8,128]{2,1,0:T(8,128)S(1)}, u32[]{:S(2)}, u32[]{:S(2)}) collective-permute-start(f32[4,8,128]{2,1,0:T(8,128)S(1)} %pad_maximum_fusion), channel_id=1, source_target_pairs={{0,8},{4,12},{8,0},{12,4},{1,9},{5,13},{9,1},{13,5},{2,10},{6,14},... | collective-permute-start | bytes 49160 | tf_op jit(solution)/shard_map/ppermute | solution.py:606
  38.7 6.0 %collective-permute-start.3 = (f32[4,8,128]{2,1,0:T(8,128)S(1)}, f32[4,8,128]{2,1,0:T(8,128)S(1)}, u32[]{:S(2)}, u32[]{:S(2)}) collective-permute-start(f32[4,8,128]{2,1,0:T(8,128)S(1)} %pad_maximum_fusion), channel_id=1, source_target_pairs={{0,4},{4,0},{8,12},{12,8},{1,5},{5,1},{9,13},{13,9},{2,6},{6,2},{1... | collective-permute-start | bytes 49160 | tf_op jit(solution)/shard_map/ppermute | solution.py:606
  56.2 12.5 %collective-permute-start.10 = (f32[8,128]{1,0:T(8,128)S(1)}, f32[8,128]{1,0:T(8,128)S(1)}, u32[]{:S(2)}, u32[]{:S(2)}) collective-permute-start(f32[8,128]{1,0:T(8,128)S(1)} %get-tuple-element.31), channel_id=1, source_target_pairs={{0,3},{1,2},{2,1},{3,0},{4,7},{5,6},{6,5},{7,4},{8,11},{9,10},{10,... | collective-permute-start | bytes 12296 | tf_op jit(solution)/shard_map/ppermute | solution.py:606
  56.3 12.4 %collective-permute-start.9 = (f32[8,128]{1,0:T(8,128)S(1)}, f32[8,128]{1,0:T(8,128)S(1)}, u32[]{:S(2)}, u32[]{:S(2)}) collective-permute-start(f32[8,128]{1,0:T(8,128)S(1)} %get-tuple-element.31), channel_id=1, source_target_pairs={{0,2},{1,3},{2,0},{3,1},{4,6},{5,7},{6,4},{7,5},{8,10},{9,11},{10,... | collective-permute-start | bytes 12296 | tf_op jit(solution)/shard_map/ppermute | solution.py:606
  56.4 12.4 %collective-permute-start.8 = (f32[8,128]{1,0:T(8,128)S(1)}, f32[8,128]{1,0:T(8,128)S(1)}, u32[]{:S(2)}, u32[]{:S(2)}) collective-permute-start(f32[8,128]{1,0:T(8,128)S(1)} %get-tuple-element.31), channel_id=1, source_target_pairs={{0,1},{1,0},{2,3},{3,2},{4,5},{5,4},{6,7},{7,6},{8,9},{9,8},{10,11... | collective-permute-start | bytes 12296 | tf_op jit(solution)/shard_map/ppermute | solution.py:606
  58.2 16.8 %collective-permute-start.14 = (f32[4,8,128]{2,1,0:T(8,128)S(1)}, f32[4,8,128]{2,1,0:T(8,128)S(1)}, u32[]{:S(2)}, u32[]{:S(2)}) collective-permute-start(f32[4,8,128]{2,1,0:T(8,128)S(1)} %get-tuple-element.32), channel_id=1, source_target_pairs={{0,1},{1,0},{2,3},{3,2},{4,5},{5,4},{6,7},{7,6},{8,9},{9,8},{10,11... | collective-permute-start | bytes 49160 | tf_op jit(solution)/shard_map/ppermute | solution.py:618
  58.2 16.8 %collective-permute-start.15 = (f32[4,8,128]{2,1,0:T(8,128)S(1)}, f32[4,8,128]{2,1,0:T(8,128)S(1)}, u32[]{:S(2)}, u32[]{:S(2)}) collective-permute-start(f32[4,8,128]{2,1,0:T(8,128)S(1)} %get-tuple-element.33), channel_id=1, source_target_pairs={{1,2},{3,4},{5,6},{7,8},{9,10},{11,12},{13,14},{15,0},{2,1},{4,3},... | collective-permute-start | bytes 49160 | tf_op jit(solution)/shard_map/ppermute | solution.py:620
  68.8 6.2 %collective-permute-start.13 = (f32[4,8,128]{2,1,0:T(8,128)S(1)}, f32[4,8,128]{2,1,0:T(8,128)S(1)}, u32[]{:S(2)}, u32[]{:S(2)}) collective-permute-start(f32[4,8,128]{2,1,0:T(8,128)S(1)} %pad_maximum_fusion.1), channel_id=1, source_target_pairs={{0,12},{4,8},{8,4},{12,0},{1,13},{5,9},{9,5},{13,1},{2,14},{6,10},... | collective-permute-start | bytes 49160 | tf_op jit(solution)/shard_map/ppermute | solution.py:606
  68.9 6.1 %collective-permute-start.12 = (f32[4,8,128]{2,1,0:T(8,128)S(1)}, f32[4,8,128]{2,1,0:T(8,128)S(1)}, u32[]{:S(2)}, u32[]{:S(2)}) collective-permute-start(f32[4,8,128]{2,1,0:T(8,128)S(1)} %pad_maximum_fusion.1), channel_id=1, source_target_pairs={{0,8},{4,12},{8,0},{12,4},{1,9},{5,13},{9,1},{13,5},{2,10},{6,14},... | collective-permute-start | bytes 49160 | tf_op jit(solution)/shard_map/ppermute | solution.py:606
  70.0 4.9 %collective-permute-start.11 = (f32[4,8,128]{2,1,0:T(8,128)S(1)}, f32[4,8,128]{2,1,0:T(8,128)S(1)}, u32[]{:S(2)}, u32[]{:S(2)}) collective-permute-start(f32[4,8,128]{2,1,0:T(8,128)S(1)} %pad_maximum_fusion.1), channel_id=1, source_target_pairs={{0,4},{4,0},{8,12},{12,8},{1,5},{5,1},{9,13},{13,9},{2,6},{6,2},{1... | collective-permute-start | bytes 49160 | tf_op jit(solution)/shard_map/ppermute | solution.py:606
  82.9 12.2 %collective-permute-start.18 = (f32[8,128]{1,0:T(8,128)S(1)}, f32[8,128]{1,0:T(8,128)S(1)}, u32[]{:S(2)}, u32[]{:S(2)}) collective-permute-start(f32[8,128]{1,0:T(8,128)S(1)} %get-tuple-element.35), channel_id=1, source_target_pairs={{0,3},{1,2},{2,1},{3,0},{4,7},{5,6},{6,5},{7,4},{8,11},{9,10},{10,... | collective-permute-start | bytes 12296 | tf_op jit(solution)/shard_map/ppermute | solution.py:606
  83.0 12.2 %collective-permute-start.17 = (f32[8,128]{1,0:T(8,128)S(1)}, f32[8,128]{1,0:T(8,128)S(1)}, u32[]{:S(2)}, u32[]{:S(2)}) collective-permute-start(f32[8,128]{1,0:T(8,128)S(1)} %get-tuple-element.35), channel_id=1, source_target_pairs={{0,2},{1,3},{2,0},{3,1},{4,6},{5,7},{6,4},{7,5},{8,10},{9,11},{10,... | collective-permute-start | bytes 12296 | tf_op jit(solution)/shard_map/ppermute | solution.py:606
  83.7 11.4 %collective-permute-start.16 = (f32[8,128]{1,0:T(8,128)S(1)}, f32[8,128]{1,0:T(8,128)S(1)}, u32[]{:S(2)}, u32[]{:S(2)}) collective-permute-start(f32[8,128]{1,0:T(8,128)S(1)} %get-tuple-element.35), channel_id=1, source_target_pairs={{0,1},{1,0},{2,3},{3,2},{4,5},{5,4},{6,7},{7,6},{8,9},{9,8},{10,11... | collective-permute-start | bytes 12296 | tf_op jit(solution)/shard_map/ppermute | solution.py:606
  84.8 16.6 %collective-permute-start.22 = (f32[4,8,128]{2,1,0:T(8,128)S(1)}, f32[4,8,128]{2,1,0:T(8,128)S(1)}, u32[]{:S(2)}, u32[]{:S(2)}) collective-permute-start(f32[4,8,128]{2,1,0:T(8,128)S(1)} %get-tuple-element.36), channel_id=1, source_target_pairs={{0,1},{1,0},{2,3},{3,2},{4,5},{5,4},{6,7},{7,6},{8,9},{9,8},{10,11... | collective-permute-start | bytes 49160 | tf_op jit(solution)/shard_map/ppermute | solution.py:618
  84.8 16.6 %collective-permute-start.23 = (f32[4,8,128]{2,1,0:T(8,128)S(1)}, f32[4,8,128]{2,1,0:T(8,128)S(1)}, u32[]{:S(2)}, u32[]{:S(2)}) collective-permute-start(f32[4,8,128]{2,1,0:T(8,128)S(1)} %get-tuple-element.37), channel_id=1, source_target_pairs={{1,2},{3,4},{5,6},{7,8},{9,10},{11,12},{13,14},{15,0},{2,1},{4,3},... | collective-permute-start | bytes 49160 | tf_op jit(solution)/shard_map/ppermute | solution.py:620
  95.2 6.2 %collective-permute-start.21 = (f32[4,8,128]{2,1,0:T(8,128)S(1)}, f32[4,8,128]{2,1,0:T(8,128)S(1)}, u32[]{:S(2)}, u32[]{:S(2)}) collective-permute-start(f32[4,8,128]{2,1,0:T(8,128)S(1)} %pad_maximum_fusion.2), channel_id=1, source_target_pairs={{0,12},{4,8},{8,4},{12,0},{1,13},{5,9},{9,5},{13,1},{2,14},{6,10},... | collective-permute-start | bytes 49160 | tf_op jit(solution)/shard_map/ppermute | solution.py:606
  96.1 5.3 %collective-permute-start.20 = (f32[4,8,128]{2,1,0:T(8,128)S(1)}, f32[4,8,128]{2,1,0:T(8,128)S(1)}, u32[]{:S(2)}, u32[]{:S(2)}) collective-permute-start(f32[4,8,128]{2,1,0:T(8,128)S(1)} %pad_maximum_fusion.2), channel_id=1, source_target_pairs={{0,8},{4,12},{8,0},{12,4},{1,9},{5,13},{9,1},{13,5},{2,10},{6,14},... | collective-permute-start | bytes 49160 | tf_op jit(solution)/shard_map/ppermute | solution.py:606
  112.5 7.3 %collective-permute-start.29 = (f32[4,8,128]{2,1,0:T(8,128)S(1)}, f32[4,8,128]{2,1,0:T(8,128)S(1)}, u32[]{:S(2)}, u32[]{:S(2)}) collective-permute-start(f32[4,8,128]{2,1,0:T(8,128)S(1)} %pad_maximum_fusion.3), channel_id=1, source_target_pairs={{0,12},{4,8},{8,4},{12,0},{1,13},{5,9},{9,5},{13,1},{2,14},{6,10},... | collective-permute-start | bytes 49160 | tf_op jit(solution)/shard_map/ppermute | solution.py:606
  (13 other events, 39.7 us)

commit v3 on v2

--- a/solution.py
+++ b/solution.py
@@ -29,16 +29,16 @@
 TABLE_LIMIT = 16 << 20
 
 
-def call(body, outs, args, smem=0, scratch=(), limit=None, cost=None, pinned=(), far=False, more=()):
+def call(body, outs, args, smem=0, scratch=(), limit=None, cost=None, pinned=(), far=False, more=(), lists=()):
     shapes = [
         pltpu.VMEM(shape, f32) if at in pinned else jax.ShapeDtypeStruct(shape, f32)
         for at, shape in enumerate(outs)
-    ]
+    ] + [jax.ShapeDtypeStruct((size,), jnp.int32) for size in lists]
     return list(pl.pallas_call(
         body,
         out_shape=shapes,
         in_specs=[SM] * smem + [pl.BlockSpec(memory_space=pltpu.HBM) if far else VM] * (len(args) - smem),
-        out_specs=[VM] * len(outs),
+        out_specs=[VM] * len(outs) + [SM] * len(lists),
         scratch_shapes=[pltpu.VMEM(shape, f32) for shape in scratch] + list(more),
         compiler_params=pltpu.CompilerParams(vmem_limit_bytes=limit or (12 << 20)),
         cost_estimate=cost,
@@ -82,6 +82,8 @@
 
 def columns(tiles, count, out):
     for t, tile in enumerate(tiles):
+        if tile.shape[0] < 8:
+            tile = jnp.concatenate([tile, jnp.zeros((8 - tile.shape[0], BLOCK), f32)], axis=0)
         turned = tile.T
         for k in range(count):
             out[t, k] = jnp.broadcast_to(turned[:, k : k + 1], (BLOCK, BLOCK))
@@ -150,15 +152,64 @@
     return out
 
 
-def edges(meta, put_core, put_ring, tiles, reach):
-    even = meta[0] % 2 == 0
-    high, low = tiles - reach, 0
-    put_core(jnp.where(even, high, low))
-    put_ring(jnp.where(even, low, high))
+def pack(weights, tiles, reach, get, payload, both):
+    payload[0] = weights
+    for k in range(reach):
+        low, high = get(k), get(tiles - reach + k)
+        if both:
+            rows = [low[0:3], high[0:3], jnp.zeros((2, BLOCK), f32)]
+            payload[1 + k] = jnp.concatenate(rows, axis=0)
+        else:
+            payload[1 + k] = low
+            payload[1 + reach + k] = high
+
+
+def relay_body(meta, *rest, plane, reach):
+    got, (out, held) = rest[:plane], rest[-2:]
+    count = held.shape[1]
+    for i in range(plane):
+        out[i] = got[i][0]
+        for k in range(count):
+            held[i, k] = got[i][1 + k]
+    own = meta[0] % plane
+    last = lax.bitwise_xor(own, plane - 1)
+    for k in range(count):
+        low, high = held[own, k], held[last, k]
+        if count == reach:
+            out[plane + k] = jnp.concatenate([low[0:3], high[3:6], low[6:8]], axis=0)
+        else:
+            out[plane + k] = low if k < reach else high
+
+
+def halo_tiles(meta, near, wide, held, plane, slabs, reach):
+    count = held.shape[1]
+    for i, ref in enumerate(near):
+        for k in range(count):
+            held[i, k] = ref[1 + k]
+    for i, ref in enumerate(wide):
+        for k in range(count):
+            held[plane + i, k] = ref[plane + k]
+    own_row, own_col = meta[0] // plane, meta[0] % plane
+    rows = slabs // plane
+    below = jnp.where(own_row == 0, rows - 1, own_row - 1)
+    above = jnp.where(own_row == rows - 1, 0, own_row + 1)
+    low = jnp.where(
+        own_col > 0,
+        lax.bitwise_xor(own_col, jnp.maximum(own_col - 1, 0)),
+        plane + lax.bitwise_xor(own_row, below),
+    )
+    high = jnp.where(
+        own_col < plane - 1,
+        lax.bitwise_xor(own_col, jnp.minimum(own_col + 1, plane - 1)),
+        plane + lax.bitwise_xor(own_row, above),
+    )
+    if count == reach:
+        return [held[low, k][3:6] for k in range(reach)] + [held[high, k][0:3] for k in range(reach)]
+    return [held[low, reach + k] for k in range(reach)] + [held[high, k] for k in range(reach)]
 
 
 def first_body(
-    meta, pos_in, alpha_in, field_in, gid_in, picks_in, stat, x0, phi, weights, core, ring,
+    meta, pos_in, alpha_in, field_in, gid_in, picks_in, stat, x0, phi, payload,
     pos, alpha, field, gid, picks, sems, *, coeff, box_height, tiles, reach
 ):
     pairs = [(pos_in, pos), (alpha_in, alpha), (field_in, field), (gid_in, gid), (picks_in, picks)]
@@ -218,17 +269,12 @@
         stat[t] = scaled[:, t * BLOCK : (t + 1) * BLOCK]
         x0[t] = vec[:, t * BLOCK : (t + 1) * BLOCK]
     rows = project(phi, x0, tiles)
-    weights[...] = jnp.concatenate(rows + [jnp.zeros((2, BLOCK), f32)], axis=0)
-
-    def put(ref):
-        def at(begin):
-            for k in range(reach):
-                ref[k] = stat[begin + k]
-                ref[reach + k] = x0[begin + k]
-
-        return at
-
-    edges(meta, put(core), put(ring), tiles, reach)
+    weights = jnp.concatenate(rows + [jnp.zeros((2, BLOCK), f32)], axis=0)
+
+    def get(k):
+        return jnp.concatenate([stat[k][0:5], x0[k][0:3]], axis=0)
+
+    pack(weights, tiles, reach, get, payload, False)
 
 
 def own_slot(b, begin, tiles, reach):
@@ -240,70 +286,104 @@
     return sum(min(reach + 1, tiles - b) for b in range(begin, end))
 
 
-def tensors_body(mask, stat, out, col, *, begin, end, tiles, reach, length_z):
-    columns([stat[t] for t in range(begin, end)], 5, col)
-
-    def visit(b, unused):
-        slot = own_slot(b, begin, tiles, reach)
-        for o in range(reach + 1):
-
-            @pl.when((b + o < tiles) & (mask[b, reach + o] != 0) if o else b >= 0)
-            def _():
-                other = stat[b + o]
-                rows = [other[k : k + 1, :] for k in range(5)]
-
-                def store(k, at, value):
-                    out[slot + o, k, at, :] = value
-
-                build_pair(lambda k, at: col[b - begin, k, at, :], rows, store, length_z)
-
+def walk(codes, begin, end, visit):
+    def step(at, code):
+        later = codes[at + 1]
+        visit(code)
+        return later
+
+    lax.fori_loop(begin, end, step, codes[begin])
+
+
+def unpack(code):
+    return code & 255, (code >> 8) & 255, code >> 16
+
+
+def tensors_body(mask, stat, out, own_list, halo_list, col, *, half, tiles, reach, length_z):
+    last = own_list.shape[0] - 2
+    n = jnp.int32(0)
+    for b in range(tiles):
+        if b == half:
+            own_list[last] = n
+        k = max(b - (tiles - reach), 0)
+        slot = b * (reach + 1) - k * (k + 1) // 2
+        for o in range(1, min(reach + 1, tiles - b)):
+            own_list[n] = jnp.int32(slot + o + (b << 8) + ((b + o) << 16))
+            n = n + mask[b, reach + o]
+    own_list[last + 1] = n
+    m = jnp.int32(0)
+    for index, (h, c, at) in enumerate(halo_pairs(tiles, reach)):
+        halo_list[m] = jnp.int32(index + (h << 8) + (c << 16))
+        m = m + mask[c, at]
+    halo_list[halo_list.shape[0] - 1] = m
+    columns([stat[t] for t in range(tiles)], 5, col)
+
+    def visit(at, unused):
+        slot, b, other = unpack(own_list[jnp.maximum(at - tiles, 0)])
+        alone = at < tiles
+        slot = jnp.where(alone, own_slot(at, 0, tiles, reach), slot)
+        b = jnp.where(alone, at, b)
+        tile = stat[jnp.where(alone, at, other)]
+        rows = [tile[k : k + 1, :] for k in range(5)]
+
+        def store(k, at, value):
+            out[slot, k, at, :] = value
+
+        build_pair(lambda k, at: col[b, k, at, :], rows, store, length_z)
         return unused
 
-    lax.fori_loop(begin, end, visit, 0)
-
-
-def own_body(mask, v, *rest, ranges, tiles, reach):
-    tabs = rest[: len(ranges)]
-    out, acc_i, acc_j, col = rest[len(ranges) :]
-    columns([v[t] for t in range(tiles)], 3, col)
-    for t in range(tiles):
+    lax.fori_loop(0, tiles + n, visit, 0)
+
+
+def own_body(codes, v, tab, *rest, begin, end, tiles, reach):
+    out, acc_i, acc_j, col, wide = rest[-5:]
+    top = min(end + reach, tiles)
+    columns([v[t] for t in range(begin, end)], 3, col)
+    for t in range(top - begin):
         for c in range(3):
             acc_j[t, c] = jnp.zeros((SUB, BLOCK), f32)
-    for (begin, end), tab in zip(ranges, tabs):
-
-        def visit(b, unused):
-            slot = own_slot(b, begin, tiles, reach)
-            for o in range(reach + 1):
-
-                @pl.when((b + o < tiles) & (mask[b, reach + o] != 0) if o else b >= 0)
-                def _():
-                    other = v[b + o]
-                    wide = [spread(other, c) for c in range(3)]
-                    acc = [acc_j[b + o, c] for c in range(3)] if o else None
-                    for step in range(BLOCK // SUB):
-                        at = slice(step * SUB, (step + 1) * SUB)
-                        t = [tab[slot + o, k, at, :] for k in range(4)]
-                        new = apply_tensor(t, wide)
-                        for c in range(3):
-                            if o == 0:
-                                acc_i[b, c, at, :] = new[c]
-                            else:
-                                acc_i[b, c, at, :] += new[c]
-                        if o:
-                            new = apply_tensor(t, [col[b, c, at, :] for c in range(3)])
-                            acc = [a + n for a, n in zip(acc, new)]
-                    if o:
-                        for c in range(3):
-                            acc_j[b + o, c] = acc[c]
-
-            return unused
-
-        lax.fori_loop(begin, end, visit, 0)
-    for t in range(tiles):
+            wide[t, c] = spread(v[begin + t], c)
+
+    def pair(b, other, slot, both):
+        at_b, at_o = b - begin, other - begin
+        vec = [wide[at_o, c] for c in range(3)]
+        acc = [acc_j[at_o, c] for c in range(3)] if both else None
+        for step in range(BLOCK // SUB):
+            at = slice(step * SUB, (step + 1) * SUB)
+            t = [tab[slot, k, at, :] for k in range(4)]
+            new = apply_tensor(t, vec)
+            for c in range(3):
+                if both:
+                    acc_i[at_b, c, at, :] += new[c]
+                else:
+                    acc_i[at_b, c, at, :] = new[c]
+            if both:
+                new = apply_tensor(t, [col[at_b, c, at, :] for c in range(3)])
+                acc = [a + n for a, n in zip(acc, new)]
+        if both:
+            for c in range(3):
+                acc_j[at_o, c] = acc[c]
+
+    def alone(b, unused):
+        pair(b, b, own_slot(b, 0, tiles, reach), False)
+        return unused
+
+    lax.fori_loop(begin, end, alone, 0)
+    last = codes.shape[0] - 2
+
+    def visit(code):
+        slot, b, other = unpack(code)
+        pair(b, other, slot, True)
+
+    walk(codes, codes[last] if begin else 0, codes[last + 1] if begin else codes[last], visit)
+    for t in range(top - begin):
         rows = []
         for c in range(3):
-            parts = [acc_i[t, c, k * SUB : (k + 1) * SUB, :] for k in range(BLOCK // SUB)]
-            rows.append(row_sum(acc_j[t, c] + lane_sums(parts)))
+            total = acc_j[t, c]
+            if t < end - begin:
+                parts = [acc_i[t, c, k * SUB : (k + 1) * SUB, :] for k in range(BLOCK // SUB)]
+                total = total + lane_sums(parts)
+            rows.append(row_sum(total))
         out[t] = jnp.concatenate(rows + [jnp.zeros((5, BLOCK), f32)], axis=0)
 
 
@@ -318,29 +398,25 @@
     return pairs
 
 
-def halo_tiles(meta, core, ring, begin, reach):
-    even = meta[0] % 2 == 0
-    low, high = [], []
-    for k in range(reach):
-        a, b = core[begin + k], ring[begin + k]
-        low.append(jnp.where(even, b, a))
-        high.append(jnp.where(even, a, b))
-    return low + high
-
-
-def halo_tensors_body(meta, mask, stat, core, ring, out, col, *, tiles, reach, length_z):
-    columns(halo_tiles(meta, core, ring, 0, reach), 5, col)
-    for index, (h, c, m) in enumerate(halo_pairs(tiles, reach)):
-
-        @pl.when(mask[c, m] != 0)
-        def _():
-            own = stat[c]
-            rows = [own[k : k + 1, :] for k in range(5)]
-
-            def store(k, at, value):
-                out[index, k, at, :] = value
-
-            build_pair(lambda k, at: col[h, k, at, :], rows, store, length_z)
+def halo_tensors_body(meta, codes, stat, *rest, tiles, plane, slabs, reach, length_z):
+    rows = slabs // plane
+    near, wide = rest[:plane], rest[plane : plane + rows]
+    out, first, col, held = rest[plane + rows :]
+    halo = halo_tiles(meta, near, wide, held, plane, slabs, reach)
+    for k, tile in enumerate(halo):
+        first[k] = tile
+    columns(halo, 5, col)
+    def visit(code):
+        index, h, c = unpack(code)
+        own = stat[c]
+        own_rows = [own[k : k + 1, :] for k in range(5)]
+
+        def store(k, at, value):
+            out[index, k, at, :] = value
+
+        build_pair(lambda k, at: col[h, k, at, :], own_rows, store, length_z)
+
+    walk(codes, 0, codes[codes.shape[0] - 1], visit)
 
 
 def far_geometry(nodes, geo, box_height):
@@ -453,47 +529,60 @@
             )
 
 
-def field_body(meta, mask, nodes, stat, v, near, phi, gathered, core, ring, halo_tab, *rest,
-               mode, tiles, reach, plane, slabs, box_height, length_z, surface, kept, offset):
+def field_body(meta, codes, nodes, stat, v, phi, halo_tab, *rest,
+               mode, tiles, reach, plane, slabs, box_height, length_z, surface, kept, half):
     rest = list(rest)
-    table = rest.pop(0) if kept else None
-    extra = [rest.pop(0) for _ in range((0, 0, 4)[mode])]
-    outs = [rest.pop(0) for _ in range((5, 6, 5)[mode])]
-    acc, col, wide, fcol, geo = rest
+
+    def take(count):
+        return [rest.pop(0) for _ in range(count)]
+
+    rows = slabs // plane
+    parts = take(2)
+    near = take(plane) if mode else []
+    bundles = take(rows)
+    first = None if mode else take(1)[0]
+    table = take(1)[0] if kept else None
+    extra = take((0, 0, 4)[mode])
+    outs = take((3, 4, 5)[mode])
+    acc, col, wide, fcol, geo, held = rest
     boxes = slabs * BOXES_DEV
     member = meta[0]
     own_row, own_col = member // plane, member % plane
 
-    def expand(k, total):
-        other = lax.rem(member + k, slabs)
-        slot = lax.bitwise_xor(other // plane, own_row) * plane + lax.bitwise_xor(other % plane, own_col)
-        tile = gathered[slot]
-        for box in range(BOXES_DEV):
-            for c in range(3):
-                wide[k * BOXES_DEV + box, c] = spread(tile, box * 3 + c)
-        return total + tile
-
-    total = lax.fori_loop(0, slabs, expand, jnp.zeros((SUB, BLOCK), f32))
+    total = jnp.zeros((SUB, BLOCK), f32)
+    for i in range(rows):
+        for j in range(plane):
+            tile = bundles[i][j]
+            total = total + tile
+            other = lax.bitwise_xor(own_row, i) * plane + lax.bitwise_xor(own_col, j) - member
+            k = jnp.where(other < 0, other + slabs, other) * BOXES_DEV
+            for box in range(BOXES_DEV):
+                for c in range(3):
+                    wide[k + box, c] = spread(tile, box * 3 + c)
     sums = jnp.sum(total, axis=1, keepdims=True)
     moment = [surface * (sums[c : c + 1] + sums[3 + c : 4 + c]) for c in range(3)]
 
-    columns(halo_tiles(meta, core, ring, offset, reach), 3, col)
+    if mode:
+        halo = halo_tiles(meta, near, bundles, held, plane, slabs, reach)
+    else:
+        halo = [first[k][5:8] for k in range(2 * reach)]
+    columns(halo, 3, col)
     for t in range(tiles):
         for c in range(3):
             acc[t, c] = jnp.zeros((SUB, BLOCK), f32)
-    for index, (h, c, m) in enumerate(halo_pairs(tiles, reach)):
-
-        @pl.when(mask[c, m] != 0)
-        def _():
-            sofar = [acc[c, k] for k in range(3)]
-            for step in range(BLOCK // SUB):
-                at = slice(step * SUB, (step + 1) * SUB)
-                new = apply_tensor(
-                    [halo_tab[index, k, at, :] for k in range(4)], [col[h, k, at, :] for k in range(3)]
-                )
-                sofar = [a + n for a, n in zip(sofar, new)]
-            for k in range(3):
-                acc[c, k] = sofar[k]
+    def visit(code):
+        index, h, c = unpack(code)
+        sofar = [acc[c, k] for k in range(3)]
+        for step in range(BLOCK // SUB):
+            at = slice(step * SUB, (step + 1) * SUB)
+            new = apply_tensor(
+                [halo_tab[index, k, at, :] for k in range(4)], [col[h, k, at, :] for k in range(3)]
+            )
+            sofar = [a + n for a, n in zip(sofar, new)]
+        for k in range(3):
+            acc[c, k] = sofar[k]
+
+    walk(codes, 0, codes[codes.shape[0] - 1], visit)
 
     if not kept:
         far_geometry(nodes, geo, box_height)
@@ -510,43 +599,39 @@
             value = phi[t, at, :]
             sofar = [a + value * fcol[box, c, at, :] for c, a in enumerate(sofar)]
         rows = [row_sum(a) - m for a, m in zip(sofar, moment)]
-        fields.append(near[t] + jnp.concatenate(rows + [zero], axis=0))
+        value = jnp.concatenate(rows + [zero], axis=0)
+        if t < parts[0].shape[0]:
+            value = value + parts[0][t]
+        if t >= half:
+            value = value + parts[1][t - half]
+        fields.append(value)
 
     def alpha(t):
         return spread(stat[t], 5)
 
     none = jnp.zeros((1, BLOCK), f32)
 
-    def send(u, weights, core_out, ring_out, scalar):
-        rows = project(phi, u, tiles)
-        weights[...] = jnp.concatenate(rows + [scalar, none], axis=0)
-
-        def at(ref):
-            def store(begin):
-                for k in range(reach):
-                    ref[k] = u[begin + k]
-
-            return store
-
-        edges(meta, at(core_out), at(ring_out), tiles, reach)
-
-    def fold(parts):
-        out = parts[0]
-        for x in parts[1:]:
+    def send(u, payload, scalar):
+        weights = jnp.concatenate(project(phi, u, tiles) + [scalar, none], axis=0)
+        pack(weights, tiles, reach, lambda k: u[k], payload, True)
+
+    def fold(terms):
+        out = terms[0]
+        for x in terms[1:]:
             out = out + x
         return row_sum(out)
 
     if mode == 0:
-        res, u, weights, core_out, ring_out = outs
+        res, u, payload = outs
         dots = []
         for t in range(tiles):
             scaled = alpha(t) * fields[t]
             res[t] = fields[t]
             u[t] = scaled
             dots.append(scaled * fields[t])
-        send(u, weights, core_out, ring_out, fold(dots))
+        send(u, payload, fold(dots))
     elif mode == 1:
-        image, u, weights, core_out, ring_out, norm = outs
+        image, u, payload, norm = outs
         dots = []
         for t in range(tiles):
             w = v[t] / alpha(t) - fields[t]
@@ -554,7 +639,7 @@
             u[t] = alpha(t) * w
             dots.append(v[t] * w)
         norm[...] = jnp.broadcast_to(sums[6:7], (SUB, BLOCK))
-        send(u, weights, core_out, ring_out, fold(dots))
+        send(u, payload, fold(dots))
     else:
         first, res, w0, norm = extra
         x1, r1, z1, q1, scal = outs
@@ -578,10 +663,11 @@
         )
 
 
-def last_body(gathered, scal, stat, res, w0, x1, r1, z1, q1, dip, out, *, tiles):
-    total = gathered[0]
-    for k in range(1, gathered.shape[0]):
-        total = total + gathered[k]
+def last_body(scal, stat, res, w0, x1, r1, z1, q1, *rest, tiles):
+    gathered, (dip, out) = rest[:-2], rest[-2:]
+    total = gathered[0][...]
+    for ref in gathered[1:]:
+        total = total + ref[...]
     sums = jnp.sum(total, axis=1, keepdims=True)
 
     def value(x):
@@ -605,20 +691,6 @@
     for s in range(1, count):
         got.append(lax.ppermute(x, axes, [(i, i ^ s) for i in range(count)]))
     return got
-
-
-def gather(x, plane, rows):
-    near = jnp.stack(swap(x, ("oct", "sub"), plane))
-    return jnp.concatenate(swap(near, "blk", rows), axis=0)
-
-
-def halo(core, ring):
-    count = lax.axis_size(RING)
-    size = lax.axis_size("sub")
-    got_core = lax.ppermute(core, "sub", [(i, i ^ 1) for i in range(size)])
-    pairs = [(i, (i + 1) % count) for i in range(1, count, 2)]
-    got_ring = lax.ppermute(ring, RING, pairs + [(b, a) for a, b in pairs])
-    return got_core, got_ring
 
 
 def on_device(positions, polarizability, permanent_field, group_id, pair_mask):
@@ -638,13 +710,17 @@
     meta = jnp.reshape(member, (1,)).astype(jnp.int32)
     mask = pair_mask
     tile_shape = (tiles, 8, BLOCK)
-    edge = (reach, 8, BLOCK)
     kept = (boxes - 1) * 4 * BLOCK * BLOCK * 4 <= TABLE_LIMIT
 
-    stat, x0, phi, weights, core, ring = call(
+    half = tiles // 2
+
+    def far_memory(x):
+        return pltpu.with_memory_space_constraint(x, pltpu.HBM)
+
+    stat, x0, phi, payload = call(
         functools.partial(first_body, coeff=coeff, box_height=box_height, tiles=tiles, reach=reach),
-        [tile_shape, tile_shape, (tiles, BLOCK, BLOCK), (8, BLOCK), (2 * reach, 8, BLOCK), (2 * reach, 8, BLOCK)],
-        [meta, positions, polarizability[None], permanent_field, group_id[None], jnp.asarray(picks)],
+        [tile_shape, tile_shape, (tiles, BLOCK, BLOCK), (1 + 2 * reach, 8, BLOCK)],
+        [meta] + [far_memory(x) for x in (positions, polarizability[None], permanent_field, group_id[None], jnp.asarray(picks))],
         smem=1,
         limit=16 << 20,
         far=True,
@@ -657,22 +733,17 @@
             pltpu.SemaphoreType.DMA((5,)),
         ],
     )
-    got_core, got_ring = halo(core, ring)
-    gathered = gather(weights, plane, rows)
-
-    ranges = [(0, tiles // 2), (tiles // 2, tiles)]
-    tabs = []
-    for begin, end in ranges:
-        count = own_slots(begin, end, tiles, reach)
-        tabs += call(
-            functools.partial(tensors_body, begin=begin, end=end, tiles=tiles, reach=reach, length_z=length_z),
-            [(count, 4, BLOCK, BLOCK)],
-            [mask, stat],
-            smem=1,
-            scratch=[(end - begin, 5, BLOCK, BLOCK)],
-            cost=pl.CostEstimate(flops=count * BLOCK * BLOCK * 70, bytes_accessed=1 << 20, transcendentals=count * BLOCK * BLOCK * 2),
-            pinned=(0,),
-        )
+    count = own_slots(0, tiles, tiles, reach)
+    tab, own_list, halo_list = call(
+        functools.partial(tensors_body, half=half, tiles=tiles, reach=reach, length_z=length_z),
+        [(count, 4, BLOCK, BLOCK)],
+        [mask, stat],
+        smem=1,
+        scratch=[(tiles, 5, BLOCK, BLOCK)],
+        cost=pl.CostEstimate(flops=count * BLOCK * BLOCK * 70, bytes_accessed=1 << 20, transcendentals=count * BLOCK * BLOCK * 2),
+        pinned=(0,),
+        lists=(count - tiles + 2, len(halo_pairs(tiles, reach)) + 1),
+    )
     table = []
     if kept:
         table = call(
@@ -683,40 +754,51 @@
             cost=pl.CostEstimate(flops=boxes * BLOCK * BLOCK * 28, bytes_accessed=1 << 20, transcendentals=boxes * BLOCK * BLOCK),
             pinned=(0,),
         )
-    (halo_tab,) = call(
-        functools.partial(halo_tensors_body, tiles=tiles, reach=reach, length_z=length_z),
-        [(len(halo_pairs(tiles, reach)), 4, BLOCK, BLOCK)],
-        [meta, mask, stat, got_core, got_ring],
-        smem=2,
-        scratch=[(2 * reach, 5, BLOCK, BLOCK)],
-        pinned=(0,),
-    )
-
-    def own_field(v):
+
+    def own_field(v, begin, end, after):
+        top = min(end + reach, tiles) - begin
         return call(
-            functools.partial(own_body, ranges=ranges, tiles=tiles, reach=reach),
-            [tile_shape],
-            [mask, v] + tabs,
+            functools.partial(own_body, begin=begin, end=end, tiles=tiles, reach=reach),
+            [(top, 8, BLOCK)],
+            [own_list, v, tab] + after,
             smem=1,
-            scratch=[(tiles, 3, BLOCK, BLOCK), (tiles, 3, SUB, BLOCK), (tiles, 3, BLOCK, BLOCK)],
-            cost=pl.CostEstimate(flops=72 * 2 * BLOCK * BLOCK * 18, bytes_accessed=1 << 20, transcendentals=0),
+            scratch=[
+                (end - begin, 3, BLOCK, BLOCK),
+                (top, 3, SUB, BLOCK),
+                (end - begin, 3, BLOCK, BLOCK),
+                (top, 3, SUB, BLOCK),
+            ],
+            cost=pl.CostEstimate(flops=72 * BLOCK * BLOCK * 18, bytes_accessed=1 << 20, transcendentals=0),
         )[0]
 
-    def field(mode, v, gathered, got_core, got_ring, extra):
-        near = own_field(v)
-        offset = reach if mode == 0 else 0
+    def exchange(payload, v):
+        near = swap(payload, ("oct", "sub"), plane)
+        first = own_field(v, 0, half, [])
+        bundle = call(
+            functools.partial(relay_body, plane=plane, reach=reach),
+            [(plane + payload.shape[0] - 1, 8, BLOCK)],
+            [meta] + near + [first],
+            smem=1,
+            scratch=[(plane, payload.shape[0] - 1, 8, BLOCK)],
+        )[0]
+        bundles = swap(bundle, "blk", rows)
+        second = own_field(v, half, tiles, [bundle])
+        return [first, second], near, bundles
+
+    def field(mode, v, parts, near, bundles, extra):
         outs = [
-            [tile_shape, tile_shape, (8, BLOCK), edge, edge],
-            [tile_shape, tile_shape, (8, BLOCK), edge, edge, (SUB, BLOCK)],
+            [tile_shape, tile_shape, (1 + reach, 8, BLOCK)],
+            [tile_shape, tile_shape, (1 + reach, 8, BLOCK), (SUB, BLOCK)],
             [tile_shape] * 4 + [(8, BLOCK)],
         ][mode]
         return call(
             functools.partial(
                 field_body, mode=mode, tiles=tiles, reach=reach, plane=plane, slabs=slabs, box_height=box_height,
-                length_z=length_z, surface=surface, kept=kept, offset=offset,
+                length_z=length_z, surface=surface, kept=kept, half=half,
             ),
             outs,
-            [meta, mask, nodes, stat, v, near, phi, gathered, got_core, got_ring, halo_tab] + table + extra,
+            [meta, halo_list, nodes, stat, v, phi, halo_tab] + parts + (near if mode else []) + bundles
+            + ([] if mode else [edge]) + table + extra,
             smem=2,
             scratch=[
                 (tiles, 3, SUB, BLOCK),
@@ -724,21 +806,32 @@
                 (boxes, 3, SUB, BLOCK),
                 (BOXES_DEV, 3, BLOCK, BLOCK),
                 (8, BLOCK, BLOCK) if not kept else (1, 8, BLOCK),
+                (plane + rows, reach, 8, BLOCK),
             ],
         )
 
-    r0, u0, weights, core, ring = field(0, x0, gathered, got_core, got_ring, [])
-    got_core, got_ring = halo(core, ring)
-    gathered = gather(weights, plane, rows)
-    w0, u1, weights, core, ring, norm = field(1, u0, gathered, got_core, got_ring, [])
-    got_core, got_ring = halo(core, ring)
-    gathered = gather(weights, plane, rows)
-    x1, r1, z1, q1, scal = field(2, u1, gathered, got_core, got_ring, [x0, r0, w0, norm])
-    gathered = gather(scal, plane, rows)
+    parts, near, bundles = exchange(payload, x0)
+    halo_tab, edge = call(
+        functools.partial(
+            halo_tensors_body, tiles=tiles, plane=plane, slabs=slabs, reach=reach, length_z=length_z
+        ),
+        [(len(halo_pairs(tiles, reach)), 4, BLOCK, BLOCK), (2 * reach, 8, BLOCK)],
+        [meta, halo_list, stat] + near + bundles,
+        smem=2,
+        scratch=[(2 * reach, 5, BLOCK, BLOCK), (plane + rows, 2 * reach, 8, BLOCK)],
+        pinned=(0,),
+    )
+    r0, u0, payload = field(0, x0, parts, near, bundles, [])
+    parts, near, bundles = exchange(payload, u0)
+    w0, u1, payload, norm = field(1, u0, parts, near, bundles, [])
+    parts, near, bundles = exchange(payload, u1)
+    x1, r1, z1, q1, scal = field(2, u1, parts, near, bundles, [x0, r0, w0, norm])
+    sums = swap(scal, ("oct", "sub"), plane)
+    sums = swap(functools.reduce(jnp.add, sums), "blk", rows)
     return call(
         functools.partial(last_body, tiles=tiles),
         [(3, atoms), (3, atoms)],
-        [gathered, scal, stat, r0, w0, x1, r1, z1, q1],
+        [scal, stat, r0, w0, x1, r1, z1, q1] + sums,
     )
 
 

time: 121 us -> 105 us (0.87)
  starting transfers between devices: 36.3 us -> 27.2 us
  waiting for transfers between devices: 9.93 us -> 5.75 us
  local copies, waits for them, and re-layouts: 4.59 us -> 0.7 us
    ppermute x6 -> x0, starting transfers between devices: 9.68 us -> none  [the longest x3 9.2 us: halo(): got_ring = lax.ppermute(ring, RING, pairs + [(b, a) for a, b in pairs])]
    ppermute x24, waiting for transfers between devices: 9.91 us -> 5.75 us  [swap(): got.append(lax.ppermute(x, axes, [(i, i ^ s) for i in range(count)]))]
    unnamed x38 -> x4, local copies, waits for them, and re-layouts: 4.57 us -> 0.7 us
    pallas_call x12 -> x17, Pallas kernels: 68.8 us -> 70 us  [call(): pl.pallas_call(body, out_shape=shapes, in_specs=[SM] * smem + [pl.BlockSp...]
  transfers between devices with their start and end apart: 30 -> 24, of which waited for: 6 -> 5; matrix products, arithmetic and copies ran while one was open for 0% -> 0% of each run, Pallas kernels for 32% -> 37%
where the time goes in v3:
time: 105 us
  Pallas kernels  70 us (67%)
  starting transfers between devices  27.2 us (26%)
  waiting for transfers between devices  5.75 us (5%)
    pallas_call x17, Pallas kernels, call(): pl.pallas_call(body, out_shape=shapes, in_specs=[SM] * smem + [pl.BlockSp...  70 us
    ppermute x24, starting transfers between devices, swap(): got.append(lax.ppermute(x, axes, [(i, i ^ s) for i in range(count)]))  27.2 us
    ppermute x24, waiting for transfers between devices, swap(): got.append(lax.ppermute(x, axes, [(i, i ^ s) for i in range(count)]))  5.75 us
  transfers between devices with their start and end apart: 24, of which 5 were waited for; matrix products, arithmetic and copies ran while one was open for 0% of the time, Pallas kernels for 37%

profile of v3, /device:TPU:0, one launch (start us, length us, event | category | flops | bytes accessed | tf_op | source)
XLA Modules:
  0.0 104.5 jit_solution(18039999492079472327)
XLA Ops:
  0.6 3.8 %shard_map.86 = (f32[16,8,128]{2,1,0:T(8,128)S(1)}, f32[16,8,128]{2,1,0:T(8,128)S(1)}, f32[16,128,128]{2,1,0:T(8,128)S(1)}, f32[9,8,128]{2,1,0:T(8,128)S(1)}) custom-call(s32[1]{0:T(128)} %bitcast.meta, f32[3,2048]{1,0:T(4,128)} %pos_in.1, f32[1,2048]{1,0:T(1,128)} %bitcast.3, f32[3,2048]{1,0:T(4,128)} %field_in.1, s32[1,2048]{1,0:T(1,128)} %bitcast.4, ...), custom_call_target="tpu_custom_call" | custom-call | tf_op jit(solution)/shard_map/pallas_call | solution.py:37
  4.4 2.4 %collective-permute-start.2 = (f32[9,8,128]{2,1,0:T(8,128)S(1)}, f32[9,8,128]{2,1,0:T(8,128)S(1)}, u32[]{:S(2)}, u32[]{:S(2)}) collective-permute-start(f32[9,8,128]{2,1,0:T(8,128)S(1)} %get-tuple-element.27.rest_0_), channel_id=1, source_target_pairs={{0,3},{1,2},{2,1},{3,0},{4,7},{5,6},{6,5},{7,4},{8,11},{9,10},{10,... | collective-permute-start | bytes 110600 | tf_op jit(solution)/shard_map/ppermute | solution.py:692
  8.2 11.5 %shard_map.87 = (f32[70,4,128,128]{3,2,1,0:T(8,128)S(1)}, s32[56]{0:T(128)S(1)}, s32[21]{0:T(128)S(1)}) custom-call(s32[16,9]{1,0:T(8,128)S(1)} %copy-done.1, f32[16,8,128]{2,1,0:T(8,128)S(1)} %get-tuple-element.23.stat), custom_call_target="tpu_custom_call" | custom-call | flops 80281600 | bytes 1048576 | tf_op jit(solution)/shard_map/pallas_call | solution.py:37
  19.8 4.3 %shard_map.88.rest_4_.rest_0_ = f32[12,8,128]{2,1,0:T(8,128)S(1)} custom-call(s32[56]{0:T(128)S(1)} %get-tuple-element.28.codes, f32[16,8,128]{2,1,0:T(8,128)S(1)} %get-tuple-element.25.v.rest_11_, f32[70,4,128,128]{3,2,1,0:T(8,128)S(1)} %get-tuple-element.29.tab), custom_call_target="tpu_custom_call" | custom-call | flops 21233664 | bytes 1048576 | tf_op jit(solution)/shard_map/pallas_call | solution.py:37
  24.2 4.2 %collective-permute-start.5 = (f32[12,8,128]{2,1,0:T(8,128)S(1)}, f32[12,8,128]{2,1,0:T(8,128)S(1)}, u32[]{:S(2)}, u32[]{:S(2)}) collective-permute-start(f32[12,8,128]{2,1,0:T(8,128)S(1)} %shard_map.89.rest_4_.rest_0_.rest_2_), channel_id=1, source_target_pairs={{0,12},{4,8},{8,4},{12,0},{1,13},{5,9},{9,5},{13,1},{2,14},{6,10},... | collective-permute-start | bytes 147464 | tf_op jit(solution)/shard_map/ppermute | solution.py:692
  29.2 2.1 %shard_map.92.rest_7_.rest_10_ = f32[31,4,128,128]{3,2,1,0:T(8,128)S(1)} custom-call(f32[8,128]{1,0:T(8,128)S(1)} %copy-done), custom_call_target="tpu_custom_call" | custom-call | flops 14680064 | bytes 1048576 | tf_op jit(solution)/shard_map/pallas_call | solution.py:37
  31.2 3.9 %shard_map.91.rest_1_ = f32[8,8,128]{2,1,0:T(8,128)S(1)} custom-call(s32[56]{0:T(128)S(1)} %get-tuple-element.28.codes, f32[16,8,128]{2,1,0:T(8,128)S(1)} %get-tuple-element.25.v.rest_11_, f32[70,4,128,128]{3,2,1,0:T(8,128)S(1)} %get-tuple-element.29.tab, f32[12,8,128]{2,1,0:T(8,128)S(1)} %shard_map.89.rest_4_.rest_0_.rest_2_), custom_call_target="tpu_custom_call" | custom-call | flops 21233664 | bytes 1048576 | tf_op jit(solution)/shard_map/pallas_call | solution.py:37
  35.2 3.8 %shard_map.90 = (f32[20,4,128,128]{3,2,1,0:T(8,128)S(1)}, f32[8,8,128]{2,1,0:T(8,128)S(1)}) custom-call(s32[1]{0:T(128)} %bitcast.meta, s32[21]{0:T(128)S(1)} %get-tuple-element.24.codes, f32[16,8,128]{2,1,0:T(8,128)S(1)} %get-tuple-element.23.stat, f32[9,8,128]{2,1,0:T(8,128)S(1)} %get-tuple-element.27.rest_0_, ...), custom_call_target="tpu_custom_call" | custom-call | tf_op jit(solution)/shard_map/pallas_call | solution.py:37
  39.0 7.8 %shard_map.93 = (f32[16,8,128]{2,1,0:T(8,128)S(1)}, f32[16,8,128]{2,1,0:T(8,128)S(1)}, f32[5,8,128]{2,1,0:T(8,128)S(1)}) custom-call(s32[1]{0:T(128)} %bitcast.meta, s32[21]{0:T(128)S(1)} %get-tuple-element.24.codes, f32[8,128]{1,0:T(8,128)S(1)} %copy-done, f32[16,8,128]{2,1,0:T(8,128)S(1)} %get-tuple-element.23.stat, ...), custom_call_target="tpu_custom_call" | custom-call | tf_op jit(solution)/shard_map/pallas_call | solution.py:37
  47.8 1.0 collective-permute-start.6
  48.7 4.3 %shard_map.94.rest_4_.rest_0_ = f32[12,8,128]{2,1,0:T(8,128)S(1)} custom-call(s32[56]{0:T(128)S(1)} %get-tuple-element.28.codes, f32[16,8,128]{2,1,0:T(8,128)S(1)} %get-tuple-element.32.v, f32[70,4,128,128]{3,2,1,0:T(8,128)S(1)} %get-tuple-element.29.tab), custom_call_target="tpu_custom_call" | custom-call | flops 21233664 | bytes 1048576 | tf_op jit(solution)/shard_map/pallas_call | solution.py:37
  53.1 3.7 %collective-permute-start.11 = (f32[8,8,128]{2,1,0:T(8,128)S(1)}, f32[8,8,128]{2,1,0:T(8,128)S(1)}, u32[]{:S(2)}, u32[]{:S(2)}) collective-permute-start(f32[8,8,128]{2,1,0:T(8,128)S(1)} %shard_map.95.rest_0_.rest_6_), channel_id=1, source_target_pairs={{0,12},{4,8},{8,4},{12,0},{1,13},{5,9},{9,5},{13,1},{2,14},{6,10},... | collective-permute-start | bytes 98312 | tf_op jit(solution)/shard_map/ppermute | solution.py:692
  57.5 4.1 %shard_map.96.rest_1_ = f32[8,8,128]{2,1,0:T(8,128)S(1)} custom-call(s32[56]{0:T(128)S(1)} %get-tuple-element.28.codes, f32[16,8,128]{2,1,0:T(8,128)S(1)} %get-tuple-element.32.v, f32[70,4,128,128]{3,2,1,0:T(8,128)S(1)} %get-tuple-element.29.tab, f32[8,8,128]{2,1,0:T(8,128)S(1)} %shard_map.95.rest_0_.rest_6_), custom_call_target="tpu_custom_call" | custom-call | flops 21233664 | bytes 1048576 | tf_op jit(solution)/shard_map/pallas_call | solution.py:37
  61.6 7.8 %shard_map.97 = (f32[16,8,128]{2,1,0:T(8,128)S(1)}, f32[16,8,128]{2,1,0:T(8,128)S(1)}, f32[5,8,128]{2,1,0:T(8,128)S(1)}, f32[8,128]{1,0:T(8,128)S(1)}) custom-call(s32[1]{0:T(128)} %bitcast.meta, s32[21]{0:T(128)S(1)} %get-tuple-element.24.codes, f32[8,128]{1,0:T(8,128)S(1)} %copy-done, f32[16,8,128]{2,1,0:T(8,128)S(1)} %get-tuple-element.23.stat, ...), custom_call_target="tpu_custom_call" | custom-call | tf_op jit(solution)/shard_map/pallas_call | solution.py:37
  70.4 1.0 collective-permute-start.12
  71.4 4.3 %shard_map.98.rest_4_.rest_0_ = f32[12,8,128]{2,1,0:T(8,128)S(1)} custom-call(s32[56]{0:T(128)S(1)} %get-tuple-element.28.codes, f32[16,8,128]{2,1,0:T(8,128)S(1)} %get-tuple-element.34.v, f32[70,4,128,128]{3,2,1,0:T(8,128)S(1)} %get-tuple-element.29.tab), custom_call_target="tpu_custom_call" | custom-call | flops 21233664 | bytes 1048576 | tf_op jit(solution)/shard_map/pallas_call | solution.py:37
  75.8 3.8 %collective-permute-start.17 = (f32[8,8,128]{2,1,0:T(8,128)S(1)}, f32[8,8,128]{2,1,0:T(8,128)S(1)}, u32[]{:S(2)}, u32[]{:S(2)}) collective-permute-start(f32[8,8,128]{2,1,0:T(8,128)S(1)} %shard_map.99.rest_0_.rest_6_), channel_id=1, source_target_pairs={{0,12},{4,8},{8,4},{12,0},{1,13},{5,9},{9,5},{13,1},{2,14},{6,10},... | collective-permute-start | bytes 98312 | tf_op jit(solution)/shard_map/ppermute | solution.py:692
  80.2 3.9 %shard_map.100.rest_1_ = f32[8,8,128]{2,1,0:T(8,128)S(1)} custom-call(s32[56]{0:T(128)S(1)} %get-tuple-element.28.codes, f32[16,8,128]{2,1,0:T(8,128)S(1)} %get-tuple-element.34.v, f32[70,4,128,128]{3,2,1,0:T(8,128)S(1)} %get-tuple-element.29.tab, f32[8,8,128]{2,1,0:T(8,128)S(1)} %shard_map.99.rest_0_.rest_6_), custom_call_target="tpu_custom_call" | custom-call | flops 21233664 | bytes 1048576 | tf_op jit(solution)/shard_map/pallas_call | solution.py:37
  84.4 7.5 %shard_map.101 = (f32[16,8,128]{2,1,0:T(8,128)S(1)}, f32[16,8,128]{2,1,0:T(8,128)S(1)}, f32[16,8,128]{2,1,0:T(8,128)S(1)}, f32[16,8,128]{2,1,0:T(8,128)S(1)}, f32[8,128]{1,0:T(8,128)S(1)}) custom-call(s32[1]{0:T(128)} %bitcast.meta, s32[21]{0:T(128)S(1)} %get-tuple-element.24.codes, f32[8,128]{1,0:T(8,128)S(1)} %copy-done, ...), custom_call_target="tpu_custom_call" | custom-call | tf_op jit(solution)/shard_map/pallas_call | solution.py:37
  92.7 1.2 %collective-permute-start.18 = (f32[8,128]{1,0:T(8,128)S(1)}, f32[8,128]{1,0:T(8,128)S(1)}, u32[]{:S(2)}, u32[]{:S(2)}) collective-permute-start(f32[8,128]{1,0:T(8,128)S(1)} %get-tuple-element.39.scal), channel_id=1, source_target_pairs={{0,1},{1,0},{2,3},{3,2},{4,5},{5,4},{6,7},{7,6},{8,9},{9,8},{10,11... | collective-permute-start | bytes 12296 | tf_op jit(solution)/shard_map/ppermute | solution.py:692
  93.9 1.2 %collective-permute-done.20 = f32[8,128]{1,0:T(8,128)S(1)} collective-permute-done((f32[8,128]{1,0:T(8,128)S(1)}, f32[8,128]{1,0:T(8,128)S(1)}, u32[]{:S(2)}, u32[]{:S(2)}) %collective-permute-start.20) | collective-permute-done | bytes 4128 | tf_op jit(solution)/shard_map/ppermute | solution.py:692
  95.7 3.6 %collective-permute-start.23 = (f32[8,128]{1,0:T(8,128)S(1)}, f32[8,128]{1,0:T(8,128)S(1)}, u32[]{:S(2)}, u32[]{:S(2)}) collective-permute-start(f32[8,128]{1,0:T(8,128)S(1)} %add_add_fusion.rest_0_), channel_id=1, source_target_pairs={{0,12},{4,8},{8,4},{12,0},{1,13},{5,9},{9,5},{13,1},{2,14},{6,10},... | collective-permute-start | bytes 12296 | tf_op jit(solution)/shard_map/ppermute | solution.py:692
  100.2 1.0 collective-permute-done.23.rest_3_
  101.2 2.6 %collective-permute-done.22.rest_2_ = f32[8,128]{1,0:T(8,128)S(1)} collective-permute-done((f32[8,128]{1,0:T(8,128)S(1)}, f32[8,128]{1,0:T(8,128)S(1)}, u32[]{:S(2)}, u32[]{:S(2)}) %collective-permute-start.22) | collective-permute-done | bytes 4128 | tf_op jit(solution)/shard_map/ppermute | solution.py:692
  (46 shorter events, 8.9 us)
Async XLA Ops:
  4.4 19.7 %collective-permute-start.2 = (f32[9,8,128]{2,1,0:T(8,128)S(1)}, f32[9,8,128]{2,1,0:T(8,128)S(1)}, u32[]{:S(2)}, u32[]{:S(2)}) collective-permute-start(f32[9,8,128]{2,1,0:T(8,128)S(1)} %get-tuple-element.27.rest_0_), channel_id=1, source_target_pairs={{0,3},{1,2},{2,1},{3,0},{4,7},{5,6},{6,5},{7,4},{8,11},{9,10},{10,... | collective-permute-start | bytes 110600 | tf_op jit(solution)/shard_map/ppermute | solution.py:692
  6.9 17.2 %collective-permute-start.1 = (f32[9,8,128]{2,1,0:T(8,128)S(1)}, f32[9,8,128]{2,1,0:T(8,128)S(1)}, u32[]{:S(2)}, u32[]{:S(2)}) collective-permute-start(f32[9,8,128]{2,1,0:T(8,128)S(1)} %get-tuple-element.27.rest_0_), channel_id=1, source_target_pairs={{0,2},{1,3},{2,0},{3,1},{4,6},{5,7},{6,4},{7,5},{8,10},{9,11},{10,... | collective-permute-start | bytes 110600 | tf_op jit(solution)/shard_map/ppermute | solution.py:692
  7.5 16.6 %collective-permute-start = (f32[9,8,128]{2,1,0:T(8,128)S(1)}, f32[9,8,128]{2,1,0:T(8,128)S(1)}, u32[]{:S(2)}, u32[]{:S(2)}) collective-permute-start(f32[9,8,128]{2,1,0:T(8,128)S(1)} %get-tuple-element.27.rest_0_), channel_id=1, source_target_pairs={{0,1},{1,0},{2,3},{3,2},{4,5},{5,4},{6,7},{7,6},{8,9},{9,8},{10,11... | collective-permute-start | bytes 110600 | tf_op jit(solution)/shard_map/ppermute | solution.py:692
  24.2 11.0 %collective-permute-start.5 = (f32[12,8,128]{2,1,0:T(8,128)S(1)}, f32[12,8,128]{2,1,0:T(8,128)S(1)}, u32[]{:S(2)}, u32[]{:S(2)}) collective-permute-start(f32[12,8,128]{2,1,0:T(8,128)S(1)} %shard_map.89.rest_4_.rest_0_.rest_2_), channel_id=1, source_target_pairs={{0,12},{4,8},{8,4},{12,0},{1,13},{5,9},{9,5},{13,1},{2,14},{6,10},... | collective-permute-start | bytes 147464 | tf_op jit(solution)/shard_map/ppermute | solution.py:692
  28.3 6.8 %collective-permute-start.4 = (f32[12,8,128]{2,1,0:T(8,128)S(1)}, f32[12,8,128]{2,1,0:T(8,128)S(1)}, u32[]{:S(2)}, u32[]{:S(2)}) collective-permute-start(f32[12,8,128]{2,1,0:T(8,128)S(1)} %shard_map.89.rest_4_.rest_0_.rest_2_), channel_id=1, source_target_pairs={{0,8},{4,12},{8,0},{12,4},{1,9},{5,13},{9,1},{13,5},{2,10},{6,14},... | collective-permute-start | bytes 147464 | tf_op jit(solution)/shard_map/ppermute | solution.py:692
  28.7 6.5 %collective-permute-start.3 = (f32[12,8,128]{2,1,0:T(8,128)S(1)}, f32[12,8,128]{2,1,0:T(8,128)S(1)}, u32[]{:S(2)}, u32[]{:S(2)}) collective-permute-start(f32[12,8,128]{2,1,0:T(8,128)S(1)} %shard_map.89.rest_4_.rest_0_.rest_2_), channel_id=1, source_target_pairs={{0,4},{4,0},{8,12},{12,8},{1,5},{5,1},{9,13},{13,9},{2,6},{6,2},{1... | collective-permute-start | bytes 147464 | tf_op jit(solution)/shard_map/ppermute | solution.py:692
  46.8 6.2 %collective-permute-start.8 = (f32[5,8,128]{2,1,0:T(8,128)S(1)}, f32[5,8,128]{2,1,0:T(8,128)S(1)}, u32[]{:S(2)}, u32[]{:S(2)}) collective-permute-start(f32[5,8,128]{2,1,0:T(8,128)S(1)} %get-tuple-element.33.rest_0_.rest_2_), channel_id=1, source_target_pairs={{0,3},{1,2},{2,1},{3,0},{4,7},{5,6},{6,5},{7,4},{8,11},{9,10},{10,... | collective-permute-start | bytes 61448 | tf_op jit(solution)/shard_map/ppermute | solution.py:692
  46.9 6.2 %collective-permute-start.7 = (f32[5,8,128]{2,1,0:T(8,128)S(1)}, f32[5,8,128]{2,1,0:T(8,128)S(1)}, u32[]{:S(2)}, u32[]{:S(2)}) collective-permute-start(f32[5,8,128]{2,1,0:T(8,128)S(1)} %get-tuple-element.33.rest_0_.rest_2_), channel_id=1, source_target_pairs={{0,2},{1,3},{2,0},{3,1},{4,6},{5,7},{6,4},{7,5},{8,10},{9,11},{10,... | collective-permute-start | bytes 61448 | tf_op jit(solution)/shard_map/ppermute | solution.py:692
  47.8 5.3 %collective-permute-start.6 = (f32[5,8,128]{2,1,0:T(8,128)S(1)}, f32[5,8,128]{2,1,0:T(8,128)S(1)}, u32[]{:S(2)}, u32[]{:S(2)}) collective-permute-start(f32[5,8,128]{2,1,0:T(8,128)S(1)} %get-tuple-element.33.rest_0_.rest_2_), channel_id=1, source_target_pairs={{0,1},{1,0},{2,3},{3,2},{4,5},{5,4},{6,7},{7,6},{8,9},{9,8},{10,11... | collective-permute-start | bytes 61448 | tf_op jit(solution)/shard_map/ppermute | solution.py:692
  53.1 8.5 %collective-permute-start.11 = (f32[8,8,128]{2,1,0:T(8,128)S(1)}, f32[8,8,128]{2,1,0:T(8,128)S(1)}, u32[]{:S(2)}, u32[]{:S(2)}) collective-permute-start(f32[8,8,128]{2,1,0:T(8,128)S(1)} %shard_map.95.rest_0_.rest_6_), channel_id=1, source_target_pairs={{0,12},{4,8},{8,4},{12,0},{1,13},{5,9},{9,5},{13,1},{2,14},{6,10},... | collective-permute-start | bytes 98312 | tf_op jit(solution)/shard_map/ppermute | solution.py:692
  56.8 4.9 %collective-permute-start.10 = (f32[8,8,128]{2,1,0:T(8,128)S(1)}, f32[8,8,128]{2,1,0:T(8,128)S(1)}, u32[]{:S(2)}, u32[]{:S(2)}) collective-permute-start(f32[8,8,128]{2,1,0:T(8,128)S(1)} %shard_map.95.rest_0_.rest_6_), channel_id=1, source_target_pairs={{0,8},{4,12},{8,0},{12,4},{1,9},{5,13},{9,1},{13,5},{2,10},{6,14},... | collective-permute-start | bytes 98312 | tf_op jit(solution)/shard_map/ppermute | solution.py:692
  56.8 4.9 %collective-permute-start.9 = (f32[8,8,128]{2,1,0:T(8,128)S(1)}, f32[8,8,128]{2,1,0:T(8,128)S(1)}, u32[]{:S(2)}, u32[]{:S(2)}) collective-permute-start(f32[8,8,128]{2,1,0:T(8,128)S(1)} %shard_map.95.rest_0_.rest_6_), channel_id=1, source_target_pairs={{0,4},{4,0},{8,12},{12,8},{1,5},{5,1},{9,13},{13,9},{2,6},{6,2},{1... | collective-permute-start | bytes 98312 | tf_op jit(solution)/shard_map/ppermute | solution.py:692
  69.5 6.2 %collective-permute-start.14 = (f32[5,8,128]{2,1,0:T(8,128)S(1)}, f32[5,8,128]{2,1,0:T(8,128)S(1)}, u32[]{:S(2)}, u32[]{:S(2)}) collective-permute-start(f32[5,8,128]{2,1,0:T(8,128)S(1)} %get-tuple-element.35.rest_0_.rest_2_), channel_id=1, source_target_pairs={{0,3},{1,2},{2,1},{3,0},{4,7},{5,6},{6,5},{7,4},{8,11},{9,10},{10,... | collective-permute-start | bytes 61448 | tf_op jit(solution)/shard_map/ppermute | solution.py:692
  69.6 6.2 %collective-permute-start.13 = (f32[5,8,128]{2,1,0:T(8,128)S(1)}, f32[5,8,128]{2,1,0:T(8,128)S(1)}, u32[]{:S(2)}, u32[]{:S(2)}) collective-permute-start(f32[5,8,128]{2,1,0:T(8,128)S(1)} %get-tuple-element.35.rest_0_.rest_2_), channel_id=1, source_target_pairs={{0,2},{1,3},{2,0},{3,1},{4,6},{5,7},{6,4},{7,5},{8,10},{9,11},{10,... | collective-permute-start | bytes 61448 | tf_op jit(solution)/shard_map/ppermute | solution.py:692
  70.4 5.3 %collective-permute-start.12 = (f32[5,8,128]{2,1,0:T(8,128)S(1)}, f32[5,8,128]{2,1,0:T(8,128)S(1)}, u32[]{:S(2)}, u32[]{:S(2)}) collective-permute-start(f32[5,8,128]{2,1,0:T(8,128)S(1)} %get-tuple-element.35.rest_0_.rest_2_), channel_id=1, source_target_pairs={{0,1},{1,0},{2,3},{3,2},{4,5},{5,4},{6,7},{7,6},{8,9},{9,8},{10,11... | collective-permute-start | bytes 61448 | tf_op jit(solution)/shard_map/ppermute | solution.py:692
  75.8 8.4 %collective-permute-start.17 = (f32[8,8,128]{2,1,0:T(8,128)S(1)}, f32[8,8,128]{2,1,0:T(8,128)S(1)}, u32[]{:S(2)}, u32[]{:S(2)}) collective-permute-start(f32[8,8,128]{2,1,0:T(8,128)S(1)} %shard_map.99.rest_0_.rest_6_), channel_id=1, source_target_pairs={{0,12},{4,8},{8,4},{12,0},{1,13},{5,9},{9,5},{13,1},{2,14},{6,10},... | collective-permute-start | bytes 98312 | tf_op jit(solution)/shard_map/ppermute | solution.py:692
  79.6 4.8 %collective-permute-start.16 = (f32[8,8,128]{2,1,0:T(8,128)S(1)}, f32[8,8,128]{2,1,0:T(8,128)S(1)}, u32[]{:S(2)}, u32[]{:S(2)}) collective-permute-start(f32[8,8,128]{2,1,0:T(8,128)S(1)} %shard_map.99.rest_0_.rest_6_), channel_id=1, source_target_pairs={{0,8},{4,12},{8,0},{12,4},{1,9},{5,13},{9,1},{13,5},{2,10},{6,14},... | collective-permute-start | bytes 98312 | tf_op jit(solution)/shard_map/ppermute | solution.py:692
  79.6 4.8 %collective-permute-start.15 = (f32[8,8,128]{2,1,0:T(8,128)S(1)}, f32[8,8,128]{2,1,0:T(8,128)S(1)}, u32[]{:S(2)}, u32[]{:S(2)}) collective-permute-start(f32[8,8,128]{2,1,0:T(8,128)S(1)} %shard_map.99.rest_0_.rest_6_), channel_id=1, source_target_pairs={{0,4},{4,0},{8,12},{12,8},{1,5},{5,1},{9,13},{13,9},{2,6},{6,2},{1... | collective-permute-start | bytes 98312 | tf_op jit(solution)/shard_map/ppermute | solution.py:692
  91.9 3.1 %collective-permute-start.20 = (f32[8,128]{1,0:T(8,128)S(1)}, f32[8,128]{1,0:T(8,128)S(1)}, u32[]{:S(2)}, u32[]{:S(2)}) collective-permute-start(f32[8,128]{1,0:T(8,128)S(1)} %get-tuple-element.39.scal), channel_id=1, source_target_pairs={{0,3},{1,2},{2,1},{3,0},{4,7},{5,6},{6,5},{7,4},{8,11},{9,10},{10,... | collective-permute-start | bytes 12296 | tf_op jit(solution)/shard_map/ppermute | solution.py:692
  92.0 3.7 %collective-permute-start.19 = (f32[8,128]{1,0:T(8,128)S(1)}, f32[8,128]{1,0:T(8,128)S(1)}, u32[]{:S(2)}, u32[]{:S(2)}) collective-permute-start(f32[8,128]{1,0:T(8,128)S(1)} %get-tuple-element.39.scal), channel_id=1, source_target_pairs={{0,2},{1,3},{2,0},{3,1},{4,6},{5,7},{6,4},{7,5},{8,10},{9,11},{10,... | collective-permute-start | bytes 12296 | tf_op jit(solution)/shard_map/ppermute | solution.py:692
  92.7 3.0 %collective-permute-start.18 = (f32[8,128]{1,0:T(8,128)S(1)}, f32[8,128]{1,0:T(8,128)S(1)}, u32[]{:S(2)}, u32[]{:S(2)}) collective-permute-start(f32[8,128]{1,0:T(8,128)S(1)} %get-tuple-element.39.scal), channel_id=1, source_target_pairs={{0,1},{1,0},{2,3},{3,2},{4,5},{5,4},{6,7},{7,6},{8,9},{9,8},{10,11... | collective-permute-start | bytes 12296 | tf_op jit(solution)/shard_map/ppermute | solution.py:692
  95.7 5.5 %collective-permute-start.23 = (f32[8,128]{1,0:T(8,128)S(1)}, f32[8,128]{1,0:T(8,128)S(1)}, u32[]{:S(2)}, u32[]{:S(2)}) collective-permute-start(f32[8,128]{1,0:T(8,128)S(1)} %add_add_fusion.rest_0_), channel_id=1, source_target_pairs={{0,12},{4,8},{8,4},{12,0},{1,13},{5,9},{9,5},{13,1},{2,14},{6,10},... | collective-permute-start | bytes 12296 | tf_op jit(solution)/shard_map/ppermute | solution.py:692
  99.3 4.5 %collective-permute-start.22 = (f32[8,128]{1,0:T(8,128)S(1)}, f32[8,128]{1,0:T(8,128)S(1)}, u32[]{:S(2)}, u32[]{:S(2)}) collective-permute-start(f32[8,128]{1,0:T(8,128)S(1)} %add_add_fusion.rest_0_), channel_id=1, source_target_pairs={{0,8},{4,12},{8,0},{12,4},{1,9},{5,13},{9,1},{13,5},{2,10},{6,14},... | collective-permute-start | bytes 12296 | tf_op jit(solution)/shard_map/ppermute | solution.py:692
  99.3 4.5 %collective-permute-start.21 = (f32[8,128]{1,0:T(8,128)S(1)}, f32[8,128]{1,0:T(8,128)S(1)}, u32[]{:S(2)}, u32[]{:S(2)}) collective-permute-start(f32[8,128]{1,0:T(8,128)S(1)} %add_add_fusion.rest_0_), channel_id=1, source_target_pairs={{0,4},{4,0},{8,12},{12,8},{1,5},{5,1},{9,13},{13,9},{2,6},{6,2},{1... | collective-permute-start | bytes 12296 | tf_op jit(solution)/shard_map/ppermute | solution.py:692
  (2 other events, 10.1 us)

commit v4 on v3

--- a/solution.py
+++ b/solution.py
@@ -15,7 +15,7 @@
 NODE_PAD = 128
 ITERS = 2
 SUB = 8
-CHUNK = 32
+CHUNK = 8
 
 side_length = 32.0
 layer_gap = 2.5
@@ -26,10 +26,11 @@
 
 VM = pl.BlockSpec(memory_space=pltpu.VMEM)
 SM = pl.BlockSpec(memory_space=pltpu.SMEM)
+FAR = pl.BlockSpec(memory_space=pltpu.HBM)
 TABLE_LIMIT = 16 << 20
 
 
-def call(body, outs, args, smem=0, scratch=(), limit=None, cost=None, pinned=(), far=False, more=(), lists=()):
+def call(body, outs, args, smem=0, scratch=(), limit=None, cost=None, pinned=(), far=0, more=(), lists=()):
     shapes = [
         pltpu.VMEM(shape, f32) if at in pinned else jax.ShapeDtypeStruct(shape, f32)
         for at, shape in enumerate(outs)
@@ -37,7 +38,7 @@
     return list(pl.pallas_call(
         body,
         out_shape=shapes,
-        in_specs=[SM] * smem + [pl.BlockSpec(memory_space=pltpu.HBM) if far else VM] * (len(args) - smem),
+        in_specs=[SM] * smem + [FAR] * far + [VM] * (len(args) - smem - far),
         out_specs=[VM] * len(outs) + [SM] * len(lists),
         scratch_shapes=[pltpu.VMEM(shape, f32) for shape in scratch] + list(more),
         compiler_params=pltpu.CompilerParams(vmem_limit_bytes=limit or (12 << 20)),
@@ -57,8 +58,11 @@
     live = index < count**3
     safe = np.where(live, index, 0)
     levels = np.stack([safe // (count * count), safe // count % count, safe % count])
-    picks = (levels[:, :, None] == np.arange(8)) * 1.0
-    picks[0] *= live[:, None]
+    picks = np.zeros((3, NODE_PAD, count, 8))
+    for d in range(3):
+        picks[d, index, levels[d], d] = 1.0
+    picks[0] *= live[:, None, None]
+    picks = picks.reshape(3 * NODE_PAD, count * 8)
     nodes = np.zeros((8, NODE_PAD))
     nodes[0] = 0.5 * (1.0 + roots[levels[0]])
     nodes[1] = 0.5 * (1.0 + roots[levels[1]])
@@ -82,11 +86,8 @@
 
 def columns(tiles, count, out):
     for t, tile in enumerate(tiles):
-        if tile.shape[0] < 8:
-            tile = jnp.concatenate([tile, jnp.zeros((8 - tile.shape[0], BLOCK), f32)], axis=0)
-        turned = tile.T
         for k in range(count):
-            out[t, k] = jnp.broadcast_to(turned[:, k : k + 1], (BLOCK, BLOCK))
+            out[t, k] = jnp.broadcast_to(tile[k : k + 1, :], (BLOCK, BLOCK)).T
 
 
 def diagonal(step):
@@ -224,32 +225,26 @@
     box = jnp.where(lane < total // BOXES_DEV, first, first + 1).astype(f32)
     p = pos[...]
     al = alpha[...]
-    coords = [
-        p[0:1] / 16.0 - 1.0,
-        p[1:2] / 16.0 - 1.0,
-        2.0 * (p[2:3] - box * box_height) / box_height - 1.0,
-    ]
+    side = jnp.concatenate([p, jnp.zeros((5, total), f32)], axis=0)
+    tall = lax.broadcasted_iota(jnp.int32, (8, total), 0) == 2
+    u = jnp.where(tall, 2.0 * (side - box * box_height) / box_height - 1.0, side / 16.0 - 1.0)
+    terms = [None, u]
+    for degree in range(2, ORDER):
+        prev = terms[-2] if degree > 2 else 1.0
+        terms.append(2.0 * u * terms[-1] - prev)
     levels = []
-    for u in coords:
-        terms = [None, u]
-        for degree in range(2, ORDER):
-            prev = terms[-2] if degree > 2 else 1.0
-            terms.append(2.0 * u * terms[-1] - prev)
-        rows = []
-        for k in range(ORDER):
-            value = float(coeff[k, 0]) + float(coeff[k, 1]) * terms[1]
-            for n in range(2, ORDER):
-                value = value + float(coeff[k, n]) * terms[n]
-            rows.append(value)
-        levels.append(jnp.concatenate(rows + [jnp.zeros((8 - ORDER, total), f32)], axis=0))
+    for k in range(ORDER):
+        value = float(coeff[k, 0]) + float(coeff[k, 1]) * terms[1]
+        for n in range(2, ORDER):
+            value = value + float(coeff[k, n]) * terms[n]
+        levels.append(value)
+    levels = jnp.concatenate(levels, axis=0)
     wide = 4 * BLOCK
     for begin in range(0, total, wide):
-        value = None
-        for d in range(3):
-            part = jnp.dot(
-                picks[d], levels[d][:, begin : begin + wide], precision=highest, preferred_element_type=f32
-            )
-            value = part if value is None else value * part
+        value = jnp.dot(
+            picks[...], levels[:, begin : begin + wide], precision=highest, preferred_element_type=f32
+        )
+        value = value[:BLOCK] * value[BLOCK : 2 * BLOCK] * value[2 * BLOCK :]
         for t in range(4):
             phi[begin // BLOCK + t] = value[:, t * BLOCK : (t + 1) * BLOCK]
     start = al * field[...]
@@ -299,7 +294,11 @@
     return code & 255, (code >> 8) & 255, code >> 16
 
 
-def tensors_body(mask, stat, out, own_list, halo_list, col, *, half, tiles, reach, length_z):
+def tensors_body(mask_in, stat, out, own_list, halo_list, col, mask, sem, *, half, tiles, reach, length_z):
+    copy = pltpu.make_async_copy(mask_in, mask, sem)
+    copy.start()
+    columns([stat[t] for t in range(tiles)], 5, col)
+    copy.wait()
     last = own_list.shape[0] - 2
     n = jnp.int32(0)
     for b in range(tiles):
@@ -316,7 +315,6 @@
         halo_list[m] = jnp.int32(index + (h << 8) + (c << 16))
         m = m + mask[c, at]
     halo_list[halo_list.shape[0] - 1] = m
-    columns([stat[t] for t in range(tiles)], 5, col)
 
     def visit(at, unused):
         slot, b, other = unpack(own_list[jnp.maximum(at - tiles, 0)])
@@ -453,12 +451,12 @@
 
     def visit(d, unused):
         def put(k, at, value):
-            out[d - 1, k, at, :] = value
+            out[at.start // SUB, d - 1, k] = value
 
         far_tensor(geo, d.astype(f32), put, box_height, length_z)
         return unused
 
-    lax.fori_loop(1, out.shape[0] + 1, visit, 0)
+    lax.fori_loop(1, out.shape[1] + 1, visit, 0)
 
 
 def apply_tensor(t, v):
@@ -471,29 +469,32 @@
 def far_nodes(table, geo, wide, fcol, boxes, box_height, length_z):
     if table is not None:
         def rows(step, unused):
-            ats = [pl.ds(pl.multiple_of(step * 2 * SUB + k * SUB, SUB), SUB) for k in range(2)]
+            ats = [pl.ds(pl.multiple_of(step * SUB, SUB), SUB)]
 
             def load(d):
-                return [[table[d - 1, k, at, :] for k in range(4)] for at in ats]
+                return [[table[step, d - 1, k] for k in range(4)]]
 
             def field(ts, k):
                 v = [wide[k, c] for c in range(3)]
                 return sum([apply_tensor(t, v) for t in ts], ())
 
             acc = field(load(boxes - 1), boxes - 1) + field(load(1), 2)
-            for d in range(2, boxes - 1):
+            def visit(d, acc):
                 ts = load(d)
                 new = field(ts, d) + field(ts, d + 1)
-                acc = tuple(a + n for a, n in zip(acc, new))
+                return tuple(a + n for a, n in zip(acc, new))
+
+            acc = visit(2, acc)
+            acc = lax.fori_loop(3, boxes - 1, visit, acc, unroll=7)
             for box in range(BOXES_DEV):
-                for half in range(2):
+                for half in range(1):
                     for c in range(3):
                         fcol[box, c, ats[half], :] = jnp.broadcast_to(
-                            jnp.sum(acc[box * 6 + half * 3 + c], axis=1, keepdims=True), (SUB, BLOCK)
+                            jnp.sum(acc[box * 3 + half * 3 + c], axis=1, keepdims=True), (SUB, BLOCK)
                         )
             return unused
 
-        lax.fori_loop(0, BLOCK // (2 * SUB), rows, 0)
+        lax.fori_loop(0, BLOCK // SUB, rows, 0)
         return
     for box in range(BOXES_DEV):
         for c in range(3):
@@ -723,7 +724,7 @@
         [meta] + [far_memory(x) for x in (positions, polarizability[None], permanent_field, group_id[None], jnp.asarray(picks))],
         smem=1,
         limit=16 << 20,
-        far=True,
+        far=5,
         more=[
             pltpu.VMEM((3, atoms), f32),
             pltpu.VMEM((1, atoms), f32),
@@ -737,9 +738,10 @@
     tab, own_list, halo_list = call(
         functools.partial(tensors_body, half=half, tiles=tiles, reach=reach, length_z=length_z),
         [(count, 4, BLOCK, BLOCK)],
-        [mask, stat],
-        smem=1,
+        [far_memory(mask), stat],
+        far=1,
         scratch=[(tiles, 5, BLOCK, BLOCK)],
+        more=[pltpu.SMEM(mask.shape, jnp.int32), pltpu.SemaphoreType.DMA],
         cost=pl.CostEstimate(flops=count * BLOCK * BLOCK * 70, bytes_accessed=1 << 20, transcendentals=count * BLOCK * BLOCK * 2),
         pinned=(0,),
         lists=(count - tiles + 2, len(halo_pairs(tiles, reach)) + 1),
@@ -748,7 +750,7 @@
     if kept:
         table = call(
             functools.partial(far_tensors_body, box_height=box_height, length_z=length_z),
-            [(boxes - 1, 4, BLOCK, BLOCK)],
+            [(BLOCK // SUB, boxes - 1, 4, SUB, BLOCK)],
             [nodes],
             scratch=[(4, BLOCK, BLOCK)],
             cost=pl.CostEstimate(flops=boxes * BLOCK * BLOCK * 28, bytes_accessed=1 << 20, transcendentals=boxes * BLOCK * BLOCK),

time: 105 us -> 96.6 us (0.920)
  Pallas kernels: 70 us -> 61.7 us
  starting transfers between devices: 27.2 us -> 30.4 us
  waiting for transfers between devices: 5.75 us -> 3.45 us
    pallas_call x17, Pallas kernels: 70 us -> 61.7 us  [call(): pl.pallas_call(body, out_shape=shapes, in_specs=[SM] * smem + [FAR] * far...]
    ppermute x24, starting transfers between devices: 27.2 us -> 30.4 us  [swap(): got.append(lax.ppermute(x, axes, [(i, i ^ s) for i in range(count)]))]
    ppermute x24, waiting for transfers between devices: 5.75 us -> 3.45 us  [swap(): got.append(lax.ppermute(x, axes, [(i, i ^ s) for i in range(count)]))]
  transfers between devices with their start and end apart: 24 -> 24, of which waited for: 5 -> 5; matrix products, arithmetic and copies ran while one was open for 0% -> 0% of each run, Pallas kernels for 37% -> 36%
where the time goes in v4:
time: 96.6 us; the launch traced here: 96.5 us
  Pallas kernels  61.7 us (64%)
  starting transfers between devices  30.4 us (31%)
  waiting for transfers between devices  3.45 us (4%)
    pallas_call x17, Pallas kernels, call(): pl.pallas_call(body, out_shape=shapes, in_specs=[SM] * smem + [FAR] * far...  61.7 us
    ppermute x24, starting transfers between devices, swap(): got.append(lax.ppermute(x, axes, [(i, i ^ s) for i in range(count)]))  30.4 us
    ppermute x24, waiting for transfers between devices, swap(): got.append(lax.ppermute(x, axes, [(i, i ^ s) for i in range(count)]))  3.45 us
  transfers between devices with their start and end apart: 24, of which 5 were waited for; matrix products, arithmetic and copies ran while one was open for 0% of the time, Pallas kernels for 36%

profile of v4, /device:TPU:0, one launch (start us, length us, event | category | flops | bytes accessed | tf_op | source)
XLA Modules:
  0.0 96.5 jit_solution(655453579399086380)
XLA Ops:
  0.6 3.8 %shard_map.86 = (f32[16,8,128]{2,1,0:T(8,128)S(1)}, f32[16,8,128]{2,1,0:T(8,128)S(1)}, f32[16,128,128]{2,1,0:T(8,128)S(1)}, f32[9,8,128]{2,1,0:T(8,128)S(1)}) custom-call(s32[1]{0:T(128)} %bitcast.meta, f32[3,2048]{1,0:T(4,128)} %pos_in.1, f32[1,2048]{1,0:T(1,128)} %bitcast.3, f32[3,2048]{1,0:T(4,128)} %field_in.1, s32[1,2048]{1,0:T(1,128)} %bitcast.4, ...), custom_call_target="tpu_custom_call" | custom-call | tf_op jit(solution)/shard_map/pallas_call | solution.py:38
  4.5 2.4 %collective-permute-start.2 = (f32[9,8,128]{2,1,0:T(8,128)S(1)}, f32[9,8,128]{2,1,0:T(8,128)S(1)}, u32[]{:S(2)}, u32[]{:S(2)}) collective-permute-start(f32[9,8,128]{2,1,0:T(8,128)S(1)} %get-tuple-element.27.rest_0_), channel_id=1, source_target_pairs={{0,3},{1,2},{2,1},{3,0},{4,7},{5,6},{6,5},{7,4},{8,11},{9,10},{10,... | collective-permute-start | bytes 110600 | tf_op jit(solution)/shard_map/ppermute | solution.py:693
  7.6 10.2 %shard_map.87 = (f32[70,4,128,128]{3,2,1,0:T(8,128)S(1)}, s32[56]{0:T(128)S(1)}, s32[21]{0:T(128)S(1)}) custom-call(s32[16,9]{1,0:T(8,128)} %mask_in.1, f32[16,8,128]{2,1,0:T(8,128)S(1)} %get-tuple-element.23.stat), custom_call_target="tpu_custom_call" | custom-call | flops 80281600 | bytes 1048576 | tf_op jit(solution)/shard_map/pallas_call | solution.py:38
  17.8 4.3 %shard_map.88.rest_4_.rest_0_ = f32[12,8,128]{2,1,0:T(8,128)S(1)} custom-call(s32[56]{0:T(128)S(1)} %get-tuple-element.28.codes, f32[16,8,128]{2,1,0:T(8,128)S(1)} %get-tuple-element.25.v.rest_11_, f32[70,4,128,128]{3,2,1,0:T(8,128)S(1)} %get-tuple-element.29.tab), custom_call_target="tpu_custom_call" | custom-call | flops 21233664 | bytes 1048576 | tf_op jit(solution)/shard_map/pallas_call | solution.py:38
  22.2 4.1 %collective-permute-start.5 = (f32[12,8,128]{2,1,0:T(8,128)S(1)}, f32[12,8,128]{2,1,0:T(8,128)S(1)}, u32[]{:S(2)}, u32[]{:S(2)}) collective-permute-start(f32[12,8,128]{2,1,0:T(8,128)S(1)} %shard_map.89.rest_4_.rest_0_.rest_2_), channel_id=1, source_target_pairs={{0,12},{4,8},{8,4},{12,0},{1,13},{5,9},{9,5},{13,1},{2,14},{6,10},... | collective-permute-start | bytes 147464 | tf_op jit(solution)/shard_map/ppermute | solution.py:693
  27.0 2.1 %shard_map.92.rest_7_.rest_10_ = f32[16,31,4,8,128]{4,3,2,1,0:T(8,128)S(1)} custom-call(f32[8,128]{1,0:T(8,128)S(1)} %copy-done), custom_call_target="tpu_custom_call" | custom-call | flops 14680064 | bytes 1048576 | tf_op jit(solution)/shard_map/pallas_call | solution.py:38
  29.0 3.3 %shard_map.91.rest_1_ = f32[8,8,128]{2,1,0:T(8,128)S(1)} custom-call(s32[56]{0:T(128)S(1)} %get-tuple-element.28.codes, f32[16,8,128]{2,1,0:T(8,128)S(1)} %get-tuple-element.25.v.rest_11_, f32[70,4,128,128]{3,2,1,0:T(8,128)S(1)} %get-tuple-element.29.tab, f32[12,8,128]{2,1,0:T(8,128)S(1)} %shard_map.89.rest_4_.rest_0_.rest_2_), custom_call_target="tpu_custom_call" | custom-call | flops 21233664 | bytes 1048576 | tf_op jit(solution)/shard_map/pallas_call | solution.py:38
  32.3 3.1 %shard_map.90 = (f32[20,4,128,128]{3,2,1,0:T(8,128)S(1)}, f32[8,8,128]{2,1,0:T(8,128)S(1)}) custom-call(s32[1]{0:T(128)} %bitcast.meta, s32[21]{0:T(128)S(1)} %get-tuple-element.24.codes, f32[16,8,128]{2,1,0:T(8,128)S(1)} %get-tuple-element.23.stat, f32[9,8,128]{2,1,0:T(8,128)S(1)} %get-tuple-element.27.rest_0_, ...), custom_call_target="tpu_custom_call" | custom-call | tf_op jit(solution)/shard_map/pallas_call | solution.py:38
  35.4 6.3 %shard_map.93 = (f32[16,8,128]{2,1,0:T(8,128)S(1)}, f32[16,8,128]{2,1,0:T(8,128)S(1)}, f32[5,8,128]{2,1,0:T(8,128)S(1)}) custom-call(s32[1]{0:T(128)} %bitcast.meta, s32[21]{0:T(128)S(1)} %get-tuple-element.24.codes, f32[8,128]{1,0:T(8,128)S(1)} %copy-done, f32[16,8,128]{2,1,0:T(8,128)S(1)} %get-tuple-element.23.stat, ...), custom_call_target="tpu_custom_call" | custom-call | tf_op jit(solution)/shard_map/pallas_call | solution.py:38
  41.7 2.0 %collective-permute-start.8 = (f32[5,8,128]{2,1,0:T(8,128)S(1)}, f32[5,8,128]{2,1,0:T(8,128)S(1)}, u32[]{:S(2)}, u32[]{:S(2)}) collective-permute-start(f32[5,8,128]{2,1,0:T(8,128)S(1)} %get-tuple-element.33.rest_0_.rest_2_), channel_id=1, source_target_pairs={{0,3},{1,2},{2,1},{3,0},{4,7},{5,6},{6,5},{7,4},{8,11},{9,10},{10,... | collective-permute-start | bytes 61448 | tf_op jit(solution)/shard_map/ppermute | solution.py:693
  43.7 1.7 %collective-permute-start.7 = (f32[5,8,128]{2,1,0:T(8,128)S(1)}, f32[5,8,128]{2,1,0:T(8,128)S(1)}, u32[]{:S(2)}, u32[]{:S(2)}) collective-permute-start(f32[5,8,128]{2,1,0:T(8,128)S(1)} %get-tuple-element.33.rest_0_.rest_2_), channel_id=1, source_target_pairs={{0,2},{1,3},{2,0},{3,1},{4,6},{5,7},{6,4},{7,5},{8,10},{9,11},{10,... | collective-permute-start | bytes 61448 | tf_op jit(solution)/shard_map/ppermute | solution.py:693
  45.5 4.3 %shard_map.94.rest_4_.rest_0_ = f32[12,8,128]{2,1,0:T(8,128)S(1)} custom-call(s32[56]{0:T(128)S(1)} %get-tuple-element.28.codes, f32[16,8,128]{2,1,0:T(8,128)S(1)} %get-tuple-element.32.v, f32[70,4,128,128]{3,2,1,0:T(8,128)S(1)} %get-tuple-element.29.tab), custom_call_target="tpu_custom_call" | custom-call | flops 21233664 | bytes 1048576 | tf_op jit(solution)/shard_map/pallas_call | solution.py:38
  49.8 2.3 %collective-permute-start.11 = (f32[8,8,128]{2,1,0:T(8,128)S(1)}, f32[8,8,128]{2,1,0:T(8,128)S(1)}, u32[]{:S(2)}, u32[]{:S(2)}) collective-permute-start(f32[8,8,128]{2,1,0:T(8,128)S(1)} %shard_map.95.rest_0_.rest_6_), channel_id=1, source_target_pairs={{0,12},{4,8},{8,4},{12,0},{1,13},{5,9},{9,5},{13,1},{2,14},{6,10},... | collective-permute-start | bytes 98312 | tf_op jit(solution)/shard_map/ppermute | solution.py:693
  52.1 2.2 %collective-permute-start.9 = (f32[8,8,128]{2,1,0:T(8,128)S(1)}, f32[8,8,128]{2,1,0:T(8,128)S(1)}, u32[]{:S(2)}, u32[]{:S(2)}) collective-permute-start(f32[8,8,128]{2,1,0:T(8,128)S(1)} %shard_map.95.rest_0_.rest_6_), channel_id=1, source_target_pairs={{0,4},{4,0},{8,12},{12,8},{1,5},{5,1},{9,13},{13,9},{2,6},{6,2},{1... | collective-permute-start | bytes 98312 | tf_op jit(solution)/shard_map/ppermute | solution.py:693
  54.3 3.3 %shard_map.96.rest_1_ = f32[8,8,128]{2,1,0:T(8,128)S(1)} custom-call(s32[56]{0:T(128)S(1)} %get-tuple-element.28.codes, f32[16,8,128]{2,1,0:T(8,128)S(1)} %get-tuple-element.32.v, f32[70,4,128,128]{3,2,1,0:T(8,128)S(1)} %get-tuple-element.29.tab, f32[8,8,128]{2,1,0:T(8,128)S(1)} %shard_map.95.rest_0_.rest_6_), custom_call_target="tpu_custom_call" | custom-call | flops 21233664 | bytes 1048576 | tf_op jit(solution)/shard_map/pallas_call | solution.py:38
  57.6 6.5 %shard_map.97 = (f32[16,8,128]{2,1,0:T(8,128)S(1)}, f32[16,8,128]{2,1,0:T(8,128)S(1)}, f32[5,8,128]{2,1,0:T(8,128)S(1)}, f32[8,128]{1,0:T(8,128)S(1)}) custom-call(s32[1]{0:T(128)} %bitcast.meta, s32[21]{0:T(128)S(1)} %get-tuple-element.24.codes, f32[8,128]{1,0:T(8,128)S(1)} %copy-done, f32[16,8,128]{2,1,0:T(8,128)S(1)} %get-tuple-element.23.stat, ...), custom_call_target="tpu_custom_call" | custom-call | tf_op jit(solution)/shard_map/pallas_call | solution.py:38
  65.0 1.8 %collective-permute-start.13 = (f32[5,8,128]{2,1,0:T(8,128)S(1)}, f32[5,8,128]{2,1,0:T(8,128)S(1)}, u32[]{:S(2)}, u32[]{:S(2)}) collective-permute-start(f32[5,8,128]{2,1,0:T(8,128)S(1)} %get-tuple-element.35.rest_0_.rest_2_), channel_id=1, source_target_pairs={{0,2},{1,3},{2,0},{3,1},{4,6},{5,7},{6,4},{7,5},{8,10},{9,11},{10,... | collective-permute-start | bytes 61448 | tf_op jit(solution)/shard_map/ppermute | solution.py:693
  66.8 4.5 %shard_map.98.rest_4_.rest_0_ = f32[12,8,128]{2,1,0:T(8,128)S(1)} custom-call(s32[56]{0:T(128)S(1)} %get-tuple-element.28.codes, f32[16,8,128]{2,1,0:T(8,128)S(1)} %get-tuple-element.34.v, f32[70,4,128,128]{3,2,1,0:T(8,128)S(1)} %get-tuple-element.29.tab), custom_call_target="tpu_custom_call" | custom-call | flops 21233664 | bytes 1048576 | tf_op jit(solution)/shard_map/pallas_call | solution.py:38
  71.3 1.8 %collective-permute-start.17 = (f32[8,8,128]{2,1,0:T(8,128)S(1)}, f32[8,8,128]{2,1,0:T(8,128)S(1)}, u32[]{:S(2)}, u32[]{:S(2)}) collective-permute-start(f32[8,8,128]{2,1,0:T(8,128)S(1)} %shard_map.99.rest_0_.rest_6_), channel_id=1, source_target_pairs={{0,12},{4,8},{8,4},{12,0},{1,13},{5,9},{9,5},{13,1},{2,14},{6,10},... | collective-permute-start | bytes 98312 | tf_op jit(solution)/shard_map/ppermute | solution.py:693
  73.1 2.7 %collective-permute-start.15 = (f32[8,8,128]{2,1,0:T(8,128)S(1)}, f32[8,8,128]{2,1,0:T(8,128)S(1)}, u32[]{:S(2)}, u32[]{:S(2)}) collective-permute-start(f32[8,8,128]{2,1,0:T(8,128)S(1)} %shard_map.99.rest_0_.rest_6_), channel_id=1, source_target_pairs={{0,4},{4,0},{8,12},{12,8},{1,5},{5,1},{9,13},{13,9},{2,6},{6,2},{1... | collective-permute-start | bytes 98312 | tf_op jit(solution)/shard_map/ppermute | solution.py:693
  75.8 3.3 %shard_map.100.rest_1_ = f32[8,8,128]{2,1,0:T(8,128)S(1)} custom-call(s32[56]{0:T(128)S(1)} %get-tuple-element.28.codes, f32[16,8,128]{2,1,0:T(8,128)S(1)} %get-tuple-element.34.v, f32[70,4,128,128]{3,2,1,0:T(8,128)S(1)} %get-tuple-element.29.tab, f32[8,8,128]{2,1,0:T(8,128)S(1)} %shard_map.99.rest_0_.rest_6_), custom_call_target="tpu_custom_call" | custom-call | flops 21233664 | bytes 1048576 | tf_op jit(solution)/shard_map/pallas_call | solution.py:38
  79.1 6.1 %shard_map.101 = (f32[16,8,128]{2,1,0:T(8,128)S(1)}, f32[16,8,128]{2,1,0:T(8,128)S(1)}, f32[16,8,128]{2,1,0:T(8,128)S(1)}, f32[16,8,128]{2,1,0:T(8,128)S(1)}, f32[8,128]{1,0:T(8,128)S(1)}) custom-call(s32[1]{0:T(128)} %bitcast.meta, s32[21]{0:T(128)S(1)} %get-tuple-element.24.codes, f32[8,128]{1,0:T(8,128)S(1)} %copy-done, ...), custom_call_target="tpu_custom_call" | custom-call | tf_op jit(solution)/shard_map/pallas_call | solution.py:38
  86.1 1.8 %collective-permute-start.19 = (f32[8,128]{1,0:T(8,128)S(1)}, f32[8,128]{1,0:T(8,128)S(1)}, u32[]{:S(2)}, u32[]{:S(2)}) collective-permute-start(f32[8,128]{1,0:T(8,128)S(1)} %get-tuple-element.39.scal), channel_id=1, source_target_pairs={{0,2},{1,3},{2,0},{3,1},{4,6},{5,7},{6,4},{7,5},{8,10},{9,11},{10,... | collective-permute-start | bytes 12296 | tf_op jit(solution)/shard_map/ppermute | solution.py:693
  91.2 2.9 %collective-permute-start.21 = (f32[8,128]{1,0:T(8,128)S(1)}, f32[8,128]{1,0:T(8,128)S(1)}, u32[]{:S(2)}, u32[]{:S(2)}) collective-permute-start(f32[8,128]{1,0:T(8,128)S(1)} %add_add_fusion.rest_0_), channel_id=1, source_target_pairs={{0,4},{4,0},{8,12},{12,8},{1,5},{5,1},{9,13},{13,9},{2,6},{6,2},{1... | collective-permute-start | bytes 12296 | tf_op jit(solution)/shard_map/ppermute | solution.py:693
  (44 shorter events, 9.0 us)
Async XLA Ops:
  4.5 17.6 %collective-permute-start.2 = (f32[9,8,128]{2,1,0:T(8,128)S(1)}, f32[9,8,128]{2,1,0:T(8,128)S(1)}, u32[]{:S(2)}, u32[]{:S(2)}) collective-permute-start(f32[9,8,128]{2,1,0:T(8,128)S(1)} %get-tuple-element.27.rest_0_), channel_id=1, source_target_pairs={{0,3},{1,2},{2,1},{3,0},{4,7},{5,6},{6,5},{7,4},{8,11},{9,10},{10,... | collective-permute-start | bytes 110600 | tf_op jit(solution)/shard_map/ppermute | solution.py:693
  6.9 15.2 %collective-permute-start.1 = (f32[9,8,128]{2,1,0:T(8,128)S(1)}, f32[9,8,128]{2,1,0:T(8,128)S(1)}, u32[]{:S(2)}, u32[]{:S(2)}) collective-permute-start(f32[9,8,128]{2,1,0:T(8,128)S(1)} %get-tuple-element.27.rest_0_), channel_id=1, source_target_pairs={{0,2},{1,3},{2,0},{3,1},{4,6},{5,7},{6,4},{7,5},{8,10},{9,11},{10,... | collective-permute-start | bytes 110600 | tf_op jit(solution)/shard_map/ppermute | solution.py:693
  7.6 14.6 %collective-permute-start = (f32[9,8,128]{2,1,0:T(8,128)S(1)}, f32[9,8,128]{2,1,0:T(8,128)S(1)}, u32[]{:S(2)}, u32[]{:S(2)}) collective-permute-start(f32[9,8,128]{2,1,0:T(8,128)S(1)} %get-tuple-element.27.rest_0_), channel_id=1, source_target_pairs={{0,1},{1,0},{2,3},{3,2},{4,5},{5,4},{6,7},{7,6},{8,9},{9,8},{10,11... | collective-permute-start | bytes 110600 | tf_op jit(solution)/shard_map/ppermute | solution.py:693
  22.2 10.1 %collective-permute-start.5 = (f32[12,8,128]{2,1,0:T(8,128)S(1)}, f32[12,8,128]{2,1,0:T(8,128)S(1)}, u32[]{:S(2)}, u32[]{:S(2)}) collective-permute-start(f32[12,8,128]{2,1,0:T(8,128)S(1)} %shard_map.89.rest_4_.rest_0_.rest_2_), channel_id=1, source_target_pairs={{0,12},{4,8},{8,4},{12,0},{1,13},{5,9},{9,5},{13,1},{2,14},{6,10},... | collective-permute-start | bytes 147464 | tf_op jit(solution)/shard_map/ppermute | solution.py:693
  26.3 6.0 %collective-permute-start.4 = (f32[12,8,128]{2,1,0:T(8,128)S(1)}, f32[12,8,128]{2,1,0:T(8,128)S(1)}, u32[]{:S(2)}, u32[]{:S(2)}) collective-permute-start(f32[12,8,128]{2,1,0:T(8,128)S(1)} %shard_map.89.rest_4_.rest_0_.rest_2_), channel_id=1, source_target_pairs={{0,8},{4,12},{8,0},{12,4},{1,9},{5,13},{9,1},{13,5},{2,10},{6,14},... | collective-permute-start | bytes 147464 | tf_op jit(solution)/shard_map/ppermute | solution.py:693
  26.3 6.0 %collective-permute-start.3 = (f32[12,8,128]{2,1,0:T(8,128)S(1)}, f32[12,8,128]{2,1,0:T(8,128)S(1)}, u32[]{:S(2)}, u32[]{:S(2)}) collective-permute-start(f32[12,8,128]{2,1,0:T(8,128)S(1)} %shard_map.89.rest_4_.rest_0_.rest_2_), channel_id=1, source_target_pairs={{0,4},{4,0},{8,12},{12,8},{1,5},{5,1},{9,13},{13,9},{2,6},{6,2},{1... | collective-permute-start | bytes 147464 | tf_op jit(solution)/shard_map/ppermute | solution.py:693
  41.7 8.1 %collective-permute-start.8 = (f32[5,8,128]{2,1,0:T(8,128)S(1)}, f32[5,8,128]{2,1,0:T(8,128)S(1)}, u32[]{:S(2)}, u32[]{:S(2)}) collective-permute-start(f32[5,8,128]{2,1,0:T(8,128)S(1)} %get-tuple-element.33.rest_0_.rest_2_), channel_id=1, source_target_pairs={{0,3},{1,2},{2,1},{3,0},{4,7},{5,6},{6,5},{7,4},{8,11},{9,10},{10,... | collective-permute-start | bytes 61448 | tf_op jit(solution)/shard_map/ppermute | solution.py:693
  43.7 6.1 %collective-permute-start.7 = (f32[5,8,128]{2,1,0:T(8,128)S(1)}, f32[5,8,128]{2,1,0:T(8,128)S(1)}, u32[]{:S(2)}, u32[]{:S(2)}) collective-permute-start(f32[5,8,128]{2,1,0:T(8,128)S(1)} %get-tuple-element.33.rest_0_.rest_2_), channel_id=1, source_target_pairs={{0,2},{1,3},{2,0},{3,1},{4,6},{5,7},{6,4},{7,5},{8,10},{9,11},{10,... | collective-permute-start | bytes 61448 | tf_op jit(solution)/shard_map/ppermute | solution.py:693
  45.4 4.4 %collective-permute-start.6 = (f32[5,8,128]{2,1,0:T(8,128)S(1)}, f32[5,8,128]{2,1,0:T(8,128)S(1)}, u32[]{:S(2)}, u32[]{:S(2)}) collective-permute-start(f32[5,8,128]{2,1,0:T(8,128)S(1)} %get-tuple-element.33.rest_0_.rest_2_), channel_id=1, source_target_pairs={{0,1},{1,0},{2,3},{3,2},{4,5},{5,4},{6,7},{7,6},{8,9},{9,8},{10,11... | collective-permute-start | bytes 61448 | tf_op jit(solution)/shard_map/ppermute | solution.py:693
  49.8 7.8 %collective-permute-start.11 = (f32[8,8,128]{2,1,0:T(8,128)S(1)}, f32[8,8,128]{2,1,0:T(8,128)S(1)}, u32[]{:S(2)}, u32[]{:S(2)}) collective-permute-start(f32[8,8,128]{2,1,0:T(8,128)S(1)} %shard_map.95.rest_0_.rest_6_), channel_id=1, source_target_pairs={{0,12},{4,8},{8,4},{12,0},{1,13},{5,9},{9,5},{13,1},{2,14},{6,10},... | collective-permute-start | bytes 98312 | tf_op jit(solution)/shard_map/ppermute | solution.py:693
  52.1 5.5 %collective-permute-start.10 = (f32[8,8,128]{2,1,0:T(8,128)S(1)}, f32[8,8,128]{2,1,0:T(8,128)S(1)}, u32[]{:S(2)}, u32[]{:S(2)}) collective-permute-start(f32[8,8,128]{2,1,0:T(8,128)S(1)} %shard_map.95.rest_0_.rest_6_), channel_id=1, source_target_pairs={{0,8},{4,12},{8,0},{12,4},{1,9},{5,13},{9,1},{13,5},{2,10},{6,14},... | collective-permute-start | bytes 98312 | tf_op jit(solution)/shard_map/ppermute | solution.py:693
  52.1 5.5 %collective-permute-start.9 = (f32[8,8,128]{2,1,0:T(8,128)S(1)}, f32[8,8,128]{2,1,0:T(8,128)S(1)}, u32[]{:S(2)}, u32[]{:S(2)}) collective-permute-start(f32[8,8,128]{2,1,0:T(8,128)S(1)} %shard_map.95.rest_0_.rest_6_), channel_id=1, source_target_pairs={{0,4},{4,0},{8,12},{12,8},{1,5},{5,1},{9,13},{13,9},{2,6},{6,2},{1... | collective-permute-start | bytes 98312 | tf_op jit(solution)/shard_map/ppermute | solution.py:693
  64.1 7.2 %collective-permute-start.14 = (f32[5,8,128]{2,1,0:T(8,128)S(1)}, f32[5,8,128]{2,1,0:T(8,128)S(1)}, u32[]{:S(2)}, u32[]{:S(2)}) collective-permute-start(f32[5,8,128]{2,1,0:T(8,128)S(1)} %get-tuple-element.35.rest_0_.rest_2_), channel_id=1, source_target_pairs={{0,3},{1,2},{2,1},{3,0},{4,7},{5,6},{6,5},{7,4},{8,11},{9,10},{10,... | collective-permute-start | bytes 61448 | tf_op jit(solution)/shard_map/ppermute | solution.py:693
  65.0 6.3 %collective-permute-start.13 = (f32[5,8,128]{2,1,0:T(8,128)S(1)}, f32[5,8,128]{2,1,0:T(8,128)S(1)}, u32[]{:S(2)}, u32[]{:S(2)}) collective-permute-start(f32[5,8,128]{2,1,0:T(8,128)S(1)} %get-tuple-element.35.rest_0_.rest_2_), channel_id=1, source_target_pairs={{0,2},{1,3},{2,0},{3,1},{4,6},{5,7},{6,4},{7,5},{8,10},{9,11},{10,... | collective-permute-start | bytes 61448 | tf_op jit(solution)/shard_map/ppermute | solution.py:693
  66.7 4.5 %collective-permute-start.12 = (f32[5,8,128]{2,1,0:T(8,128)S(1)}, f32[5,8,128]{2,1,0:T(8,128)S(1)}, u32[]{:S(2)}, u32[]{:S(2)}) collective-permute-start(f32[5,8,128]{2,1,0:T(8,128)S(1)} %get-tuple-element.35.rest_0_.rest_2_), channel_id=1, source_target_pairs={{0,1},{1,0},{2,3},{3,2},{4,5},{5,4},{6,7},{7,6},{8,9},{9,8},{10,11... | collective-permute-start | bytes 61448 | tf_op jit(solution)/shard_map/ppermute | solution.py:693
  71.3 7.8 %collective-permute-start.17 = (f32[8,8,128]{2,1,0:T(8,128)S(1)}, f32[8,8,128]{2,1,0:T(8,128)S(1)}, u32[]{:S(2)}, u32[]{:S(2)}) collective-permute-start(f32[8,8,128]{2,1,0:T(8,128)S(1)} %shard_map.99.rest_0_.rest_6_), channel_id=1, source_target_pairs={{0,12},{4,8},{8,4},{12,0},{1,13},{5,9},{9,5},{13,1},{2,14},{6,10},... | collective-permute-start | bytes 98312 | tf_op jit(solution)/shard_map/ppermute | solution.py:693
  73.1 6.0 %collective-permute-start.16 = (f32[8,8,128]{2,1,0:T(8,128)S(1)}, f32[8,8,128]{2,1,0:T(8,128)S(1)}, u32[]{:S(2)}, u32[]{:S(2)}) collective-permute-start(f32[8,8,128]{2,1,0:T(8,128)S(1)} %shard_map.99.rest_0_.rest_6_), channel_id=1, source_target_pairs={{0,8},{4,12},{8,0},{12,4},{1,9},{5,13},{9,1},{13,5},{2,10},{6,14},... | collective-permute-start | bytes 98312 | tf_op jit(solution)/shard_map/ppermute | solution.py:693
  73.1 6.0 %collective-permute-start.15 = (f32[8,8,128]{2,1,0:T(8,128)S(1)}, f32[8,8,128]{2,1,0:T(8,128)S(1)}, u32[]{:S(2)}, u32[]{:S(2)}) collective-permute-start(f32[8,8,128]{2,1,0:T(8,128)S(1)} %shard_map.99.rest_0_.rest_6_), channel_id=1, source_target_pairs={{0,4},{4,0},{8,12},{12,8},{1,5},{5,1},{9,13},{13,9},{2,6},{6,2},{1... | collective-permute-start | bytes 98312 | tf_op jit(solution)/shard_map/ppermute | solution.py:693
  85.2 3.1 %collective-permute-start.20 = (f32[8,128]{1,0:T(8,128)S(1)}, f32[8,128]{1,0:T(8,128)S(1)}, u32[]{:S(2)}, u32[]{:S(2)}) collective-permute-start(f32[8,128]{1,0:T(8,128)S(1)} %get-tuple-element.39.scal), channel_id=1, source_target_pairs={{0,3},{1,2},{2,1},{3,0},{4,7},{5,6},{6,5},{7,4},{8,11},{9,10},{10,... | collective-permute-start | bytes 12296 | tf_op jit(solution)/shard_map/ppermute | solution.py:693
  86.1 3.6 %collective-permute-start.19 = (f32[8,128]{1,0:T(8,128)S(1)}, f32[8,128]{1,0:T(8,128)S(1)}, u32[]{:S(2)}, u32[]{:S(2)}) collective-permute-start(f32[8,128]{1,0:T(8,128)S(1)} %get-tuple-element.39.scal), channel_id=1, source_target_pairs={{0,2},{1,3},{2,0},{3,1},{4,6},{5,7},{6,4},{7,5},{8,10},{9,11},{10,... | collective-permute-start | bytes 12296 | tf_op jit(solution)/shard_map/ppermute | solution.py:693
  87.8 1.9 %collective-permute-start.18 = (f32[8,128]{1,0:T(8,128)S(1)}, f32[8,128]{1,0:T(8,128)S(1)}, u32[]{:S(2)}, u32[]{:S(2)}) collective-permute-start(f32[8,128]{1,0:T(8,128)S(1)} %get-tuple-element.39.scal), channel_id=1, source_target_pairs={{0,1},{1,0},{2,3},{3,2},{4,5},{5,4},{6,7},{7,6},{8,9},{9,8},{10,11... | collective-permute-start | bytes 12296 | tf_op jit(solution)/shard_map/ppermute | solution.py:693
  89.7 5.5 %collective-permute-start.23 = (f32[8,128]{1,0:T(8,128)S(1)}, f32[8,128]{1,0:T(8,128)S(1)}, u32[]{:S(2)}, u32[]{:S(2)}) collective-permute-start(f32[8,128]{1,0:T(8,128)S(1)} %add_add_fusion.rest_0_), channel_id=1, source_target_pairs={{0,12},{4,8},{8,4},{12,0},{1,13},{5,9},{9,5},{13,1},{2,14},{6,10},... | collective-permute-start | bytes 12296 | tf_op jit(solution)/shard_map/ppermute | solution.py:693
  91.2 4.5 %collective-permute-start.22 = (f32[8,128]{1,0:T(8,128)S(1)}, f32[8,128]{1,0:T(8,128)S(1)}, u32[]{:S(2)}, u32[]{:S(2)}) collective-permute-start(f32[8,128]{1,0:T(8,128)S(1)} %add_add_fusion.rest_0_), channel_id=1, source_target_pairs={{0,8},{4,12},{8,0},{12,4},{1,9},{5,13},{9,1},{13,5},{2,10},{6,14},... | collective-permute-start | bytes 12296 | tf_op jit(solution)/shard_map/ppermute | solution.py:693
  91.2 4.5 %collective-permute-start.21 = (f32[8,128]{1,0:T(8,128)S(1)}, f32[8,128]{1,0:T(8,128)S(1)}, u32[]{:S(2)}, u32[]{:S(2)}) collective-permute-start(f32[8,128]{1,0:T(8,128)S(1)} %add_add_fusion.rest_0_), channel_id=1, source_target_pairs={{0,4},{4,0},{8,12},{12,8},{1,5},{5,1},{9,13},{13,9},{2,6},{6,2},{1... | collective-permute-start | bytes 12296 | tf_op jit(solution)/shard_map/ppermute | solution.py:693
  (1 other events, 9.2 us)

commit v5 on v4

--- a/solution.py
+++ b/solution.py
@@ -58,11 +58,11 @@
     live = index < count**3
     safe = np.where(live, index, 0)
     levels = np.stack([safe // (count * count), safe // count % count, safe % count])
-    picks = np.zeros((3, NODE_PAD, count, 8))
+    picks = np.zeros((3, NODE_PAD, 6, 8))
     for d in range(3):
         picks[d, index, levels[d], d] = 1.0
     picks[0] *= live[:, None, None]
-    picks = picks.reshape(3 * NODE_PAD, count * 8)
+    picks = np.tile(picks.reshape(3 * NODE_PAD, 48), (1, 3))
     nodes = np.zeros((8, NODE_PAD))
     nodes[0] = 0.5 * (1.0 + roots[levels[0]])
     nodes[1] = 0.5 * (1.0 + roots[levels[1]])
@@ -120,7 +120,7 @@
         decay = jnp.exp(-s)
         small = s * (1.0 - s * (0.5 - s * (1.0 / 6.0 - s * (1.0 / 24.0))))
         three = jnp.where(s < 0.015625, small, 1.0 - decay)
-        five = (three - s * decay) * (3.0 * inv_two * inv_three)
+        five = ((three - s * decay) * inv_three) * (3.0 * inv_two)
         for k, value in enumerate(tensor(five, three * inv_three, dx, dy, dz)):
             put(k, at, value)
 
@@ -238,12 +238,16 @@
         for n in range(2, ORDER):
             value = value + float(coeff[k, n]) * terms[n]
         levels.append(value)
-    levels = jnp.concatenate(levels, axis=0)
+    levels = jnp.concatenate(levels + [jnp.zeros((8, total), f32)] * (6 - ORDER), axis=0)
+    pieces = []
+    for k in range(3):
+        pieces.append(levels.astype(jnp.bfloat16))
+        levels = levels - pieces[-1].astype(f32)
+    levels = jnp.concatenate(pieces, axis=0)
+    chosen = picks[...].astype(jnp.bfloat16)
     wide = 4 * BLOCK
     for begin in range(0, total, wide):
-        value = jnp.dot(
-            picks[...], levels[:, begin : begin + wide], precision=highest, preferred_element_type=f32
-        )
+        value = jnp.dot(chosen, levels[:, begin : begin + wide], preferred_element_type=f32)
         value = value[:BLOCK] * value[BLOCK : 2 * BLOCK] * value[2 * BLOCK :]
         for t in range(4):
             phi[begin // BLOCK + t] = value[:, t * BLOCK : (t + 1) * BLOCK]
@@ -485,16 +489,18 @@
                 return tuple(a + n for a, n in zip(acc, new))
 
             acc = visit(2, acc)
-            acc = lax.fori_loop(3, boxes - 1, visit, acc, unroll=7)
+            acc = lax.fori_loop(3, boxes - 1, visit, acc, unroll=14)
             for box in range(BOXES_DEV):
-                for half in range(1):
-                    for c in range(3):
-                        fcol[box, c, ats[half], :] = jnp.broadcast_to(
-                            jnp.sum(acc[box * 3 + half * 3 + c], axis=1, keepdims=True), (SUB, BLOCK)
-                        )
+                for c in range(3):
+                    fcol[box, c, ats[0], :] = acc[box * 3 + c]
             return unused
 
         lax.fori_loop(0, BLOCK // SUB, rows, 0)
+        for box in range(BOXES_DEV):
+            for c in range(3):
+                fcol[box, c] = jnp.broadcast_to(
+                    jnp.sum(fcol[box, c], axis=1, keepdims=True), (BLOCK, BLOCK)
+                )
         return
     for box in range(BOXES_DEV):
         for c in range(3):

time: 96.6 us -> 92.2 us (0.954)
  Pallas kernels: 61.7 us -> 57.1 us
  waiting for transfers between devices: 3.45 us -> 6.41 us
  starting transfers between devices: 30.4 us -> 27.8 us
    pallas_call x17, Pallas kernels: 61.7 us -> 57.1 us  [call(): pl.pallas_call(body, out_shape=shapes, in_specs=[SM] * smem + [FAR] * far...]
    ppermute x24, waiting for transfers between devices: 3.45 us -> 6.41 us  [swap(): got.append(lax.ppermute(x, axes, [(i, i ^ s) for i in range(count)]))]
    ppermute x24, starting transfers between devices: 30.4 us -> 27.8 us  [swap(): got.append(lax.ppermute(x, axes, [(i, i ^ s) for i in range(count)]))]
  transfers between devices with their start and end apart: 24 -> 24, of which waited for: 5 -> 6; matrix products, arithmetic and copies ran while one was open for 0% -> 0% of each run, Pallas kernels for 36% -> 39%
where the time goes in v5:
time: 92.2 us
  Pallas kernels  57.1 us (62%)
  starting transfers between devices  27.8 us (30%)
  waiting for transfers between devices  6.41 us (7%)
    pallas_call x17, Pallas kernels, call(): pl.pallas_call(body, out_shape=shapes, in_specs=[SM] * smem + [FAR] * far...  57.1 us
    ppermute x24, starting transfers between devices, swap(): got.append(lax.ppermute(x, axes, [(i, i ^ s) for i in range(count)]))  27.8 us
    ppermute x24, waiting for transfers between devices, swap(): got.append(lax.ppermute(x, axes, [(i, i ^ s) for i in range(count)]))  6.41 us
  transfers between devices with their start and end apart: 24, of which 6 were waited for; matrix products, arithmetic and copies ran while one was open for 0% of the time, Pallas kernels for 39%

profile of v5, /device:TPU:0, one launch (start us, length us, event | category | flops | bytes accessed | tf_op | source)
XLA Modules:
  0.0 92.2 jit_solution(2169224228679158572)
XLA Ops:
  0.6 1.9 %shard_map.86 = (f32[16,8,128]{2,1,0:T(8,128)S(1)}, f32[16,8,128]{2,1,0:T(8,128)S(1)}, f32[16,128,128]{2,1,0:T(8,128)S(1)}, f32[9,8,128]{2,1,0:T(8,128)S(1)}) custom-call(s32[1]{0:T(128)} %bitcast.meta, f32[3,2048]{1,0:T(4,128)} %pos_in.1, f32[1,2048]{1,0:T(1,128)} %bitcast.3, f32[3,2048]{1,0:T(4,128)} %field_in.1, s32[1,2048]{1,0:T(1,128)} %bitcast.4, ...), custom_call_target="tpu_custom_call" | custom-call | tf_op jit(solution)/shard_map/pallas_call | solution.py:38
  2.5 2.4 %collective-permute-start.2 = (f32[9,8,128]{2,1,0:T(8,128)S(1)}, f32[9,8,128]{2,1,0:T(8,128)S(1)}, u32[]{:S(2)}, u32[]{:S(2)}) collective-permute-start(f32[9,8,128]{2,1,0:T(8,128)S(1)} %get-tuple-element.27.rest_0_), channel_id=1, source_target_pairs={{0,3},{1,2},{2,1},{3,0},{4,7},{5,6},{6,5},{7,4},{8,11},{9,10},{10,... | collective-permute-start | bytes 110600 | tf_op jit(solution)/shard_map/ppermute | solution.py:699
  5.7 10.6 %shard_map.87 = (f32[70,4,128,128]{3,2,1,0:T(8,128)S(1)}, s32[56]{0:T(128)S(1)}, s32[21]{0:T(128)S(1)}) custom-call(s32[16,9]{1,0:T(8,128)} %mask_in.1, f32[16,8,128]{2,1,0:T(8,128)S(1)} %get-tuple-element.23.stat), custom_call_target="tpu_custom_call" | custom-call | flops 80281600 | bytes 1048576 | tf_op jit(solution)/shard_map/pallas_call | solution.py:38
  16.2 4.3 %shard_map.88.rest_4_.rest_0_ = f32[12,8,128]{2,1,0:T(8,128)S(1)} custom-call(s32[56]{0:T(128)S(1)} %get-tuple-element.28.codes, f32[16,8,128]{2,1,0:T(8,128)S(1)} %get-tuple-element.25.v.rest_11_, f32[70,4,128,128]{3,2,1,0:T(8,128)S(1)} %get-tuple-element.29.tab), custom_call_target="tpu_custom_call" | custom-call | flops 21233664 | bytes 1048576 | tf_op jit(solution)/shard_map/pallas_call | solution.py:38
  20.6 4.4 %collective-permute-start.5 = (f32[12,8,128]{2,1,0:T(8,128)S(1)}, f32[12,8,128]{2,1,0:T(8,128)S(1)}, u32[]{:S(2)}, u32[]{:S(2)}) collective-permute-start(f32[12,8,128]{2,1,0:T(8,128)S(1)} %shard_map.89.rest_4_.rest_0_.rest_2_), channel_id=1, source_target_pairs={{0,12},{4,8},{8,4},{12,0},{1,13},{5,9},{9,5},{13,1},{2,14},{6,10},... | collective-permute-start | bytes 147464 | tf_op jit(solution)/shard_map/ppermute | solution.py:699
  25.7 2.1 %shard_map.92.rest_7_.rest_10_ = f32[16,31,4,8,128]{4,3,2,1,0:T(8,128)S(1)} custom-call(f32[8,128]{1,0:T(8,128)S(1)} %copy-done), custom_call_target="tpu_custom_call" | custom-call | flops 14680064 | bytes 1048576 | tf_op jit(solution)/shard_map/pallas_call | solution.py:38
  27.8 3.5 %shard_map.91.rest_1_ = f32[8,8,128]{2,1,0:T(8,128)S(1)} custom-call(s32[56]{0:T(128)S(1)} %get-tuple-element.28.codes, f32[16,8,128]{2,1,0:T(8,128)S(1)} %get-tuple-element.25.v.rest_11_, f32[70,4,128,128]{3,2,1,0:T(8,128)S(1)} %get-tuple-element.29.tab, f32[12,8,128]{2,1,0:T(8,128)S(1)} %shard_map.89.rest_4_.rest_0_.rest_2_), custom_call_target="tpu_custom_call" | custom-call | flops 21233664 | bytes 1048576 | tf_op jit(solution)/shard_map/pallas_call | solution.py:38
  31.2 3.2 %shard_map.90 = (f32[20,4,128,128]{3,2,1,0:T(8,128)S(1)}, f32[8,8,128]{2,1,0:T(8,128)S(1)}) custom-call(s32[1]{0:T(128)} %bitcast.meta, s32[21]{0:T(128)S(1)} %get-tuple-element.24.codes, f32[16,8,128]{2,1,0:T(8,128)S(1)} %get-tuple-element.23.stat, f32[9,8,128]{2,1,0:T(8,128)S(1)} %get-tuple-element.27.rest_0_, ...), custom_call_target="tpu_custom_call" | custom-call | tf_op jit(solution)/shard_map/pallas_call | solution.py:38
  34.5 5.1 %shard_map.93 = (f32[16,8,128]{2,1,0:T(8,128)S(1)}, f32[16,8,128]{2,1,0:T(8,128)S(1)}, f32[5,8,128]{2,1,0:T(8,128)S(1)}) custom-call(s32[1]{0:T(128)} %bitcast.meta, s32[21]{0:T(128)S(1)} %get-tuple-element.24.codes, f32[8,128]{1,0:T(8,128)S(1)} %copy-done, f32[16,8,128]{2,1,0:T(8,128)S(1)} %get-tuple-element.23.stat, ...), custom_call_target="tpu_custom_call" | custom-call | tf_op jit(solution)/shard_map/pallas_call | solution.py:38
  41.6 4.3 %shard_map.94.rest_4_.rest_0_ = f32[12,8,128]{2,1,0:T(8,128)S(1)} custom-call(s32[56]{0:T(128)S(1)} %get-tuple-element.28.codes, f32[16,8,128]{2,1,0:T(8,128)S(1)} %get-tuple-element.32.v, f32[70,4,128,128]{3,2,1,0:T(8,128)S(1)} %get-tuple-element.29.tab), custom_call_target="tpu_custom_call" | custom-call | flops 21233664 | bytes 1048576 | tf_op jit(solution)/shard_map/pallas_call | solution.py:38
  45.9 4.3 %collective-permute-start.11 = (f32[8,8,128]{2,1,0:T(8,128)S(1)}, f32[8,8,128]{2,1,0:T(8,128)S(1)}, u32[]{:S(2)}, u32[]{:S(2)}) collective-permute-start(f32[8,8,128]{2,1,0:T(8,128)S(1)} %shard_map.95.rest_0_.rest_6_), channel_id=1, source_target_pairs={{0,12},{4,8},{8,4},{12,0},{1,13},{5,9},{9,5},{13,1},{2,14},{6,10},... | collective-permute-start | bytes 98312 | tf_op jit(solution)/shard_map/ppermute | solution.py:699
  50.9 3.5 %shard_map.96.rest_1_ = f32[8,8,128]{2,1,0:T(8,128)S(1)} custom-call(s32[56]{0:T(128)S(1)} %get-tuple-element.28.codes, f32[16,8,128]{2,1,0:T(8,128)S(1)} %get-tuple-element.32.v, f32[70,4,128,128]{3,2,1,0:T(8,128)S(1)} %get-tuple-element.29.tab, f32[8,8,128]{2,1,0:T(8,128)S(1)} %shard_map.95.rest_0_.rest_6_), custom_call_target="tpu_custom_call" | custom-call | flops 21233664 | bytes 1048576 | tf_op jit(solution)/shard_map/pallas_call | solution.py:38
  55.0 5.2 %shard_map.97 = (f32[16,8,128]{2,1,0:T(8,128)S(1)}, f32[16,8,128]{2,1,0:T(8,128)S(1)}, f32[5,8,128]{2,1,0:T(8,128)S(1)}, f32[8,128]{1,0:T(8,128)S(1)}) custom-call(s32[1]{0:T(128)} %bitcast.meta, s32[21]{0:T(128)S(1)} %get-tuple-element.24.codes, f32[8,128]{1,0:T(8,128)S(1)} %copy-done, f32[16,8,128]{2,1,0:T(8,128)S(1)} %get-tuple-element.23.stat, ...), custom_call_target="tpu_custom_call" | custom-call | tf_op jit(solution)/shard_map/pallas_call | solution.py:38
  60.9 1.4 %collective-permute-start.12 = (f32[5,8,128]{2,1,0:T(8,128)S(1)}, f32[5,8,128]{2,1,0:T(8,128)S(1)}, u32[]{:S(2)}, u32[]{:S(2)}) collective-permute-start(f32[5,8,128]{2,1,0:T(8,128)S(1)} %get-tuple-element.35.rest_0_.rest_2_), channel_id=1, source_target_pairs={{0,1},{1,0},{2,3},{3,2},{4,5},{5,4},{6,7},{7,6},{8,9},{9,8},{10,11... | collective-permute-start | bytes 61448 | tf_op jit(solution)/shard_map/ppermute | solution.py:699
  62.2 4.3 %shard_map.98.rest_4_.rest_0_ = f32[12,8,128]{2,1,0:T(8,128)S(1)} custom-call(s32[56]{0:T(128)S(1)} %get-tuple-element.28.codes, f32[16,8,128]{2,1,0:T(8,128)S(1)} %get-tuple-element.34.v, f32[70,4,128,128]{3,2,1,0:T(8,128)S(1)} %get-tuple-element.29.tab), custom_call_target="tpu_custom_call" | custom-call | flops 21233664 | bytes 1048576 | tf_op jit(solution)/shard_map/pallas_call | solution.py:38
  66.6 3.5 %collective-permute-start.17 = (f32[8,8,128]{2,1,0:T(8,128)S(1)}, f32[8,8,128]{2,1,0:T(8,128)S(1)}, u32[]{:S(2)}, u32[]{:S(2)}) collective-permute-start(f32[8,8,128]{2,1,0:T(8,128)S(1)} %shard_map.99.rest_0_.rest_6_), channel_id=1, source_target_pairs={{0,12},{4,8},{8,4},{12,0},{1,13},{5,9},{9,5},{13,1},{2,14},{6,10},... | collective-permute-start | bytes 98312 | tf_op jit(solution)/shard_map/ppermute | solution.py:699
  71.0 3.5 %shard_map.100.rest_1_ = f32[8,8,128]{2,1,0:T(8,128)S(1)} custom-call(s32[56]{0:T(128)S(1)} %get-tuple-element.28.codes, f32[16,8,128]{2,1,0:T(8,128)S(1)} %get-tuple-element.34.v, f32[70,4,128,128]{3,2,1,0:T(8,128)S(1)} %get-tuple-element.29.tab, f32[8,8,128]{2,1,0:T(8,128)S(1)} %shard_map.99.rest_0_.rest_6_), custom_call_target="tpu_custom_call" | custom-call | flops 21233664 | bytes 1048576 | tf_op jit(solution)/shard_map/pallas_call | solution.py:38
  74.9 4.9 %shard_map.101 = (f32[16,8,128]{2,1,0:T(8,128)S(1)}, f32[16,8,128]{2,1,0:T(8,128)S(1)}, f32[16,8,128]{2,1,0:T(8,128)S(1)}, f32[16,8,128]{2,1,0:T(8,128)S(1)}, f32[8,128]{1,0:T(8,128)S(1)}) custom-call(s32[1]{0:T(128)} %bitcast.meta, s32[21]{0:T(128)S(1)} %get-tuple-element.24.codes, f32[8,128]{1,0:T(8,128)S(1)} %copy-done, ...), custom_call_target="tpu_custom_call" | custom-call | tf_op jit(solution)/shard_map/pallas_call | solution.py:38
  80.3 1.4 %collective-permute-start.18 = (f32[8,128]{1,0:T(8,128)S(1)}, f32[8,128]{1,0:T(8,128)S(1)}, u32[]{:S(2)}, u32[]{:S(2)}) collective-permute-start(f32[8,128]{1,0:T(8,128)S(1)} %get-tuple-element.39.scal), channel_id=1, source_target_pairs={{0,1},{1,0},{2,3},{3,2},{4,5},{5,4},{6,7},{7,6},{8,9},{9,8},{10,11... | collective-permute-start | bytes 12296 | tf_op jit(solution)/shard_map/ppermute | solution.py:699
  81.7 1.2 %collective-permute-done.20 = f32[8,128]{1,0:T(8,128)S(1)} collective-permute-done((f32[8,128]{1,0:T(8,128)S(1)}, f32[8,128]{1,0:T(8,128)S(1)}, u32[]{:S(2)}, u32[]{:S(2)}) %collective-permute-start.20) | collective-permute-done | bytes 4128 | tf_op jit(solution)/shard_map/ppermute | solution.py:699
  83.5 3.4 %collective-permute-start.23 = (f32[8,128]{1,0:T(8,128)S(1)}, f32[8,128]{1,0:T(8,128)S(1)}, u32[]{:S(2)}, u32[]{:S(2)}) collective-permute-start(f32[8,128]{1,0:T(8,128)S(1)} %add_add_fusion.rest_0_), channel_id=1, source_target_pairs={{0,12},{4,8},{8,4},{12,0},{1,13},{5,9},{9,5},{13,1},{2,14},{6,10},... | collective-permute-start | bytes 12296 | tf_op jit(solution)/shard_map/ppermute | solution.py:699
  86.9 1.0 %collective-permute-start.21 = (f32[8,128]{1,0:T(8,128)S(1)}, f32[8,128]{1,0:T(8,128)S(1)}, u32[]{:S(2)}, u32[]{:S(2)}) collective-permute-start(f32[8,128]{1,0:T(8,128)S(1)} %add_add_fusion.rest_0_), channel_id=1, source_target_pairs={{0,4},{4,0},{8,12},{12,8},{1,5},{5,1},{9,13},{13,9},{2,6},{6,2},{1... | collective-permute-start | bytes 12296 | tf_op jit(solution)/shard_map/ppermute | solution.py:699
  88.0 1.0 %collective-permute-done.23.rest_3_ = f32[8,128]{1,0:T(8,128)S(1)} collective-permute-done((f32[8,128]{1,0:T(8,128)S(1)}, f32[8,128]{1,0:T(8,128)S(1)}, u32[]{:S(2)}, u32[]{:S(2)}) %collective-permute-start.23) | collective-permute-done | bytes 4128 | tf_op jit(solution)/shard_map/ppermute | solution.py:699
  89.0 2.4 %collective-permute-done.22.rest_2_ = f32[8,128]{1,0:T(8,128)S(1)} collective-permute-done((f32[8,128]{1,0:T(8,128)S(1)}, f32[8,128]{1,0:T(8,128)S(1)}, u32[]{:S(2)}, u32[]{:S(2)}) %collective-permute-start.22) | collective-permute-done | bytes 4128 | tf_op jit(solution)/shard_map/ppermute | solution.py:699
  (44 shorter events, 8.5 us)
Async XLA Ops:
  2.5 18.0 %collective-permute-start.2 = (f32[9,8,128]{2,1,0:T(8,128)S(1)}, f32[9,8,128]{2,1,0:T(8,128)S(1)}, u32[]{:S(2)}, u32[]{:S(2)}) collective-permute-start(f32[9,8,128]{2,1,0:T(8,128)S(1)} %get-tuple-element.27.rest_0_), channel_id=1, source_target_pairs={{0,3},{1,2},{2,1},{3,0},{4,7},{5,6},{6,5},{7,4},{8,11},{9,10},{10,... | collective-permute-start | bytes 110600 | tf_op jit(solution)/shard_map/ppermute | solution.py:699
  5.0 15.6 %collective-permute-start.1 = (f32[9,8,128]{2,1,0:T(8,128)S(1)}, f32[9,8,128]{2,1,0:T(8,128)S(1)}, u32[]{:S(2)}, u32[]{:S(2)}) collective-permute-start(f32[9,8,128]{2,1,0:T(8,128)S(1)} %get-tuple-element.27.rest_0_), channel_id=1, source_target_pairs={{0,2},{1,3},{2,0},{3,1},{4,6},{5,7},{6,4},{7,5},{8,10},{9,11},{10,... | collective-permute-start | bytes 110600 | tf_op jit(solution)/shard_map/ppermute | solution.py:699
  5.6 14.9 %collective-permute-start = (f32[9,8,128]{2,1,0:T(8,128)S(1)}, f32[9,8,128]{2,1,0:T(8,128)S(1)}, u32[]{:S(2)}, u32[]{:S(2)}) collective-permute-start(f32[9,8,128]{2,1,0:T(8,128)S(1)} %get-tuple-element.27.rest_0_), channel_id=1, source_target_pairs={{0,1},{1,0},{2,3},{3,2},{4,5},{5,4},{6,7},{7,6},{8,9},{9,8},{10,11... | collective-permute-start | bytes 110600 | tf_op jit(solution)/shard_map/ppermute | solution.py:699
  20.6 10.6 %collective-permute-start.5 = (f32[12,8,128]{2,1,0:T(8,128)S(1)}, f32[12,8,128]{2,1,0:T(8,128)S(1)}, u32[]{:S(2)}, u32[]{:S(2)}) collective-permute-start(f32[12,8,128]{2,1,0:T(8,128)S(1)} %shard_map.89.rest_4_.rest_0_.rest_2_), channel_id=1, source_target_pairs={{0,12},{4,8},{8,4},{12,0},{1,13},{5,9},{9,5},{13,1},{2,14},{6,10},... | collective-permute-start | bytes 147464 | tf_op jit(solution)/shard_map/ppermute | solution.py:699
  25.0 6.2 %collective-permute-start.4 = (f32[12,8,128]{2,1,0:T(8,128)S(1)}, f32[12,8,128]{2,1,0:T(8,128)S(1)}, u32[]{:S(2)}, u32[]{:S(2)}) collective-permute-start(f32[12,8,128]{2,1,0:T(8,128)S(1)} %shard_map.89.rest_4_.rest_0_.rest_2_), channel_id=1, source_target_pairs={{0,8},{4,12},{8,0},{12,4},{1,9},{5,13},{9,1},{13,5},{2,10},{6,14},... | collective-permute-start | bytes 147464 | tf_op jit(solution)/shard_map/ppermute | solution.py:699
  25.0 6.2 %collective-permute-start.3 = (f32[12,8,128]{2,1,0:T(8,128)S(1)}, f32[12,8,128]{2,1,0:T(8,128)S(1)}, u32[]{:S(2)}, u32[]{:S(2)}) collective-permute-start(f32[12,8,128]{2,1,0:T(8,128)S(1)} %shard_map.89.rest_4_.rest_0_.rest_2_), channel_id=1, source_target_pairs={{0,4},{4,0},{8,12},{12,8},{1,5},{5,1},{9,13},{13,9},{2,6},{6,2},{1... | collective-permute-start | bytes 147464 | tf_op jit(solution)/shard_map/ppermute | solution.py:699
  39.6 6.2 %collective-permute-start.8 = (f32[5,8,128]{2,1,0:T(8,128)S(1)}, f32[5,8,128]{2,1,0:T(8,128)S(1)}, u32[]{:S(2)}, u32[]{:S(2)}) collective-permute-start(f32[5,8,128]{2,1,0:T(8,128)S(1)} %get-tuple-element.33.rest_0_.rest_2_), channel_id=1, source_target_pairs={{0,3},{1,2},{2,1},{3,0},{4,7},{5,6},{6,5},{7,4},{8,11},{9,10},{10,... | collective-permute-start | bytes 61448 | tf_op jit(solution)/shard_map/ppermute | solution.py:699
  39.7 6.2 %collective-permute-start.7 = (f32[5,8,128]{2,1,0:T(8,128)S(1)}, f32[5,8,128]{2,1,0:T(8,128)S(1)}, u32[]{:S(2)}, u32[]{:S(2)}) collective-permute-start(f32[5,8,128]{2,1,0:T(8,128)S(1)} %get-tuple-element.33.rest_0_.rest_2_), channel_id=1, source_target_pairs={{0,2},{1,3},{2,0},{3,1},{4,6},{5,7},{6,4},{7,5},{8,10},{9,11},{10,... | collective-permute-start | bytes 61448 | tf_op jit(solution)/shard_map/ppermute | solution.py:699
  40.6 5.3 %collective-permute-start.6 = (f32[5,8,128]{2,1,0:T(8,128)S(1)}, f32[5,8,128]{2,1,0:T(8,128)S(1)}, u32[]{:S(2)}, u32[]{:S(2)}) collective-permute-start(f32[5,8,128]{2,1,0:T(8,128)S(1)} %get-tuple-element.33.rest_0_.rest_2_), channel_id=1, source_target_pairs={{0,1},{1,0},{2,3},{3,2},{4,5},{5,4},{6,7},{7,6},{8,9},{9,8},{10,11... | collective-permute-start | bytes 61448 | tf_op jit(solution)/shard_map/ppermute | solution.py:699
  45.9 8.4 %collective-permute-start.11 = (f32[8,8,128]{2,1,0:T(8,128)S(1)}, f32[8,8,128]{2,1,0:T(8,128)S(1)}, u32[]{:S(2)}, u32[]{:S(2)}) collective-permute-start(f32[8,8,128]{2,1,0:T(8,128)S(1)} %shard_map.95.rest_0_.rest_6_), channel_id=1, source_target_pairs={{0,12},{4,8},{8,4},{12,0},{1,13},{5,9},{9,5},{13,1},{2,14},{6,10},... | collective-permute-start | bytes 98312 | tf_op jit(solution)/shard_map/ppermute | solution.py:699
  50.2 4.8 %collective-permute-start.10 = (f32[8,8,128]{2,1,0:T(8,128)S(1)}, f32[8,8,128]{2,1,0:T(8,128)S(1)}, u32[]{:S(2)}, u32[]{:S(2)}) collective-permute-start(f32[8,8,128]{2,1,0:T(8,128)S(1)} %shard_map.95.rest_0_.rest_6_), channel_id=1, source_target_pairs={{0,8},{4,12},{8,0},{12,4},{1,9},{5,13},{9,1},{13,5},{2,10},{6,14},... | collective-permute-start | bytes 98312 | tf_op jit(solution)/shard_map/ppermute | solution.py:699
  50.2 4.8 %collective-permute-start.9 = (f32[8,8,128]{2,1,0:T(8,128)S(1)}, f32[8,8,128]{2,1,0:T(8,128)S(1)}, u32[]{:S(2)}, u32[]{:S(2)}) collective-permute-start(f32[8,8,128]{2,1,0:T(8,128)S(1)} %shard_map.95.rest_0_.rest_6_), channel_id=1, source_target_pairs={{0,4},{4,0},{8,12},{12,8},{1,5},{5,1},{9,13},{13,9},{2,6},{6,2},{1... | collective-permute-start | bytes 98312 | tf_op jit(solution)/shard_map/ppermute | solution.py:699
  60.3 6.2 %collective-permute-start.14 = (f32[5,8,128]{2,1,0:T(8,128)S(1)}, f32[5,8,128]{2,1,0:T(8,128)S(1)}, u32[]{:S(2)}, u32[]{:S(2)}) collective-permute-start(f32[5,8,128]{2,1,0:T(8,128)S(1)} %get-tuple-element.35.rest_0_.rest_2_), channel_id=1, source_target_pairs={{0,3},{1,2},{2,1},{3,0},{4,7},{5,6},{6,5},{7,4},{8,11},{9,10},{10,... | collective-permute-start | bytes 61448 | tf_op jit(solution)/shard_map/ppermute | solution.py:699
  60.4 6.2 %collective-permute-start.13 = (f32[5,8,128]{2,1,0:T(8,128)S(1)}, f32[5,8,128]{2,1,0:T(8,128)S(1)}, u32[]{:S(2)}, u32[]{:S(2)}) collective-permute-start(f32[5,8,128]{2,1,0:T(8,128)S(1)} %get-tuple-element.35.rest_0_.rest_2_), channel_id=1, source_target_pairs={{0,2},{1,3},{2,0},{3,1},{4,6},{5,7},{6,4},{7,5},{8,10},{9,11},{10,... | collective-permute-start | bytes 61448 | tf_op jit(solution)/shard_map/ppermute | solution.py:699
  60.9 5.7 %collective-permute-start.12 = (f32[5,8,128]{2,1,0:T(8,128)S(1)}, f32[5,8,128]{2,1,0:T(8,128)S(1)}, u32[]{:S(2)}, u32[]{:S(2)}) collective-permute-start(f32[5,8,128]{2,1,0:T(8,128)S(1)} %get-tuple-element.35.rest_0_.rest_2_), channel_id=1, source_target_pairs={{0,1},{1,0},{2,3},{3,2},{4,5},{5,4},{6,7},{7,6},{8,9},{9,8},{10,11... | collective-permute-start | bytes 61448 | tf_op jit(solution)/shard_map/ppermute | solution.py:699
  66.6 7.9 %collective-permute-start.17 = (f32[8,8,128]{2,1,0:T(8,128)S(1)}, f32[8,8,128]{2,1,0:T(8,128)S(1)}, u32[]{:S(2)}, u32[]{:S(2)}) collective-permute-start(f32[8,8,128]{2,1,0:T(8,128)S(1)} %shard_map.99.rest_0_.rest_6_), channel_id=1, source_target_pairs={{0,12},{4,8},{8,4},{12,0},{1,13},{5,9},{9,5},{13,1},{2,14},{6,10},... | collective-permute-start | bytes 98312 | tf_op jit(solution)/shard_map/ppermute | solution.py:699
  70.1 4.8 %collective-permute-start.16 = (f32[8,8,128]{2,1,0:T(8,128)S(1)}, f32[8,8,128]{2,1,0:T(8,128)S(1)}, u32[]{:S(2)}, u32[]{:S(2)}) collective-permute-start(f32[8,8,128]{2,1,0:T(8,128)S(1)} %shard_map.99.rest_0_.rest_6_), channel_id=1, source_target_pairs={{0,8},{4,12},{8,0},{12,4},{1,9},{5,13},{9,1},{13,5},{2,10},{6,14},... | collective-permute-start | bytes 98312 | tf_op jit(solution)/shard_map/ppermute | solution.py:699
  70.1 4.8 %collective-permute-start.15 = (f32[8,8,128]{2,1,0:T(8,128)S(1)}, f32[8,8,128]{2,1,0:T(8,128)S(1)}, u32[]{:S(2)}, u32[]{:S(2)}) collective-permute-start(f32[8,8,128]{2,1,0:T(8,128)S(1)} %shard_map.99.rest_0_.rest_6_), channel_id=1, source_target_pairs={{0,4},{4,0},{8,12},{12,8},{1,5},{5,1},{9,13},{13,9},{2,6},{6,2},{1... | collective-permute-start | bytes 98312 | tf_op jit(solution)/shard_map/ppermute | solution.py:699
  79.8 3.1 %collective-permute-start.20 = (f32[8,128]{1,0:T(8,128)S(1)}, f32[8,128]{1,0:T(8,128)S(1)}, u32[]{:S(2)}, u32[]{:S(2)}) collective-permute-start(f32[8,128]{1,0:T(8,128)S(1)} %get-tuple-element.39.scal), channel_id=1, source_target_pairs={{0,3},{1,2},{2,1},{3,0},{4,7},{5,6},{6,5},{7,4},{8,11},{9,10},{10,... | collective-permute-start | bytes 12296 | tf_op jit(solution)/shard_map/ppermute | solution.py:699
  79.8 3.7 %collective-permute-start.19 = (f32[8,128]{1,0:T(8,128)S(1)}, f32[8,128]{1,0:T(8,128)S(1)}, u32[]{:S(2)}, u32[]{:S(2)}) collective-permute-start(f32[8,128]{1,0:T(8,128)S(1)} %get-tuple-element.39.scal), channel_id=1, source_target_pairs={{0,2},{1,3},{2,0},{3,1},{4,6},{5,7},{6,4},{7,5},{8,10},{9,11},{10,... | collective-permute-start | bytes 12296 | tf_op jit(solution)/shard_map/ppermute | solution.py:699
  80.3 3.2 %collective-permute-start.18 = (f32[8,128]{1,0:T(8,128)S(1)}, f32[8,128]{1,0:T(8,128)S(1)}, u32[]{:S(2)}, u32[]{:S(2)}) collective-permute-start(f32[8,128]{1,0:T(8,128)S(1)} %get-tuple-element.39.scal), channel_id=1, source_target_pairs={{0,1},{1,0},{2,3},{3,2},{4,5},{5,4},{6,7},{7,6},{8,9},{9,8},{10,11... | collective-permute-start | bytes 12296 | tf_op jit(solution)/shard_map/ppermute | solution.py:699
  83.5 5.5 %collective-permute-start.23 = (f32[8,128]{1,0:T(8,128)S(1)}, f32[8,128]{1,0:T(8,128)S(1)}, u32[]{:S(2)}, u32[]{:S(2)}) collective-permute-start(f32[8,128]{1,0:T(8,128)S(1)} %add_add_fusion.rest_0_), channel_id=1, source_target_pairs={{0,12},{4,8},{8,4},{12,0},{1,13},{5,9},{9,5},{13,1},{2,14},{6,10},... | collective-permute-start | bytes 12296 | tf_op jit(solution)/shard_map/ppermute | solution.py:699
  86.9 4.5 %collective-permute-start.22 = (f32[8,128]{1,0:T(8,128)S(1)}, f32[8,128]{1,0:T(8,128)S(1)}, u32[]{:S(2)}, u32[]{:S(2)}) collective-permute-start(f32[8,128]{1,0:T(8,128)S(1)} %add_add_fusion.rest_0_), channel_id=1, source_target_pairs={{0,8},{4,12},{8,0},{12,4},{1,9},{5,13},{9,1},{13,5},{2,10},{6,14},... | collective-permute-start | bytes 12296 | tf_op jit(solution)/shard_map/ppermute | solution.py:699
  86.9 4.5 %collective-permute-start.21 = (f32[8,128]{1,0:T(8,128)S(1)}, f32[8,128]{1,0:T(8,128)S(1)}, u32[]{:S(2)}, u32[]{:S(2)}) collective-permute-start(f32[8,128]{1,0:T(8,128)S(1)} %add_add_fusion.rest_0_), channel_id=1, source_target_pairs={{0,4},{4,0},{8,12},{12,8},{1,5},{5,1},{9,13},{13,9},{2,6},{6,2},{1... | collective-permute-start | bytes 12296 | tf_op jit(solution)/shard_map/ppermute | solution.py:699
  (1 other events, 9.5 us)

commit v6 on v5

--- a/solution.py
+++ b/solution.py
@@ -298,10 +298,47 @@
     return code & 255, (code >> 8) & 255, code >> 16
 
 
-def tensors_body(mask_in, stat, out, own_list, halo_list, col, mask, sem, *, half, tiles, reach, length_z):
+def apply_pair(tab, slot, vec, col, acc_i, acc_j, both):
+    acc = [acc_j(c)[...] for c in range(3)] if both else None
+    for step in range(BLOCK // SUB):
+        at = slice(step * SUB, (step + 1) * SUB)
+        t = [tab[slot, k, at, :] for k in range(4)]
+        new = apply_tensor(t, vec)
+        for c in range(3):
+            if both:
+                acc_i(c)[at, :] += new[c]
+            else:
+                acc_i(c)[at, :] = new[c]
+        if both:
+            new = apply_tensor(t, [col(c, at) for c in range(3)])
+            acc = [a + n for a, n in zip(acc, new)]
+    if both:
+        for c in range(3):
+            acc_j(c)[...] = acc[c]
+
+
+def gather_sums(out, acc_i, acc_j, tall, count):
+    for t in range(tall):
+        rows = []
+        for c in range(3):
+            total = acc_j[t, c]
+            if t < count:
+                parts = [acc_i[t, c, k * SUB : (k + 1) * SUB, :] for k in range(BLOCK // SUB)]
+                total = total + lane_sums(parts)
+            rows.append(row_sum(total))
+        out[t] = jnp.concatenate(rows + [jnp.zeros((5, BLOCK), f32)], axis=0)
+
+
+def tensors_body(
+    mask_in, stat, v, out, near, own_list, halo_list, col, acc_i, acc_j, wide, mask, sem, *, half, tiles, reach, length_z
+):
     copy = pltpu.make_async_copy(mask_in, mask, sem)
     copy.start()
-    columns([stat[t] for t in range(tiles)], 5, col)
+    columns([jnp.concatenate([stat[t][0:5], v[t][0:3]], axis=0) for t in range(tiles)], 8, col)
+    for t in range(tiles):
+        for c in range(3):
+            acc_j[t, c] = jnp.zeros((SUB, BLOCK), f32)
+            wide[t, c] = spread(v[t], c)
     copy.wait()
     last = own_list.shape[0] - 2
     n = jnp.int32(0)
@@ -320,21 +357,31 @@
         m = m + mask[c, at]
     halo_list[halo_list.shape[0] - 1] = m
 
-    def visit(at, unused):
-        slot, b, other = unpack(own_list[jnp.maximum(at - tiles, 0)])
-        alone = at < tiles
-        slot = jnp.where(alone, own_slot(at, 0, tiles, reach), slot)
-        b = jnp.where(alone, at, b)
-        tile = stat[jnp.where(alone, at, other)]
+    def pair(slot, b, other, both):
+        tile = stat[other]
         rows = [tile[k : k + 1, :] for k in range(5)]
 
         def store(k, at, value):
             out[slot, k, at, :] = value
 
         build_pair(lambda k, at: col[b, k, at, :], rows, store, length_z)
+        apply_pair(
+            out,
+            slot,
+            [wide[other, c] for c in range(3)],
+            lambda c, at: col[b, 5 + c, at, :],
+            lambda c: acc_i.at[b, c],
+            lambda c: acc_j.at[other, c],
+            both,
+        )
+
+    def alone(b, unused):
+        pair(own_slot(b, 0, tiles, reach), b, b, False)
         return unused
 
-    lax.fori_loop(0, tiles + n, visit, 0)
+    lax.fori_loop(0, tiles, alone, 0)
+    walk(own_list, 0, n, lambda code: pair(*unpack(code), True))
+    gather_sums(near, acc_i, acc_j, tiles, tiles)
 
 
 def own_body(codes, v, tab, *rest, begin, end, tiles, reach):
@@ -346,47 +393,31 @@
             acc_j[t, c] = jnp.zeros((SUB, BLOCK), f32)
             wide[t, c] = spread(v[begin + t], c)
 
-    def pair(b, other, slot, both):
+    def pair(slot, b, other, both):
         at_b, at_o = b - begin, other - begin
-        vec = [wide[at_o, c] for c in range(3)]
-        acc = [acc_j[at_o, c] for c in range(3)] if both else None
-        for step in range(BLOCK // SUB):
-            at = slice(step * SUB, (step + 1) * SUB)
-            t = [tab[slot, k, at, :] for k in range(4)]
-            new = apply_tensor(t, vec)
-            for c in range(3):
-                if both:
-                    acc_i[at_b, c, at, :] += new[c]
-                else:
-                    acc_i[at_b, c, at, :] = new[c]
-            if both:
-                new = apply_tensor(t, [col[at_b, c, at, :] for c in range(3)])
-                acc = [a + n for a, n in zip(acc, new)]
-        if both:
-            for c in range(3):
-                acc_j[at_o, c] = acc[c]
+        apply_pair(
+            tab,
+            slot,
+            [wide[at_o, c] for c in range(3)],
+            lambda c, at: col[at_b, c, at, :],
+            lambda c: acc_i.at[at_b, c],
+            lambda c: acc_j.at[at_o, c],
+            both,
+        )
 
     def alone(b, unused):
-        pair(b, b, own_slot(b, 0, tiles, reach), False)
+        pair(own_slot(b, 0, tiles, reach), b, b, False)
         return unused
 
     lax.fori_loop(begin, end, alone, 0)
     last = codes.shape[0] - 2
-
-    def visit(code):
-        slot, b, other = unpack(code)
-        pair(b, other, slot, True)
-
-    walk(codes, codes[last] if begin else 0, codes[last + 1] if begin else codes[last], visit)
-    for t in range(top - begin):
-        rows = []
-        for c in range(3):
-            total = acc_j[t, c]
-            if t < end - begin:
-                parts = [acc_i[t, c, k * SUB : (k + 1) * SUB, :] for k in range(BLOCK // SUB)]
-                total = total + lane_sums(parts)
-            rows.append(row_sum(total))
-        out[t] = jnp.concatenate(rows + [jnp.zeros((5, BLOCK), f32)], axis=0)
+    walk(
+        codes,
+        codes[last] if begin else 0,
+        codes[last + 1] if begin else codes[last],
+        lambda code: pair(*unpack(code), True),
+    )
+    gather_sums(out, acc_i, acc_j, top - begin, end - begin)
 
 
 def halo_pairs(tiles, reach):
@@ -400,27 +431,6 @@
     return pairs
 
 
-def halo_tensors_body(meta, codes, stat, *rest, tiles, plane, slabs, reach, length_z):
-    rows = slabs // plane
-    near, wide = rest[:plane], rest[plane : plane + rows]
-    out, first, col, held = rest[plane + rows :]
-    halo = halo_tiles(meta, near, wide, held, plane, slabs, reach)
-    for k, tile in enumerate(halo):
-        first[k] = tile
-    columns(halo, 5, col)
-    def visit(code):
-        index, h, c = unpack(code)
-        own = stat[c]
-        own_rows = [own[k : k + 1, :] for k in range(5)]
-
-        def store(k, at, value):
-            out[index, k, at, :] = value
-
-        build_pair(lambda k, at: col[h, k, at, :], own_rows, store, length_z)
-
-    walk(codes, 0, codes[codes.shape[0] - 1], visit)
-
-
 def far_geometry(nodes, geo, box_height):
     turned = nodes[...].T
     row = nodes[...]
@@ -437,30 +447,40 @@
     geo[3] = dx * dx + dy * dy + box_height * box_height
 
 
-def far_tensor(geo, apart, put, box_height, length_z):
+def far_tensor(geo, shift, put, length_z, wrapped):
     for step in range(BLOCK // CHUNK):
         at = slice(step * CHUNK, (step + 1) * CHUNK)
         dx, dy = geo[0, at, :], geo[1, at, :]
-        dz = wrap_z(geo[2, at, :] - apart * box_height, length_z)
+        dz = geo[2, at, :] - shift
+        if wrapped:
+            dz = wrap_z(dz, length_z)
         inv = lax.rsqrt(geo[3, at, :] + dz * dz)
         inv_two = inv * inv
-        three = inv * inv_two
-        five = 3.0 * three * inv_two
-        for k, value in enumerate(tensor(five, three, dx, dy, dz)):
+        root = (math.sqrt(3.0) * inv_two) * (inv * lax.rsqrt(inv))
+        for k, value in enumerate((root * dx, root * dy, root * dz, inv * inv_two)):
             put(k, at, value)
 
 
-def far_tensors_body(nodes, out, geo, *, box_height, length_z):
+def far_tensors_body(nodes, after, out, geo, *, boxes, box_height, length_z):
     far_geometry(nodes, geo, box_height)
 
-    def visit(d, unused):
+    def visit(d, shift, wrapped):
         def put(k, at, value):
             out[at.start // SUB, d - 1, k] = value
 
-        far_tensor(geo, d.astype(f32), put, box_height, length_z)
+        far_tensor(geo, shift.astype(f32) * box_height, put, length_z, wrapped)
+
+    def below(d, unused):
+        visit(d, d, False)
         return unused
 
-    lax.fori_loop(1, out.shape[1] + 1, visit, 0)
+    def above(d, unused):
+        visit(d, d - boxes, False)
+        return unused
+
+    lax.fori_loop(1, boxes // 2, below, 0)
+    visit(boxes // 2, jnp.int32(boxes // 2), True)
+    lax.fori_loop(boxes // 2 + 1, boxes, above, 0)
 
 
 def apply_tensor(t, v):
@@ -510,7 +530,7 @@
         def hold(k, at, value):
             geo[4 + k, at, :] = value
 
-        far_tensor(geo, d.astype(f32), hold, box_height, length_z)
+        far_tensor(geo, d.astype(f32) * box_height, hold, length_z, True)
         for box in range(BOXES_DEV):
 
             @pl.when(d < boxes - 1 if box else d > 1)
@@ -536,7 +556,7 @@
             )
 
 
-def field_body(meta, codes, nodes, stat, v, phi, halo_tab, *rest,
+def field_body(meta, codes, nodes, stat, v, phi, *rest,
                mode, tiles, reach, plane, slabs, box_height, length_z, surface, kept, half):
     rest = list(rest)
 
@@ -544,13 +564,15 @@
         return [rest.pop(0) for _ in range(count)]
 
     rows = slabs // plane
-    parts = take(2)
-    near = take(plane) if mode else []
+    parts = take(2 if mode else 1)
+    halo_tab = take(1)[0] if mode else None
+    near = take(plane)
     bundles = take(rows)
-    first = None if mode else take(1)[0]
     table = take(1)[0] if kept else None
     extra = take((0, 0, 4)[mode])
     outs = take((3, 4, 5)[mode])
+    if not mode:
+        halo_tab = take(1)[0]
     acc, col, wide, fcol, geo, held = rest
     boxes = slabs * BOXES_DEV
     member = meta[0]
@@ -569,21 +591,27 @@
     sums = jnp.sum(total, axis=1, keepdims=True)
     moment = [surface * (sums[c : c + 1] + sums[3 + c : 4 + c]) for c in range(3)]
 
-    if mode:
-        halo = halo_tiles(meta, near, bundles, held, plane, slabs, reach)
-    else:
-        halo = [first[k][5:8] for k in range(2 * reach)]
-    columns(halo, 3, col)
+    halo = halo_tiles(meta, near, bundles, held, plane, slabs, reach)
+    lead = 0 if mode else 5
+    columns(halo, lead + 3, col)
     for t in range(tiles):
         for c in range(3):
             acc[t, c] = jnp.zeros((SUB, BLOCK), f32)
     def visit(code):
         index, h, c = unpack(code)
+        if not mode:
+            own = stat[c]
+            own_rows = [own[k : k + 1, :] for k in range(5)]
+
+            def store(k, at, value):
+                halo_tab[index, k, at, :] = value
+
+            build_pair(lambda k, at: col[h, k, at, :], own_rows, store, length_z)
         sofar = [acc[c, k] for k in range(3)]
         for step in range(BLOCK // SUB):
             at = slice(step * SUB, (step + 1) * SUB)
             new = apply_tensor(
-                [halo_tab[index, k, at, :] for k in range(4)], [col[h, k, at, :] for k in range(3)]
+                [halo_tab[index, k, at, :] for k in range(4)], [col[h, lead + k, at, :] for k in range(3)]
             )
             sofar = [a + n for a, n in zip(sofar, new)]
         for k in range(3):
@@ -609,7 +637,7 @@
         value = jnp.concatenate(rows + [zero], axis=0)
         if t < parts[0].shape[0]:
             value = value + parts[0][t]
-        if t >= half:
+        if mode and t >= half:
             value = value + parts[1][t - half]
         fields.append(value)
 
@@ -741,23 +769,31 @@
         ],
     )
     count = own_slots(0, tiles, tiles, reach)
-    tab, own_list, halo_list = call(
+    tab, near_zero, own_list, halo_list = call(
         functools.partial(tensors_body, half=half, tiles=tiles, reach=reach, length_z=length_z),
-        [(count, 4, BLOCK, BLOCK)],
-        [far_memory(mask), stat],
+        [(count, 4, BLOCK, BLOCK), tile_shape],
+        [far_memory(mask), stat, x0],
         far=1,
-        scratch=[(tiles, 5, BLOCK, BLOCK)],
+        scratch=[
+            (tiles, 8, BLOCK, BLOCK),
+            (tiles, 3, BLOCK, BLOCK),
+            (tiles, 3, SUB, BLOCK),
+            (tiles, 3, SUB, BLOCK),
+        ],
         more=[pltpu.SMEM(mask.shape, jnp.int32), pltpu.SemaphoreType.DMA],
         cost=pl.CostEstimate(flops=count * BLOCK * BLOCK * 70, bytes_accessed=1 << 20, transcendentals=count * BLOCK * BLOCK * 2),
+        limit=18 << 20,
         pinned=(0,),
         lists=(count - tiles + 2, len(halo_pairs(tiles, reach)) + 1),
     )
-    table = []
-    if kept:
-        table = call(
-            functools.partial(far_tensors_body, box_height=box_height, length_z=length_z),
+
+    def far_tables(after):
+        if not kept:
+            return []
+        return call(
+            functools.partial(far_tensors_body, boxes=boxes, box_height=box_height, length_z=length_z),
             [(BLOCK // SUB, boxes - 1, 4, SUB, BLOCK)],
-            [nodes],
+            [nodes, after],
             scratch=[(4, BLOCK, BLOCK)],
             cost=pl.CostEstimate(flops=boxes * BLOCK * BLOCK * 28, bytes_accessed=1 << 20, transcendentals=boxes * BLOCK * BLOCK),
             pinned=(0,),
@@ -779,23 +815,27 @@
             cost=pl.CostEstimate(flops=72 * BLOCK * BLOCK * 18, bytes_accessed=1 << 20, transcendentals=0),
         )[0]
 
+    def relay(near, after):
+        size = near[0].shape[0] - 1
+        return call(
+            functools.partial(relay_body, plane=plane, reach=reach),
+            [(plane + size, 8, BLOCK)],
+            [meta] + near + [after],
+            smem=1,
+            scratch=[(plane, size, 8, BLOCK)],
+        )[0]
+
     def exchange(payload, v):
         near = swap(payload, ("oct", "sub"), plane)
         first = own_field(v, 0, half, [])
-        bundle = call(
-            functools.partial(relay_body, plane=plane, reach=reach),
-            [(plane + payload.shape[0] - 1, 8, BLOCK)],
-            [meta] + near + [first],
-            smem=1,
-            scratch=[(plane, payload.shape[0] - 1, 8, BLOCK)],
-        )[0]
+        bundle = relay(near, first)
         bundles = swap(bundle, "blk", rows)
         second = own_field(v, half, tiles, [bundle])
         return [first, second], near, bundles
 
-    def field(mode, v, parts, near, bundles, extra):
+    def field(mode, v, parts, halo_tab, near, bundles, extra):
         outs = [
-            [tile_shape, tile_shape, (1 + reach, 8, BLOCK)],
+            [tile_shape, tile_shape, (1 + reach, 8, BLOCK), (len(halo_pairs(tiles, reach)), 4, BLOCK, BLOCK)],
             [tile_shape, tile_shape, (1 + reach, 8, BLOCK), (SUB, BLOCK)],
             [tile_shape] * 4 + [(8, BLOCK)],
         ][mode]
@@ -805,35 +845,28 @@
                 length_z=length_z, surface=surface, kept=kept, half=half,
             ),
             outs,
-            [meta, halo_list, nodes, stat, v, phi, halo_tab] + parts + (near if mode else []) + bundles
-            + ([] if mode else [edge]) + table + extra,
+            [meta, halo_list, nodes, stat, v, phi] + parts + halo_tab + near + bundles + table + extra,
             smem=2,
+            pinned=() if mode else (3,),
             scratch=[
                 (tiles, 3, SUB, BLOCK),
-                (2 * reach, 3, BLOCK, BLOCK),
+                (2 * reach, 3 if mode else 8, BLOCK, BLOCK),
                 (boxes, 3, SUB, BLOCK),
                 (BOXES_DEV, 3, BLOCK, BLOCK),
                 (8, BLOCK, BLOCK) if not kept else (1, 8, BLOCK),
-                (plane + rows, reach, 8, BLOCK),
+                (plane + rows, reach if mode else 2 * reach, 8, BLOCK),
             ],
         )
 
-    parts, near, bundles = exchange(payload, x0)
-    halo_tab, edge = call(
-        functools.partial(
-            halo_tensors_body, tiles=tiles, plane=plane, slabs=slabs, reach=reach, length_z=length_z
-        ),
-        [(len(halo_pairs(tiles, reach)), 4, BLOCK, BLOCK), (2 * reach, 8, BLOCK)],
-        [meta, halo_list, stat] + near + bundles,
-        smem=2,
-        scratch=[(2 * reach, 5, BLOCK, BLOCK), (plane + rows, 2 * reach, 8, BLOCK)],
-        pinned=(0,),
-    )
-    r0, u0, payload = field(0, x0, parts, near, bundles, [])
+    near = swap(payload, ("oct", "sub"), plane)
+    bundle = relay(near, near_zero)
+    bundles = swap(bundle, "blk", rows)
+    table = far_tables(bundle)
+    r0, u0, payload, halo_tab = field(0, x0, [near_zero], [], near, bundles, [])
     parts, near, bundles = exchange(payload, u0)
-    w0, u1, payload, norm = field(1, u0, parts, near, bundles, [])
+    w0, u1, payload, norm = field(1, u0, parts, [halo_tab], near, bundles, [])
     parts, near, bundles = exchange(payload, u1)
-    x1, r1, z1, q1, scal = field(2, u1, parts, near, bundles, [x0, r0, w0, norm])
+    x1, r1, z1, q1, scal = field(2, u1, parts, [halo_tab], near, bundles, [x0, r0, w0, norm])
     sums = swap(scal, ("oct", "sub"), plane)
     sums = swap(functools.reduce(jnp.add, sums), "blk", rows)
     return call(

time: 92.2 us -> 86.9 us (0.943)
  Pallas kernels: 57.1 us -> 52.4 us
  starting transfers between devices: 27.8 us -> 26.7 us
    pallas_call x17 -> x14, Pallas kernels: 57.1 us -> 52.4 us  [call(): pl.pallas_call(body, out_shape=shapes, in_specs=[SM] * smem + [FAR] * far...]
    ppermute x24, starting transfers between devices: 27.8 us -> 26.7 us  [swap(): got.append(lax.ppermute(x, axes, [(i, i ^ s) for i in range(count)]))]
  transfers between devices with their start and end apart: 24 -> 24, of which waited for: 6 -> 7; matrix products, arithmetic and copies ran while one was open for 0% -> 0% of each run, Pallas kernels for 39% -> 37%
where the time goes in v6:
time: 86.9 us; the launch traced here: 86.4 us
  Pallas kernels  52.4 us (60%)
  starting transfers between devices  26.7 us (31%)
  waiting for transfers between devices  5.76 us (7%)
  between operations  0.87 us (1%)
    pallas_call x14, Pallas kernels, call(): pl.pallas_call(body, out_shape=shapes, in_specs=[SM] * smem + [FAR] * far...  52.4 us
    ppermute x24, starting transfers between devices, swap(): got.append(lax.ppermute(x, axes, [(i, i ^ s) for i in range(count)]))  26.7 us
    ppermute x24, waiting for transfers between devices, swap(): got.append(lax.ppermute(x, axes, [(i, i ^ s) for i in range(count)]))  5.76 us
  transfers between devices with their start and end apart: 24, of which 7 were waited for; matrix products, arithmetic and copies ran while one was open for 0% of the time, Pallas kernels for 37%

profile of v6, /device:TPU:0, one launch (start us, length us, event | category | flops | bytes accessed | tf_op | source)
XLA Modules:
  0.0 86.4 jit_solution(839206070628431656)
XLA Ops:
  0.6 1.9 %shard_map.86 = (f32[16,8,128]{2,1,0:T(8,128)S(1)}, f32[16,8,128]{2,1,0:T(8,128)S(1)}, f32[16,128,128]{2,1,0:T(8,128)S(1)}, f32[9,8,128]{2,1,0:T(8,128)S(1)}) custom-call(s32[1]{0:T(128)} %bitcast.meta, f32[3,2048]{1,0:T(4,128)} %pos_in.1, f32[1,2048]{1,0:T(1,128)} %bitcast.3, f32[3,2048]{1,0:T(4,128)} %field_in.1, s32[1,2048]{1,0:T(1,128)} %bitcast.4, ...), custom_call_target="tpu_custom_call" | custom-call | tf_op jit(solution)/shard_map/pallas_call | solution.py:38
  2.5 2.4 %collective-permute-start.2 = (f32[9,8,128]{2,1,0:T(8,128)S(1)}, f32[9,8,128]{2,1,0:T(8,128)S(1)}, u32[]{:S(2)}, u32[]{:S(2)}) collective-permute-start(f32[9,8,128]{2,1,0:T(8,128)S(1)} %get-tuple-element.28.rest_0_.rest_1_), channel_id=1, source_target_pairs={{0,3},{1,2},{2,1},{3,0},{4,7},{5,6},{6,5},{7,4},{8,11},{9,10},{10,... | collective-permute-start | bytes 110600 | tf_op jit(solution)/shard_map/ppermute | solution.py:727
  5.6 14.3 %shard_map.87 = (f32[70,4,128,128]{3,2,1,0:T(8,128)S(1)}, f32[16,8,128]{2,1,0:T(8,128)S(1)}, s32[56]{0:T(128)S(1)}, s32[21]{0:T(128)S(1)}) custom-call(s32[16,9]{1,0:T(8,128)} %mask_in.1, f32[16,8,128]{2,1,0:T(8,128)S(1)} %get-tuple-element.23.stat, f32[16,8,128]{2,1,0:T(8,128)S(1)} %get-tuple-element.24.v.rest_12_), custom_call_target="tpu_custom_call" | custom-call | flops 80281600 | bytes 1048576 | tf_op jit(solution)/shard_map/pallas_call | solution.py:38
  20.0 3.7 %collective-permute-start.5 = (f32[12,8,128]{2,1,0:T(8,128)S(1)}, f32[12,8,128]{2,1,0:T(8,128)S(1)}, u32[]{:S(2)}, u32[]{:S(2)}) collective-permute-start(f32[12,8,128]{2,1,0:T(8,128)S(1)} %shard_map.88.after.rest_5_), channel_id=1, source_target_pairs={{0,12},{4,8},{8,4},{12,0},{1,13},{5,9},{9,5},{13,1},{2,14},{6,10},... | collective-permute-start | bytes 147464 | tf_op jit(solution)/shard_map/ppermute | solution.py:727
  25.2 1.4 %shard_map.89.rest_9_.rest_11_ = f32[16,31,4,8,128]{4,3,2,1,0:T(8,128)S(1)} custom-call(f32[8,128]{1,0:T(8,128)S(1)} %copy-done, f32[12,8,128]{2,1,0:T(8,128)S(1)} %shard_map.88.after.rest_5_), custom_call_target="tpu_custom_call" | custom-call | flops 14680064 | bytes 1048576 | tf_op jit(solution)/shard_map/pallas_call | solution.py:38
  26.6 2.2 %collective-permute-done.4.rest_7_ = f32[12,8,128]{2,1,0:T(8,128)S(1)} collective-permute-done((f32[12,8,128]{2,1,0:T(8,128)S(1)}, f32[12,8,128]{2,1,0:T(8,128)S(1)}, u32[]{:S(2)}, u32[]{:S(2)}) %collective-permute-start.4) | collective-permute-done | bytes 49184 | tf_op jit(solution)/shard_map/ppermute | solution.py:727
  28.9 7.9 %shard_map.90 = (f32[16,8,128]{2,1,0:T(8,128)S(1)}, f32[16,8,128]{2,1,0:T(8,128)S(1)}, f32[5,8,128]{2,1,0:T(8,128)S(1)}, f32[20,4,128,128]{3,2,1,0:T(8,128)S(1)}) custom-call(s32[1]{0:T(128)} %bitcast.meta, s32[21]{0:T(128)S(1)} %get-tuple-element.25.codes, f32[8,128]{1,0:T(8,128)S(1)} %copy-done, f32[16,8,128]{2,1,0:T(8,128)S(1)} %get-tuple-element.23.stat, ...), custom_call_target="tpu_custom_call" | custom-call | tf_op jit(solution)/shard_map/pallas_call | solution.py:38
  37.4 0.8 collective-permute-start.7
  38.7 4.3 %shard_map.91.rest_4_.rest_0_ = f32[12,8,128]{2,1,0:T(8,128)S(1)} custom-call(s32[56]{0:T(128)S(1)} %get-tuple-element.30.codes, f32[16,8,128]{2,1,0:T(8,128)S(1)} %get-tuple-element.29.v, f32[70,4,128,128]{3,2,1,0:T(8,128)S(1)} %get-tuple-element.31.tab), custom_call_target="tpu_custom_call" | custom-call | flops 21233664 | bytes 1048576 | tf_op jit(solution)/shard_map/pallas_call | solution.py:38
  43.1 1.8 %collective-permute-start.11 = (f32[8,8,128]{2,1,0:T(8,128)S(1)}, f32[8,8,128]{2,1,0:T(8,128)S(1)}, u32[]{:S(2)}, u32[]{:S(2)}) collective-permute-start(f32[8,8,128]{2,1,0:T(8,128)S(1)} %shard_map.92.rest_0_.rest_7_), channel_id=1, source_target_pairs={{0,12},{4,8},{8,4},{12,0},{1,13},{5,9},{9,5},{13,1},{2,14},{6,10},... | collective-permute-start | bytes 98312 | tf_op jit(solution)/shard_map/ppermute | solution.py:727
  45.4 2.2 %collective-permute-start.9 = (f32[8,8,128]{2,1,0:T(8,128)S(1)}, f32[8,8,128]{2,1,0:T(8,128)S(1)}, u32[]{:S(2)}, u32[]{:S(2)}) collective-permute-start(f32[8,8,128]{2,1,0:T(8,128)S(1)} %shard_map.92.rest_0_.rest_7_), channel_id=1, source_target_pairs={{0,4},{4,0},{8,12},{12,8},{1,5},{5,1},{9,13},{13,9},{2,6},{6,2},{1... | collective-permute-start | bytes 98312 | tf_op jit(solution)/shard_map/ppermute | solution.py:727
  47.5 3.7 %shard_map.93.rest_1_ = f32[8,8,128]{2,1,0:T(8,128)S(1)} custom-call(s32[56]{0:T(128)S(1)} %get-tuple-element.30.codes, f32[16,8,128]{2,1,0:T(8,128)S(1)} %get-tuple-element.29.v, f32[70,4,128,128]{3,2,1,0:T(8,128)S(1)} %get-tuple-element.31.tab, f32[8,8,128]{2,1,0:T(8,128)S(1)} %shard_map.92.rest_0_.rest_7_), custom_call_target="tpu_custom_call" | custom-call | flops 21233664 | bytes 1048576 | tf_op jit(solution)/shard_map/pallas_call | solution.py:38
  51.3 5.3 %shard_map.94 = (f32[16,8,128]{2,1,0:T(8,128)S(1)}, f32[16,8,128]{2,1,0:T(8,128)S(1)}, f32[5,8,128]{2,1,0:T(8,128)S(1)}, f32[8,128]{1,0:T(8,128)S(1)}) custom-call(s32[1]{0:T(128)} %bitcast.meta, s32[21]{0:T(128)S(1)} %get-tuple-element.25.codes, f32[8,128]{1,0:T(8,128)S(1)} %copy-done.1, f32[16,8,128]{2,1,0:T(8,128)S(1)} %get-tuple-element.23.stat, ...), custom_call_target="tpu_custom_call" | custom-call | tf_op jit(solution)/shard_map/pallas_call | solution.py:38
  57.3 1.2 %collective-permute-start.12 = (f32[5,8,128]{2,1,0:T(8,128)S(1)}, f32[5,8,128]{2,1,0:T(8,128)S(1)}, u32[]{:S(2)}, u32[]{:S(2)}) collective-permute-start(f32[5,8,128]{2,1,0:T(8,128)S(1)} %get-tuple-element.35.rest_0_.rest_3_), channel_id=1, source_target_pairs={{0,1},{1,0},{2,3},{3,2},{4,5},{5,4},{6,7},{7,6},{8,9},{9,8},{10,11... | collective-permute-start | bytes 61448 | tf_op jit(solution)/shard_map/ppermute | solution.py:727
  58.5 4.3 %shard_map.95.rest_4_.rest_0_ = f32[12,8,128]{2,1,0:T(8,128)S(1)} custom-call(s32[56]{0:T(128)S(1)} %get-tuple-element.30.codes, f32[16,8,128]{2,1,0:T(8,128)S(1)} %get-tuple-element.34.v, f32[70,4,128,128]{3,2,1,0:T(8,128)S(1)} %get-tuple-element.31.tab), custom_call_target="tpu_custom_call" | custom-call | flops 21233664 | bytes 1048576 | tf_op jit(solution)/shard_map/pallas_call | solution.py:38
  62.8 1.5 %collective-permute-start.17 = (f32[8,8,128]{2,1,0:T(8,128)S(1)}, f32[8,8,128]{2,1,0:T(8,128)S(1)}, u32[]{:S(2)}, u32[]{:S(2)}) collective-permute-start(f32[8,8,128]{2,1,0:T(8,128)S(1)} %shard_map.96.rest_0_.rest_7_), channel_id=1, source_target_pairs={{0,12},{4,8},{8,4},{12,0},{1,13},{5,9},{9,5},{13,1},{2,14},{6,10},... | collective-permute-start | bytes 98312 | tf_op jit(solution)/shard_map/ppermute | solution.py:727
  64.5 2.8 %collective-permute-start.15 = (f32[8,8,128]{2,1,0:T(8,128)S(1)}, f32[8,8,128]{2,1,0:T(8,128)S(1)}, u32[]{:S(2)}, u32[]{:S(2)}) collective-permute-start(f32[8,8,128]{2,1,0:T(8,128)S(1)} %shard_map.96.rest_0_.rest_7_), channel_id=1, source_target_pairs={{0,4},{4,0},{8,12},{12,8},{1,5},{5,1},{9,13},{13,9},{2,6},{6,2},{1... | collective-permute-start | bytes 98312 | tf_op jit(solution)/shard_map/ppermute | solution.py:727
  67.3 3.7 %shard_map.97.rest_1_ = f32[8,8,128]{2,1,0:T(8,128)S(1)} custom-call(s32[56]{0:T(128)S(1)} %get-tuple-element.30.codes, f32[16,8,128]{2,1,0:T(8,128)S(1)} %get-tuple-element.34.v, f32[70,4,128,128]{3,2,1,0:T(8,128)S(1)} %get-tuple-element.31.tab, f32[8,8,128]{2,1,0:T(8,128)S(1)} %shard_map.96.rest_0_.rest_7_), custom_call_target="tpu_custom_call" | custom-call | flops 21233664 | bytes 1048576 | tf_op jit(solution)/shard_map/pallas_call | solution.py:38
  71.0 4.9 %shard_map.98 = (f32[16,8,128]{2,1,0:T(8,128)S(1)}, f32[16,8,128]{2,1,0:T(8,128)S(1)}, f32[16,8,128]{2,1,0:T(8,128)S(1)}, f32[16,8,128]{2,1,0:T(8,128)S(1)}, f32[8,128]{1,0:T(8,128)S(1)}) custom-call(s32[1]{0:T(128)} %bitcast.meta, s32[21]{0:T(128)S(1)} %get-tuple-element.25.codes, f32[8,128]{1,0:T(8,128)S(1)} %copy-done.1, ...), custom_call_target="tpu_custom_call" | custom-call | tf_op jit(solution)/shard_map/pallas_call | solution.py:38
  76.3 1.5 %collective-permute-start.18 = (f32[8,128]{1,0:T(8,128)S(1)}, f32[8,128]{1,0:T(8,128)S(1)}, u32[]{:S(2)}, u32[]{:S(2)}) collective-permute-start(f32[8,128]{1,0:T(8,128)S(1)} %get-tuple-element.39.scal), channel_id=1, source_target_pairs={{0,1},{1,0},{2,3},{3,2},{4,5},{5,4},{6,7},{7,6},{8,9},{9,8},{10,11... | collective-permute-start | bytes 12296 | tf_op jit(solution)/shard_map/ppermute | solution.py:727
  77.8 1.2 %collective-permute-done.20 = f32[8,128]{1,0:T(8,128)S(1)} collective-permute-done((f32[8,128]{1,0:T(8,128)S(1)}, f32[8,128]{1,0:T(8,128)S(1)}, u32[]{:S(2)}, u32[]{:S(2)}) %collective-permute-start.20) | collective-permute-done | bytes 4128 | tf_op jit(solution)/shard_map/ppermute | solution.py:727
  79.6 1.3 %collective-permute-start.23 = (f32[8,128]{1,0:T(8,128)S(1)}, f32[8,128]{1,0:T(8,128)S(1)}, u32[]{:S(2)}, u32[]{:S(2)}) collective-permute-start(f32[8,128]{1,0:T(8,128)S(1)} %add_add_fusion.rest_0_), channel_id=1, source_target_pairs={{0,12},{4,8},{8,4},{12,0},{1,13},{5,9},{9,5},{13,1},{2,14},{6,10},... | collective-permute-start | bytes 12296 | tf_op jit(solution)/shard_map/ppermute | solution.py:727
  81.1 3.0 %collective-permute-start.21 = (f32[8,128]{1,0:T(8,128)S(1)}, f32[8,128]{1,0:T(8,128)S(1)}, u32[]{:S(2)}, u32[]{:S(2)}) collective-permute-start(f32[8,128]{1,0:T(8,128)S(1)} %add_add_fusion.rest_0_), channel_id=1, source_target_pairs={{0,4},{4,0},{8,12},{12,8},{1,5},{5,1},{9,13},{13,9},{2,6},{6,2},{1... | collective-permute-start | bytes 12296 | tf_op jit(solution)/shard_map/ppermute | solution.py:727
  84.1 1.0 %collective-permute-done.23.rest_3_ = f32[8,128]{1,0:T(8,128)S(1)} collective-permute-done((f32[8,128]{1,0:T(8,128)S(1)}, f32[8,128]{1,0:T(8,128)S(1)}, u32[]{:S(2)}, u32[]{:S(2)}) %collective-permute-start.23) | collective-permute-done | bytes 4128 | tf_op jit(solution)/shard_map/ppermute | solution.py:727
  (43 shorter events, 7.3 us)
Async XLA Ops:
  2.5 17.5 %collective-permute-start.2 = (f32[9,8,128]{2,1,0:T(8,128)S(1)}, f32[9,8,128]{2,1,0:T(8,128)S(1)}, u32[]{:S(2)}, u32[]{:S(2)}) collective-permute-start(f32[9,8,128]{2,1,0:T(8,128)S(1)} %get-tuple-element.28.rest_0_.rest_1_), channel_id=1, source_target_pairs={{0,3},{1,2},{2,1},{3,0},{4,7},{5,6},{6,5},{7,4},{8,11},{9,10},{10,... | collective-permute-start | bytes 110600 | tf_op jit(solution)/shard_map/ppermute | solution.py:727
  5.0 15.0 %collective-permute-start.1 = (f32[9,8,128]{2,1,0:T(8,128)S(1)}, f32[9,8,128]{2,1,0:T(8,128)S(1)}, u32[]{:S(2)}, u32[]{:S(2)}) collective-permute-start(f32[9,8,128]{2,1,0:T(8,128)S(1)} %get-tuple-element.28.rest_0_.rest_1_), channel_id=1, source_target_pairs={{0,2},{1,3},{2,0},{3,1},{4,6},{5,7},{6,4},{7,5},{8,10},{9,11},{10,... | collective-permute-start | bytes 110600 | tf_op jit(solution)/shard_map/ppermute | solution.py:727
  5.6 14.4 %collective-permute-start = (f32[9,8,128]{2,1,0:T(8,128)S(1)}, f32[9,8,128]{2,1,0:T(8,128)S(1)}, u32[]{:S(2)}, u32[]{:S(2)}) collective-permute-start(f32[9,8,128]{2,1,0:T(8,128)S(1)} %get-tuple-element.28.rest_0_.rest_1_), channel_id=1, source_target_pairs={{0,1},{1,0},{2,3},{3,2},{4,5},{5,4},{6,7},{7,6},{8,9},{9,8},{10,11... | collective-permute-start | bytes 110600 | tf_op jit(solution)/shard_map/ppermute | solution.py:727
  20.0 6.6 %collective-permute-start.5 = (f32[12,8,128]{2,1,0:T(8,128)S(1)}, f32[12,8,128]{2,1,0:T(8,128)S(1)}, u32[]{:S(2)}, u32[]{:S(2)}) collective-permute-start(f32[12,8,128]{2,1,0:T(8,128)S(1)} %shard_map.88.after.rest_5_), channel_id=1, source_target_pairs={{0,12},{4,8},{8,4},{12,0},{1,13},{5,9},{9,5},{13,1},{2,14},{6,10},... | collective-permute-start | bytes 147464 | tf_op jit(solution)/shard_map/ppermute | solution.py:727
  23.8 5.0 %collective-permute-start.4 = (f32[12,8,128]{2,1,0:T(8,128)S(1)}, f32[12,8,128]{2,1,0:T(8,128)S(1)}, u32[]{:S(2)}, u32[]{:S(2)}) collective-permute-start(f32[12,8,128]{2,1,0:T(8,128)S(1)} %shard_map.88.after.rest_5_), channel_id=1, source_target_pairs={{0,8},{4,12},{8,0},{12,4},{1,9},{5,13},{9,1},{13,5},{2,10},{6,14},... | collective-permute-start | bytes 147464 | tf_op jit(solution)/shard_map/ppermute | solution.py:727
  23.8 5.1 %collective-permute-start.3 = (f32[12,8,128]{2,1,0:T(8,128)S(1)}, f32[12,8,128]{2,1,0:T(8,128)S(1)}, u32[]{:S(2)}, u32[]{:S(2)}) collective-permute-start(f32[12,8,128]{2,1,0:T(8,128)S(1)} %shard_map.88.after.rest_5_), channel_id=1, source_target_pairs={{0,4},{4,0},{8,12},{12,8},{1,5},{5,1},{9,13},{13,9},{2,6},{6,2},{1... | collective-permute-start | bytes 147464 | tf_op jit(solution)/shard_map/ppermute | solution.py:727
  36.8 6.2 %collective-permute-start.8 = (f32[5,8,128]{2,1,0:T(8,128)S(1)}, f32[5,8,128]{2,1,0:T(8,128)S(1)}, u32[]{:S(2)}, u32[]{:S(2)}) collective-permute-start(f32[5,8,128]{2,1,0:T(8,128)S(1)} %get-tuple-element.32.rest_0_.rest_3_), channel_id=1, source_target_pairs={{0,3},{1,2},{2,1},{3,0},{4,7},{5,6},{6,5},{7,4},{8,11},{9,10},{10,... | collective-permute-start | bytes 61448 | tf_op jit(solution)/shard_map/ppermute | solution.py:727
  37.4 5.7 %collective-permute-start.7 = (f32[5,8,128]{2,1,0:T(8,128)S(1)}, f32[5,8,128]{2,1,0:T(8,128)S(1)}, u32[]{:S(2)}, u32[]{:S(2)}) collective-permute-start(f32[5,8,128]{2,1,0:T(8,128)S(1)} %get-tuple-element.32.rest_0_.rest_3_), channel_id=1, source_target_pairs={{0,2},{1,3},{2,0},{3,1},{4,6},{5,7},{6,4},{7,5},{8,10},{9,11},{10,... | collective-permute-start | bytes 61448 | tf_op jit(solution)/shard_map/ppermute | solution.py:727
  38.2 4.9 %collective-permute-start.6 = (f32[5,8,128]{2,1,0:T(8,128)S(1)}, f32[5,8,128]{2,1,0:T(8,128)S(1)}, u32[]{:S(2)}, u32[]{:S(2)}) collective-permute-start(f32[5,8,128]{2,1,0:T(8,128)S(1)} %get-tuple-element.32.rest_0_.rest_3_), channel_id=1, source_target_pairs={{0,1},{1,0},{2,3},{3,2},{4,5},{5,4},{6,7},{7,6},{8,9},{9,8},{10,11... | collective-permute-start | bytes 61448 | tf_op jit(solution)/shard_map/ppermute | solution.py:727
  43.1 8.2 %collective-permute-start.11 = (f32[8,8,128]{2,1,0:T(8,128)S(1)}, f32[8,8,128]{2,1,0:T(8,128)S(1)}, u32[]{:S(2)}, u32[]{:S(2)}) collective-permute-start(f32[8,8,128]{2,1,0:T(8,128)S(1)} %shard_map.92.rest_0_.rest_7_), channel_id=1, source_target_pairs={{0,12},{4,8},{8,4},{12,0},{1,13},{5,9},{9,5},{13,1},{2,14},{6,10},... | collective-permute-start | bytes 98312 | tf_op jit(solution)/shard_map/ppermute | solution.py:727
  44.9 6.4 %collective-permute-start.10 = (f32[8,8,128]{2,1,0:T(8,128)S(1)}, f32[8,8,128]{2,1,0:T(8,128)S(1)}, u32[]{:S(2)}, u32[]{:S(2)}) collective-permute-start(f32[8,8,128]{2,1,0:T(8,128)S(1)} %shard_map.92.rest_0_.rest_7_), channel_id=1, source_target_pairs={{0,8},{4,12},{8,0},{12,4},{1,9},{5,13},{9,1},{13,5},{2,10},{6,14},... | collective-permute-start | bytes 98312 | tf_op jit(solution)/shard_map/ppermute | solution.py:727
  45.4 5.9 %collective-permute-start.9 = (f32[8,8,128]{2,1,0:T(8,128)S(1)}, f32[8,8,128]{2,1,0:T(8,128)S(1)}, u32[]{:S(2)}, u32[]{:S(2)}) collective-permute-start(f32[8,8,128]{2,1,0:T(8,128)S(1)} %shard_map.92.rest_0_.rest_7_), channel_id=1, source_target_pairs={{0,4},{4,0},{8,12},{12,8},{1,5},{5,1},{9,13},{13,9},{2,6},{6,2},{1... | collective-permute-start | bytes 98312 | tf_op jit(solution)/shard_map/ppermute | solution.py:727
  56.5 6.2 %collective-permute-start.14 = (f32[5,8,128]{2,1,0:T(8,128)S(1)}, f32[5,8,128]{2,1,0:T(8,128)S(1)}, u32[]{:S(2)}, u32[]{:S(2)}) collective-permute-start(f32[5,8,128]{2,1,0:T(8,128)S(1)} %get-tuple-element.35.rest_0_.rest_3_), channel_id=1, source_target_pairs={{0,3},{1,2},{2,1},{3,0},{4,7},{5,6},{6,5},{7,4},{8,11},{9,10},{10,... | collective-permute-start | bytes 61448 | tf_op jit(solution)/shard_map/ppermute | solution.py:727
  56.6 6.1 %collective-permute-start.13 = (f32[5,8,128]{2,1,0:T(8,128)S(1)}, f32[5,8,128]{2,1,0:T(8,128)S(1)}, u32[]{:S(2)}, u32[]{:S(2)}) collective-permute-start(f32[5,8,128]{2,1,0:T(8,128)S(1)} %get-tuple-element.35.rest_0_.rest_3_), channel_id=1, source_target_pairs={{0,2},{1,3},{2,0},{3,1},{4,6},{5,7},{6,4},{7,5},{8,10},{9,11},{10,... | collective-permute-start | bytes 61448 | tf_op jit(solution)/shard_map/ppermute | solution.py:727
  57.3 5.5 %collective-permute-start.12 = (f32[5,8,128]{2,1,0:T(8,128)S(1)}, f32[5,8,128]{2,1,0:T(8,128)S(1)}, u32[]{:S(2)}, u32[]{:S(2)}) collective-permute-start(f32[5,8,128]{2,1,0:T(8,128)S(1)} %get-tuple-element.35.rest_0_.rest_3_), channel_id=1, source_target_pairs={{0,1},{1,0},{2,3},{3,2},{4,5},{5,4},{6,7},{7,6},{8,9},{9,8},{10,11... | collective-permute-start | bytes 61448 | tf_op jit(solution)/shard_map/ppermute | solution.py:727
  62.8 8.2 %collective-permute-start.17 = (f32[8,8,128]{2,1,0:T(8,128)S(1)}, f32[8,8,128]{2,1,0:T(8,128)S(1)}, u32[]{:S(2)}, u32[]{:S(2)}) collective-permute-start(f32[8,8,128]{2,1,0:T(8,128)S(1)} %shard_map.96.rest_0_.rest_7_), channel_id=1, source_target_pairs={{0,12},{4,8},{8,4},{12,0},{1,13},{5,9},{9,5},{13,1},{2,14},{6,10},... | collective-permute-start | bytes 98312 | tf_op jit(solution)/shard_map/ppermute | solution.py:727
  64.3 6.6 %collective-permute-start.16 = (f32[8,8,128]{2,1,0:T(8,128)S(1)}, f32[8,8,128]{2,1,0:T(8,128)S(1)}, u32[]{:S(2)}, u32[]{:S(2)}) collective-permute-start(f32[8,8,128]{2,1,0:T(8,128)S(1)} %shard_map.96.rest_0_.rest_7_), channel_id=1, source_target_pairs={{0,8},{4,12},{8,0},{12,4},{1,9},{5,13},{9,1},{13,5},{2,10},{6,14},... | collective-permute-start | bytes 98312 | tf_op jit(solution)/shard_map/ppermute | solution.py:727
  64.5 6.5 %collective-permute-start.15 = (f32[8,8,128]{2,1,0:T(8,128)S(1)}, f32[8,8,128]{2,1,0:T(8,128)S(1)}, u32[]{:S(2)}, u32[]{:S(2)}) collective-permute-start(f32[8,8,128]{2,1,0:T(8,128)S(1)} %shard_map.96.rest_0_.rest_7_), channel_id=1, source_target_pairs={{0,4},{4,0},{8,12},{12,8},{1,5},{5,1},{9,13},{13,9},{2,6},{6,2},{1... | collective-permute-start | bytes 98312 | tf_op jit(solution)/shard_map/ppermute | solution.py:727
  75.9 3.1 %collective-permute-start.20 = (f32[8,128]{1,0:T(8,128)S(1)}, f32[8,128]{1,0:T(8,128)S(1)}, u32[]{:S(2)}, u32[]{:S(2)}) collective-permute-start(f32[8,128]{1,0:T(8,128)S(1)} %get-tuple-element.39.scal), channel_id=1, source_target_pairs={{0,3},{1,2},{2,1},{3,0},{4,7},{5,6},{6,5},{7,4},{8,11},{9,10},{10,... | collective-permute-start | bytes 12296 | tf_op jit(solution)/shard_map/ppermute | solution.py:727
  76.0 3.7 %collective-permute-start.19 = (f32[8,128]{1,0:T(8,128)S(1)}, f32[8,128]{1,0:T(8,128)S(1)}, u32[]{:S(2)}, u32[]{:S(2)}) collective-permute-start(f32[8,128]{1,0:T(8,128)S(1)} %get-tuple-element.39.scal), channel_id=1, source_target_pairs={{0,2},{1,3},{2,0},{3,1},{4,6},{5,7},{6,4},{7,5},{8,10},{9,11},{10,... | collective-permute-start | bytes 12296 | tf_op jit(solution)/shard_map/ppermute | solution.py:727
  76.3 3.3 %collective-permute-start.18 = (f32[8,128]{1,0:T(8,128)S(1)}, f32[8,128]{1,0:T(8,128)S(1)}, u32[]{:S(2)}, u32[]{:S(2)}) collective-permute-start(f32[8,128]{1,0:T(8,128)S(1)} %get-tuple-element.39.scal), channel_id=1, source_target_pairs={{0,1},{1,0},{2,3},{3,2},{4,5},{5,4},{6,7},{7,6},{8,9},{9,8},{10,11... | collective-permute-start | bytes 12296 | tf_op jit(solution)/shard_map/ppermute | solution.py:727
  79.6 5.5 %collective-permute-start.23 = (f32[8,128]{1,0:T(8,128)S(1)}, f32[8,128]{1,0:T(8,128)S(1)}, u32[]{:S(2)}, u32[]{:S(2)}) collective-permute-start(f32[8,128]{1,0:T(8,128)S(1)} %add_add_fusion.rest_0_), channel_id=1, source_target_pairs={{0,12},{4,8},{8,4},{12,0},{1,13},{5,9},{9,5},{13,1},{2,14},{6,10},... | collective-permute-start | bytes 12296 | tf_op jit(solution)/shard_map/ppermute | solution.py:727
  81.0 4.5 %collective-permute-start.22 = (f32[8,128]{1,0:T(8,128)S(1)}, f32[8,128]{1,0:T(8,128)S(1)}, u32[]{:S(2)}, u32[]{:S(2)}) collective-permute-start(f32[8,128]{1,0:T(8,128)S(1)} %add_add_fusion.rest_0_), channel_id=1, source_target_pairs={{0,8},{4,12},{8,0},{12,4},{1,9},{5,13},{9,1},{13,5},{2,10},{6,14},... | collective-permute-start | bytes 12296 | tf_op jit(solution)/shard_map/ppermute | solution.py:727
  81.1 4.6 %collective-permute-start.21 = (f32[8,128]{1,0:T(8,128)S(1)}, f32[8,128]{1,0:T(8,128)S(1)}, u32[]{:S(2)}, u32[]{:S(2)}) collective-permute-start(f32[8,128]{1,0:T(8,128)S(1)} %add_add_fusion.rest_0_), channel_id=1, source_target_pairs={{0,4},{4,0},{8,12},{12,8},{1,5},{5,1},{9,13},{13,9},{2,6},{6,2},{1... | collective-permute-start | bytes 12296 | tf_op jit(solution)/shard_map/ppermute | solution.py:727
  (2 other events, 8.9 us)

commit v7 on v6

--- a/solution.py
+++ b/solution.py
@@ -104,13 +104,12 @@
     return jnp.sum(x, axis=0, keepdims=True)
 
 
-def build_pair(col, rows, put, length_z):
+def build_pair(col, rows, put, length_z, rows_target=False):
     wide = [jnp.broadcast_to(r, (CHUNK, BLOCK)) for r in rows]
     for step in range(BLOCK // CHUNK):
         at = slice(step * CHUNK, (step + 1) * CHUNK)
-        dx = wrap_unit(col(0, at) - wide[0])
-        dy = wrap_unit(col(1, at) - wide[1])
-        dz = wrap_z(col(2, at) - wide[2], length_z)
+        gap = [wide[k] - col(k, at) if rows_target else col(k, at) - wide[k] for k in range(3)]
+        dx, dy, dz = wrap_unit(gap[0]), wrap_unit(gap[1]), wrap_z(gap[2], length_z)
         keep = col(4, at) != wide[4]
         dist = jnp.where(keep, dx * dx + dy * dy + dz * dz, 1e24)
         inv = lax.rsqrt(dist)
@@ -606,7 +605,7 @@
             def store(k, at, value):
                 halo_tab[index, k, at, :] = value
 
-            build_pair(lambda k, at: col[h, k, at, :], own_rows, store, length_z)
+            build_pair(lambda k, at: col[h, k, at, :], own_rows, store, length_z, True)
         sofar = [acc[c, k] for k in range(3)]
         for step in range(BLOCK // SUB):
             at = slice(step * SUB, (step + 1) * SUB)

time: 86.9 us -> 86.4 us (level)
  Pallas kernels: 52.4 us -> 50.7 us
  starting transfers between devices: 26.7 us -> 28 us
    pallas_call x14, Pallas kernels: 52.4 us -> 50.7 us  [call(): pl.pallas_call(body, out_shape=shapes, in_specs=[SM] * smem + [FAR] * far...]
    ppermute x24, starting transfers between devices: 26.7 us -> 28 us  [swap(): got.append(lax.ppermute(x, axes, [(i, i ^ s) for i in range(count)]))]
  transfers between devices with their start and end apart: 24 -> 24, of which waited for: 7 -> 6; matrix products, arithmetic and copies ran while one was open for 0% -> 0% of each run, Pallas kernels for 37% -> 36%
where the time goes in v7:
time: 86.4 us; the launch traced here: 86.3 us
  Pallas kernels  50.7 us (59%)
  starting transfers between devices  28 us (32%)
  waiting for transfers between devices  6.14 us (7%)
    pallas_call x14, Pallas kernels, call(): pl.pallas_call(body, out_shape=shapes, in_specs=[SM] * smem + [FAR] * far...  50.7 us
    ppermute x24, starting transfers between devices, swap(): got.append(lax.ppermute(x, axes, [(i, i ^ s) for i in range(count)]))  28 us
    ppermute x24, waiting for transfers between devices, swap(): got.append(lax.ppermute(x, axes, [(i, i ^ s) for i in range(count)]))  6.14 us
  transfers between devices with their start and end apart: 24, of which 6 were waited for; matrix products, arithmetic and copies ran while one was open for 0% of the time, Pallas kernels for 36%

profile of v7, /device:TPU:0, one launch (start us, length us, event | category | flops | bytes accessed | tf_op | source)
XLA Modules:
  0.0 86.3 jit_solution(12410231505885357699)
XLA Ops:
  0.6 1.9 %shard_map.86 = (f32[16,8,128]{2,1,0:T(8,128)S(1)}, f32[16,8,128]{2,1,0:T(8,128)S(1)}, f32[16,128,128]{2,1,0:T(8,128)S(1)}, f32[9,8,128]{2,1,0:T(8,128)S(1)}) custom-call(s32[1]{0:T(128)} %bitcast.meta, f32[3,2048]{1,0:T(4,128)} %pos_in.1, f32[1,2048]{1,0:T(1,128)} %bitcast.3, f32[3,2048]{1,0:T(4,128)} %field_in.1, s32[1,2048]{1,0:T(1,128)} %bitcast.4, ...), custom_call_target="tpu_custom_call" | custom-call | tf_op jit(solution)/shard_map/pallas_call | solution.py:38
  2.5 2.4 %collective-permute-start.2 = (f32[9,8,128]{2,1,0:T(8,128)S(1)}, f32[9,8,128]{2,1,0:T(8,128)S(1)}, u32[]{:S(2)}, u32[]{:S(2)}) collective-permute-start(f32[9,8,128]{2,1,0:T(8,128)S(1)} %get-tuple-element.28.rest_0_.rest_1_), channel_id=1, source_target_pairs={{0,3},{1,2},{2,1},{3,0},{4,7},{5,6},{6,5},{7,4},{8,11},{9,10},{10,... | collective-permute-start | bytes 110600 | tf_op jit(solution)/shard_map/ppermute | solution.py:726
  5.6 14.2 %shard_map.87 = (f32[70,4,128,128]{3,2,1,0:T(8,128)S(1)}, f32[16,8,128]{2,1,0:T(8,128)S(1)}, s32[56]{0:T(128)S(1)}, s32[21]{0:T(128)S(1)}) custom-call(s32[16,9]{1,0:T(8,128)} %mask_in.1, f32[16,8,128]{2,1,0:T(8,128)S(1)} %get-tuple-element.23.stat, f32[16,8,128]{2,1,0:T(8,128)S(1)} %get-tuple-element.24.v.rest_12_), custom_call_target="tpu_custom_call" | custom-call | flops 80281600 | bytes 1048576 | tf_op jit(solution)/shard_map/pallas_call | solution.py:38
  19.9 1.2 %collective-permute-start.5 = (f32[12,8,128]{2,1,0:T(8,128)S(1)}, f32[12,8,128]{2,1,0:T(8,128)S(1)}, u32[]{:S(2)}, u32[]{:S(2)}) collective-permute-start(f32[12,8,128]{2,1,0:T(8,128)S(1)} %shard_map.88.after.rest_5_), channel_id=1, source_target_pairs={{0,12},{4,8},{8,4},{12,0},{1,13},{5,9},{9,5},{13,1},{2,14},{6,10},... | collective-permute-start | bytes 147464 | tf_op jit(solution)/shard_map/ppermute | solution.py:726
  21.0 2.4 %collective-permute-start.4 = (f32[12,8,128]{2,1,0:T(8,128)S(1)}, f32[12,8,128]{2,1,0:T(8,128)S(1)}, u32[]{:S(2)}, u32[]{:S(2)}) collective-permute-start(f32[12,8,128]{2,1,0:T(8,128)S(1)} %shard_map.88.after.rest_5_), channel_id=1, source_target_pairs={{0,8},{4,12},{8,0},{12,4},{1,9},{5,13},{9,1},{13,5},{2,10},{6,14},... | collective-permute-start | bytes 147464 | tf_op jit(solution)/shard_map/ppermute | solution.py:726
  25.0 1.4 %shard_map.89.rest_9_.rest_11_ = f32[16,31,4,8,128]{4,3,2,1,0:T(8,128)S(1)} custom-call(f32[8,128]{1,0:T(8,128)S(1)} %copy-done, f32[12,8,128]{2,1,0:T(8,128)S(1)} %shard_map.88.after.rest_5_), custom_call_target="tpu_custom_call" | custom-call | flops 14680064 | bytes 1048576 | tf_op jit(solution)/shard_map/pallas_call | solution.py:38
  26.5 2.2 %collective-permute-done.4.rest_7_ = f32[12,8,128]{2,1,0:T(8,128)S(1)} collective-permute-done((f32[12,8,128]{2,1,0:T(8,128)S(1)}, f32[12,8,128]{2,1,0:T(8,128)S(1)}, u32[]{:S(2)}, u32[]{:S(2)}) %collective-permute-start.4) | collective-permute-done | bytes 49184 | tf_op jit(solution)/shard_map/ppermute | solution.py:726
  28.6 7.0 %shard_map.90 = (f32[16,8,128]{2,1,0:T(8,128)S(1)}, f32[16,8,128]{2,1,0:T(8,128)S(1)}, f32[5,8,128]{2,1,0:T(8,128)S(1)}, f32[20,4,128,128]{3,2,1,0:T(8,128)S(1)}) custom-call(s32[1]{0:T(128)} %bitcast.meta, s32[21]{0:T(128)S(1)} %get-tuple-element.25.codes, f32[8,128]{1,0:T(8,128)S(1)} %copy-done, f32[16,8,128]{2,1,0:T(8,128)S(1)} %get-tuple-element.23.stat, ...), custom_call_target="tpu_custom_call" | custom-call | tf_op jit(solution)/shard_map/pallas_call | solution.py:38
  36.5 1.7 %collective-permute-start.7 = (f32[5,8,128]{2,1,0:T(8,128)S(1)}, f32[5,8,128]{2,1,0:T(8,128)S(1)}, u32[]{:S(2)}, u32[]{:S(2)}) collective-permute-start(f32[5,8,128]{2,1,0:T(8,128)S(1)} %get-tuple-element.32.rest_0_.rest_3_), channel_id=1, source_target_pairs={{0,2},{1,3},{2,0},{3,1},{4,6},{5,7},{6,4},{7,5},{8,10},{9,11},{10,... | collective-permute-start | bytes 61448 | tf_op jit(solution)/shard_map/ppermute | solution.py:726
  38.2 4.3 %shard_map.91.rest_4_.rest_0_ = f32[12,8,128]{2,1,0:T(8,128)S(1)} custom-call(s32[56]{0:T(128)S(1)} %get-tuple-element.30.codes, f32[16,8,128]{2,1,0:T(8,128)S(1)} %get-tuple-element.29.v, f32[70,4,128,128]{3,2,1,0:T(8,128)S(1)} %get-tuple-element.31.tab), custom_call_target="tpu_custom_call" | custom-call | flops 21233664 | bytes 1048576 | tf_op jit(solution)/shard_map/pallas_call | solution.py:38
  42.5 1.5 %collective-permute-start.11 = (f32[8,8,128]{2,1,0:T(8,128)S(1)}, f32[8,8,128]{2,1,0:T(8,128)S(1)}, u32[]{:S(2)}, u32[]{:S(2)}) collective-permute-start(f32[8,8,128]{2,1,0:T(8,128)S(1)} %shard_map.92.rest_0_.rest_7_), channel_id=1, source_target_pairs={{0,12},{4,8},{8,4},{12,0},{1,13},{5,9},{9,5},{13,1},{2,14},{6,10},... | collective-permute-start | bytes 98312 | tf_op jit(solution)/shard_map/ppermute | solution.py:726
  44.2 2.8 %collective-permute-start.9 = (f32[8,8,128]{2,1,0:T(8,128)S(1)}, f32[8,8,128]{2,1,0:T(8,128)S(1)}, u32[]{:S(2)}, u32[]{:S(2)}) collective-permute-start(f32[8,8,128]{2,1,0:T(8,128)S(1)} %shard_map.92.rest_0_.rest_7_), channel_id=1, source_target_pairs={{0,4},{4,0},{8,12},{12,8},{1,5},{5,1},{9,13},{13,9},{2,6},{6,2},{1... | collective-permute-start | bytes 98312 | tf_op jit(solution)/shard_map/ppermute | solution.py:726
  47.0 3.6 %shard_map.93.rest_1_ = f32[8,8,128]{2,1,0:T(8,128)S(1)} custom-call(s32[56]{0:T(128)S(1)} %get-tuple-element.30.codes, f32[16,8,128]{2,1,0:T(8,128)S(1)} %get-tuple-element.29.v, f32[70,4,128,128]{3,2,1,0:T(8,128)S(1)} %get-tuple-element.31.tab, f32[8,8,128]{2,1,0:T(8,128)S(1)} %shard_map.92.rest_0_.rest_7_), custom_call_target="tpu_custom_call" | custom-call | flops 21233664 | bytes 1048576 | tf_op jit(solution)/shard_map/pallas_call | solution.py:38
  50.6 5.0 %shard_map.94 = (f32[16,8,128]{2,1,0:T(8,128)S(1)}, f32[16,8,128]{2,1,0:T(8,128)S(1)}, f32[5,8,128]{2,1,0:T(8,128)S(1)}, f32[8,128]{1,0:T(8,128)S(1)}) custom-call(s32[1]{0:T(128)} %bitcast.meta, s32[21]{0:T(128)S(1)} %get-tuple-element.25.codes, f32[8,128]{1,0:T(8,128)S(1)} %copy-done.1, f32[16,8,128]{2,1,0:T(8,128)S(1)} %get-tuple-element.23.stat, ...), custom_call_target="tpu_custom_call" | custom-call | tf_op jit(solution)/shard_map/pallas_call | solution.py:38
  56.6 1.3 %collective-permute-start.13 = (f32[5,8,128]{2,1,0:T(8,128)S(1)}, f32[5,8,128]{2,1,0:T(8,128)S(1)}, u32[]{:S(2)}, u32[]{:S(2)}) collective-permute-start(f32[5,8,128]{2,1,0:T(8,128)S(1)} %get-tuple-element.35.rest_0_.rest_3_), channel_id=1, source_target_pairs={{0,2},{1,3},{2,0},{3,1},{4,6},{5,7},{6,4},{7,5},{8,10},{9,11},{10,... | collective-permute-start | bytes 61448 | tf_op jit(solution)/shard_map/ppermute | solution.py:726
  57.9 4.3 %shard_map.95.rest_4_.rest_0_ = f32[12,8,128]{2,1,0:T(8,128)S(1)} custom-call(s32[56]{0:T(128)S(1)} %get-tuple-element.30.codes, f32[16,8,128]{2,1,0:T(8,128)S(1)} %get-tuple-element.34.v, f32[70,4,128,128]{3,2,1,0:T(8,128)S(1)} %get-tuple-element.31.tab), custom_call_target="tpu_custom_call" | custom-call | flops 21233664 | bytes 1048576 | tf_op jit(solution)/shard_map/pallas_call | solution.py:38
  62.2 1.2 %collective-permute-start.17 = (f32[8,8,128]{2,1,0:T(8,128)S(1)}, f32[8,8,128]{2,1,0:T(8,128)S(1)}, u32[]{:S(2)}, u32[]{:S(2)}) collective-permute-start(f32[8,8,128]{2,1,0:T(8,128)S(1)} %shard_map.96.rest_0_.rest_7_), channel_id=1, source_target_pairs={{0,12},{4,8},{8,4},{12,0},{1,13},{5,9},{9,5},{13,1},{2,14},{6,10},... | collective-permute-start | bytes 98312 | tf_op jit(solution)/shard_map/ppermute | solution.py:726
  64.0 2.7 %collective-permute-start.15 = (f32[8,8,128]{2,1,0:T(8,128)S(1)}, f32[8,8,128]{2,1,0:T(8,128)S(1)}, u32[]{:S(2)}, u32[]{:S(2)}) collective-permute-start(f32[8,8,128]{2,1,0:T(8,128)S(1)} %shard_map.96.rest_0_.rest_7_), channel_id=1, source_target_pairs={{0,4},{4,0},{8,12},{12,8},{1,5},{5,1},{9,13},{13,9},{2,6},{6,2},{1... | collective-permute-start | bytes 98312 | tf_op jit(solution)/shard_map/ppermute | solution.py:726
  66.7 3.6 %shard_map.97.rest_1_ = f32[8,8,128]{2,1,0:T(8,128)S(1)} custom-call(s32[56]{0:T(128)S(1)} %get-tuple-element.30.codes, f32[16,8,128]{2,1,0:T(8,128)S(1)} %get-tuple-element.34.v, f32[70,4,128,128]{3,2,1,0:T(8,128)S(1)} %get-tuple-element.31.tab, f32[8,8,128]{2,1,0:T(8,128)S(1)} %shard_map.96.rest_0_.rest_7_), custom_call_target="tpu_custom_call" | custom-call | flops 21233664 | bytes 1048576 | tf_op jit(solution)/shard_map/pallas_call | solution.py:38
  70.3 4.6 %shard_map.98 = (f32[16,8,128]{2,1,0:T(8,128)S(1)}, f32[16,8,128]{2,1,0:T(8,128)S(1)}, f32[16,8,128]{2,1,0:T(8,128)S(1)}, f32[16,8,128]{2,1,0:T(8,128)S(1)}, f32[8,128]{1,0:T(8,128)S(1)}) custom-call(s32[1]{0:T(128)} %bitcast.meta, s32[21]{0:T(128)S(1)} %get-tuple-element.25.codes, f32[8,128]{1,0:T(8,128)S(1)} %copy-done.1, ...), custom_call_target="tpu_custom_call" | custom-call | tf_op jit(solution)/shard_map/pallas_call | solution.py:38
  75.9 1.2 %collective-permute-start.19 = (f32[8,128]{1,0:T(8,128)S(1)}, f32[8,128]{1,0:T(8,128)S(1)}, u32[]{:S(2)}, u32[]{:S(2)}) collective-permute-start(f32[8,128]{1,0:T(8,128)S(1)} %get-tuple-element.39.scal), channel_id=1, source_target_pairs={{0,2},{1,3},{2,0},{3,1},{4,6},{5,7},{6,4},{7,5},{8,10},{9,11},{10,... | collective-permute-start | bytes 12296 | tf_op jit(solution)/shard_map/ppermute | solution.py:726
  78.0 1.5 %collective-permute-done.19 = f32[8,128]{1,0:T(8,128)S(1)} collective-permute-done((f32[8,128]{1,0:T(8,128)S(1)}, f32[8,128]{1,0:T(8,128)S(1)}, u32[]{:S(2)}, u32[]{:S(2)}) %collective-permute-start.19) | collective-permute-done | bytes 4128 | tf_op jit(solution)/shard_map/ppermute | solution.py:726
  79.5 1.2 %collective-permute-start.23 = (f32[8,128]{1,0:T(8,128)S(1)}, f32[8,128]{1,0:T(8,128)S(1)}, u32[]{:S(2)}, u32[]{:S(2)}) collective-permute-start(f32[8,128]{1,0:T(8,128)S(1)} %add_add_fusion.rest_0_), channel_id=1, source_target_pairs={{0,12},{4,8},{8,4},{12,0},{1,13},{5,9},{9,5},{13,1},{2,14},{6,10},... | collective-permute-start | bytes 12296 | tf_op jit(solution)/shard_map/ppermute | solution.py:726
  81.2 2.8 %collective-permute-start.21 = (f32[8,128]{1,0:T(8,128)S(1)}, f32[8,128]{1,0:T(8,128)S(1)}, u32[]{:S(2)}, u32[]{:S(2)}) collective-permute-start(f32[8,128]{1,0:T(8,128)S(1)} %add_add_fusion.rest_0_), channel_id=1, source_target_pairs={{0,4},{4,0},{8,12},{12,8},{1,5},{5,1},{9,13},{13,9},{2,6},{6,2},{1... | collective-permute-start | bytes 12296 | tf_op jit(solution)/shard_map/ppermute | solution.py:726
  (43 shorter events, 9.6 us)
Async XLA Ops:
  2.5 17.3 %collective-permute-start.2 = (f32[9,8,128]{2,1,0:T(8,128)S(1)}, f32[9,8,128]{2,1,0:T(8,128)S(1)}, u32[]{:S(2)}, u32[]{:S(2)}) collective-permute-start(f32[9,8,128]{2,1,0:T(8,128)S(1)} %get-tuple-element.28.rest_0_.rest_1_), channel_id=1, source_target_pairs={{0,3},{1,2},{2,1},{3,0},{4,7},{5,6},{6,5},{7,4},{8,11},{9,10},{10,... | collective-permute-start | bytes 110600 | tf_op jit(solution)/shard_map/ppermute | solution.py:726
  5.0 14.9 %collective-permute-start.1 = (f32[9,8,128]{2,1,0:T(8,128)S(1)}, f32[9,8,128]{2,1,0:T(8,128)S(1)}, u32[]{:S(2)}, u32[]{:S(2)}) collective-permute-start(f32[9,8,128]{2,1,0:T(8,128)S(1)} %get-tuple-element.28.rest_0_.rest_1_), channel_id=1, source_target_pairs={{0,2},{1,3},{2,0},{3,1},{4,6},{5,7},{6,4},{7,5},{8,10},{9,11},{10,... | collective-permute-start | bytes 110600 | tf_op jit(solution)/shard_map/ppermute | solution.py:726
  5.6 14.2 %collective-permute-start = (f32[9,8,128]{2,1,0:T(8,128)S(1)}, f32[9,8,128]{2,1,0:T(8,128)S(1)}, u32[]{:S(2)}, u32[]{:S(2)}) collective-permute-start(f32[9,8,128]{2,1,0:T(8,128)S(1)} %get-tuple-element.28.rest_0_.rest_1_), channel_id=1, source_target_pairs={{0,1},{1,0},{2,3},{3,2},{4,5},{5,4},{6,7},{7,6},{8,9},{9,8},{10,11... | collective-permute-start | bytes 110600 | tf_op jit(solution)/shard_map/ppermute | solution.py:726
  19.9 6.6 %collective-permute-start.5 = (f32[12,8,128]{2,1,0:T(8,128)S(1)}, f32[12,8,128]{2,1,0:T(8,128)S(1)}, u32[]{:S(2)}, u32[]{:S(2)}) collective-permute-start(f32[12,8,128]{2,1,0:T(8,128)S(1)} %shard_map.88.after.rest_5_), channel_id=1, source_target_pairs={{0,12},{4,8},{8,4},{12,0},{1,13},{5,9},{9,5},{13,1},{2,14},{6,10},... | collective-permute-start | bytes 147464 | tf_op jit(solution)/shard_map/ppermute | solution.py:726
  21.0 7.6 %collective-permute-start.4 = (f32[12,8,128]{2,1,0:T(8,128)S(1)}, f32[12,8,128]{2,1,0:T(8,128)S(1)}, u32[]{:S(2)}, u32[]{:S(2)}) collective-permute-start(f32[12,8,128]{2,1,0:T(8,128)S(1)} %shard_map.88.after.rest_5_), channel_id=1, source_target_pairs={{0,8},{4,12},{8,0},{12,4},{1,9},{5,13},{9,1},{13,5},{2,10},{6,14},... | collective-permute-start | bytes 147464 | tf_op jit(solution)/shard_map/ppermute | solution.py:726
  23.4 5.2 %collective-permute-start.3 = (f32[12,8,128]{2,1,0:T(8,128)S(1)}, f32[12,8,128]{2,1,0:T(8,128)S(1)}, u32[]{:S(2)}, u32[]{:S(2)}) collective-permute-start(f32[12,8,128]{2,1,0:T(8,128)S(1)} %shard_map.88.after.rest_5_), channel_id=1, source_target_pairs={{0,4},{4,0},{8,12},{12,8},{1,5},{5,1},{9,13},{13,9},{2,6},{6,2},{1... | collective-permute-start | bytes 147464 | tf_op jit(solution)/shard_map/ppermute | solution.py:726
  35.7 6.8 %collective-permute-start.8 = (f32[5,8,128]{2,1,0:T(8,128)S(1)}, f32[5,8,128]{2,1,0:T(8,128)S(1)}, u32[]{:S(2)}, u32[]{:S(2)}) collective-permute-start(f32[5,8,128]{2,1,0:T(8,128)S(1)} %get-tuple-element.32.rest_0_.rest_3_), channel_id=1, source_target_pairs={{0,3},{1,2},{2,1},{3,0},{4,7},{5,6},{6,5},{7,4},{8,11},{9,10},{10,... | collective-permute-start | bytes 61448 | tf_op jit(solution)/shard_map/ppermute | solution.py:726
  36.5 6.0 %collective-permute-start.7 = (f32[5,8,128]{2,1,0:T(8,128)S(1)}, f32[5,8,128]{2,1,0:T(8,128)S(1)}, u32[]{:S(2)}, u32[]{:S(2)}) collective-permute-start(f32[5,8,128]{2,1,0:T(8,128)S(1)} %get-tuple-element.32.rest_0_.rest_3_), channel_id=1, source_target_pairs={{0,2},{1,3},{2,0},{3,1},{4,6},{5,7},{6,4},{7,5},{8,10},{9,11},{10,... | collective-permute-start | bytes 61448 | tf_op jit(solution)/shard_map/ppermute | solution.py:726
  38.1 4.3 %collective-permute-start.6 = (f32[5,8,128]{2,1,0:T(8,128)S(1)}, f32[5,8,128]{2,1,0:T(8,128)S(1)}, u32[]{:S(2)}, u32[]{:S(2)}) collective-permute-start(f32[5,8,128]{2,1,0:T(8,128)S(1)} %get-tuple-element.32.rest_0_.rest_3_), channel_id=1, source_target_pairs={{0,1},{1,0},{2,3},{3,2},{4,5},{5,4},{6,7},{7,6},{8,9},{9,8},{10,11... | collective-permute-start | bytes 61448 | tf_op jit(solution)/shard_map/ppermute | solution.py:726
  42.5 8.1 %collective-permute-start.11 = (f32[8,8,128]{2,1,0:T(8,128)S(1)}, f32[8,8,128]{2,1,0:T(8,128)S(1)}, u32[]{:S(2)}, u32[]{:S(2)}) collective-permute-start(f32[8,8,128]{2,1,0:T(8,128)S(1)} %shard_map.92.rest_0_.rest_7_), channel_id=1, source_target_pairs={{0,12},{4,8},{8,4},{12,0},{1,13},{5,9},{9,5},{13,1},{2,14},{6,10},... | collective-permute-start | bytes 98312 | tf_op jit(solution)/shard_map/ppermute | solution.py:726
  44.0 6.6 %collective-permute-start.10 = (f32[8,8,128]{2,1,0:T(8,128)S(1)}, f32[8,8,128]{2,1,0:T(8,128)S(1)}, u32[]{:S(2)}, u32[]{:S(2)}) collective-permute-start(f32[8,8,128]{2,1,0:T(8,128)S(1)} %shard_map.92.rest_0_.rest_7_), channel_id=1, source_target_pairs={{0,8},{4,12},{8,0},{12,4},{1,9},{5,13},{9,1},{13,5},{2,10},{6,14},... | collective-permute-start | bytes 98312 | tf_op jit(solution)/shard_map/ppermute | solution.py:726
  44.2 6.4 %collective-permute-start.9 = (f32[8,8,128]{2,1,0:T(8,128)S(1)}, f32[8,8,128]{2,1,0:T(8,128)S(1)}, u32[]{:S(2)}, u32[]{:S(2)}) collective-permute-start(f32[8,8,128]{2,1,0:T(8,128)S(1)} %shard_map.92.rest_0_.rest_7_), channel_id=1, source_target_pairs={{0,4},{4,0},{8,12},{12,8},{1,5},{5,1},{9,13},{13,9},{2,6},{6,2},{1... | collective-permute-start | bytes 98312 | tf_op jit(solution)/shard_map/ppermute | solution.py:726
  55.6 6.6 %collective-permute-start.14 = (f32[5,8,128]{2,1,0:T(8,128)S(1)}, f32[5,8,128]{2,1,0:T(8,128)S(1)}, u32[]{:S(2)}, u32[]{:S(2)}) collective-permute-start(f32[5,8,128]{2,1,0:T(8,128)S(1)} %get-tuple-element.35.rest_0_.rest_3_), channel_id=1, source_target_pairs={{0,3},{1,2},{2,1},{3,0},{4,7},{5,6},{6,5},{7,4},{8,11},{9,10},{10,... | collective-permute-start | bytes 61448 | tf_op jit(solution)/shard_map/ppermute | solution.py:726
  56.6 5.6 %collective-permute-start.13 = (f32[5,8,128]{2,1,0:T(8,128)S(1)}, f32[5,8,128]{2,1,0:T(8,128)S(1)}, u32[]{:S(2)}, u32[]{:S(2)}) collective-permute-start(f32[5,8,128]{2,1,0:T(8,128)S(1)} %get-tuple-element.35.rest_0_.rest_3_), channel_id=1, source_target_pairs={{0,2},{1,3},{2,0},{3,1},{4,6},{5,7},{6,4},{7,5},{8,10},{9,11},{10,... | collective-permute-start | bytes 61448 | tf_op jit(solution)/shard_map/ppermute | solution.py:726
  57.9 4.3 %collective-permute-start.12 = (f32[5,8,128]{2,1,0:T(8,128)S(1)}, f32[5,8,128]{2,1,0:T(8,128)S(1)}, u32[]{:S(2)}, u32[]{:S(2)}) collective-permute-start(f32[5,8,128]{2,1,0:T(8,128)S(1)} %get-tuple-element.35.rest_0_.rest_3_), channel_id=1, source_target_pairs={{0,1},{1,0},{2,3},{3,2},{4,5},{5,4},{6,7},{7,6},{8,9},{9,8},{10,11... | collective-permute-start | bytes 61448 | tf_op jit(solution)/shard_map/ppermute | solution.py:726
  62.2 8.1 %collective-permute-start.17 = (f32[8,8,128]{2,1,0:T(8,128)S(1)}, f32[8,8,128]{2,1,0:T(8,128)S(1)}, u32[]{:S(2)}, u32[]{:S(2)}) collective-permute-start(f32[8,8,128]{2,1,0:T(8,128)S(1)} %shard_map.96.rest_0_.rest_7_), channel_id=1, source_target_pairs={{0,12},{4,8},{8,4},{12,0},{1,13},{5,9},{9,5},{13,1},{2,14},{6,10},... | collective-permute-start | bytes 98312 | tf_op jit(solution)/shard_map/ppermute | solution.py:726
  63.5 6.8 %collective-permute-start.16 = (f32[8,8,128]{2,1,0:T(8,128)S(1)}, f32[8,8,128]{2,1,0:T(8,128)S(1)}, u32[]{:S(2)}, u32[]{:S(2)}) collective-permute-start(f32[8,8,128]{2,1,0:T(8,128)S(1)} %shard_map.96.rest_0_.rest_7_), channel_id=1, source_target_pairs={{0,8},{4,12},{8,0},{12,4},{1,9},{5,13},{9,1},{13,5},{2,10},{6,14},... | collective-permute-start | bytes 98312 | tf_op jit(solution)/shard_map/ppermute | solution.py:726
  64.0 6.3 %collective-permute-start.15 = (f32[8,8,128]{2,1,0:T(8,128)S(1)}, f32[8,8,128]{2,1,0:T(8,128)S(1)}, u32[]{:S(2)}, u32[]{:S(2)}) collective-permute-start(f32[8,8,128]{2,1,0:T(8,128)S(1)} %shard_map.96.rest_0_.rest_7_), channel_id=1, source_target_pairs={{0,4},{4,0},{8,12},{12,8},{1,5},{5,1},{9,13},{13,9},{2,6},{6,2},{1... | collective-permute-start | bytes 98312 | tf_op jit(solution)/shard_map/ppermute | solution.py:726
  74.9 3.1 %collective-permute-start.20 = (f32[8,128]{1,0:T(8,128)S(1)}, f32[8,128]{1,0:T(8,128)S(1)}, u32[]{:S(2)}, u32[]{:S(2)}) collective-permute-start(f32[8,128]{1,0:T(8,128)S(1)} %get-tuple-element.39.scal), channel_id=1, source_target_pairs={{0,3},{1,2},{2,1},{3,0},{4,7},{5,6},{6,5},{7,4},{8,11},{9,10},{10,... | collective-permute-start | bytes 12296 | tf_op jit(solution)/shard_map/ppermute | solution.py:726
  75.9 3.6 %collective-permute-start.19 = (f32[8,128]{1,0:T(8,128)S(1)}, f32[8,128]{1,0:T(8,128)S(1)}, u32[]{:S(2)}, u32[]{:S(2)}) collective-permute-start(f32[8,128]{1,0:T(8,128)S(1)} %get-tuple-element.39.scal), channel_id=1, source_target_pairs={{0,2},{1,3},{2,0},{3,1},{4,6},{5,7},{6,4},{7,5},{8,10},{9,11},{10,... | collective-permute-start | bytes 12296 | tf_op jit(solution)/shard_map/ppermute | solution.py:726
  77.2 2.4 %collective-permute-start.18 = (f32[8,128]{1,0:T(8,128)S(1)}, f32[8,128]{1,0:T(8,128)S(1)}, u32[]{:S(2)}, u32[]{:S(2)}) collective-permute-start(f32[8,128]{1,0:T(8,128)S(1)} %get-tuple-element.39.scal), channel_id=1, source_target_pairs={{0,1},{1,0},{2,3},{3,2},{4,5},{5,4},{6,7},{7,6},{8,9},{9,8},{10,11... | collective-permute-start | bytes 12296 | tf_op jit(solution)/shard_map/ppermute | solution.py:726
  79.5 5.5 %collective-permute-start.23 = (f32[8,128]{1,0:T(8,128)S(1)}, f32[8,128]{1,0:T(8,128)S(1)}, u32[]{:S(2)}, u32[]{:S(2)}) collective-permute-start(f32[8,128]{1,0:T(8,128)S(1)} %add_add_fusion.rest_0_), channel_id=1, source_target_pairs={{0,12},{4,8},{8,4},{12,0},{1,13},{5,9},{9,5},{13,1},{2,14},{6,10},... | collective-permute-start | bytes 12296 | tf_op jit(solution)/shard_map/ppermute | solution.py:726
  80.7 4.5 %collective-permute-start.22 = (f32[8,128]{1,0:T(8,128)S(1)}, f32[8,128]{1,0:T(8,128)S(1)}, u32[]{:S(2)}, u32[]{:S(2)}) collective-permute-start(f32[8,128]{1,0:T(8,128)S(1)} %add_add_fusion.rest_0_), channel_id=1, source_target_pairs={{0,8},{4,12},{8,0},{12,4},{1,9},{5,13},{9,1},{13,5},{2,10},{6,14},... | collective-permute-start | bytes 12296 | tf_op jit(solution)/shard_map/ppermute | solution.py:726
  81.2 4.4 %collective-permute-start.21 = (f32[8,128]{1,0:T(8,128)S(1)}, f32[8,128]{1,0:T(8,128)S(1)}, u32[]{:S(2)}, u32[]{:S(2)}) collective-permute-start(f32[8,128]{1,0:T(8,128)S(1)} %add_add_fusion.rest_0_), channel_id=1, source_target_pairs={{0,4},{4,0},{8,12},{12,8},{1,5},{5,1},{9,13},{13,9},{2,6},{6,2},{1... | collective-permute-start | bytes 12296 | tf_op jit(solution)/shard_map/ppermute | solution.py:726
  (2 other events, 8.8 us)
